TPU v7x, 32 devices: a whole 2x2x4 slice. The times are simulated.
32 devices in a mesh: tm: 16 (over z, y, x), pix: 2 (over core).
Axes of the slice: x: 2, y: 2, z: 4, core: 2. Of those that a mesh axis runs over, the one named last changes fastest.
Arguments:
- frames: float32 [2048, 16384], P('tm', 'pix'), may hold values from 0.04 to 830, as said below
- ref_weight: float32 [16384], P('pix'), may hold values from 0.02 to 15, as said below
Outputs:
- correlation: float32 [4, 16, 16384], P(None, None, 'pix')
Inputs may be any that keep to these rules, and one draw needn't show every extreme that they name: `frames`: positive intensities. `ref_weight`: positive weights.
All inputs are finite; a program needn't handle non-finite values.
Results may differ from a plain program's by a relative error of at most 0.0001.
Values sent between devices are 32-bit elements; how exact they have to be, the bound alone decides.
No kernel may reach another device: no remote copies, remote signals or barrier semaphores. Data moves between devices by JAX's collectives and lax.ppermute only.
A program may use at most 64 MiB of HBM per device.

v0:
```python
import jax
import jax.numpy as jnp
from jax import lax
from jax.sharding import PartitionSpec as P

LEVELS = 4
LAGS = 16


def from_behind(block, axis, distance):
    devices = range(lax.axis_size(axis))
    route = [(i - distance, i) for i in devices if i - distance in devices]
    return lax.ppermute(block, axis, route)


def coarsen(series):
    half_rows = series.shape[0] // 2
    return series.reshape(half_rows, 2, series.shape[1]).sum(axis=1) * 0.5


def lag_sums(extended, row_count):
    return jnp.stack(
        [
            jnp.sum(extended[:row_count] * extended[lag_index : lag_index + row_count], axis=0)
            for lag_index in range(1, LAGS + 1)
        ]
    )


def on_device(frames, ref_weight):
    frame_rows = frames.shape[0]
    numer = jnp.sum(frames * ref_weight[None, :], axis=1)
    numer_all, weight_all = lax.psum((numer, jnp.sum(ref_weight)), "pix")
    signal = frames + (numer_all / weight_all)[:, None]
    total_frames = frame_rows * lax.axis_size("tm")
    column_sum = jnp.sum(signal, axis=0)
    current = signal
    level_totals = []
    column_all = column_sum
    for level in range(LEVELS):
        level_rows = frame_rows >> level
        tail_rows = from_behind(current[:LAGS], "tm", -1)
        extended = jnp.concatenate([current, tail_rows], axis=0)
        partial_value = lag_sums(extended, level_rows)
        summed, column_all = lax.psum((partial_value, column_sum), "tm")
        level_totals.append(summed)
        if level < LEVELS - 1:
            current = coarsen(current)
    totals = jnp.stack(level_totals)
    pixel_mean = column_all / total_frames
    pair_counts = jnp.asarray(
        [
            [(total_frames >> level) - lag_index for lag_index in range(1, LAGS + 1)]
            for level in range(LEVELS)
        ],
        jnp.float32,
    )
    return totals / (pair_counts[:, :, None] * (pixel_mean * pixel_mean)[None, None, :])


def solution(mesh):
    return jax.shard_map(
        on_device,
        mesh=mesh,
        in_specs=(P("tm", "pix"), P("pix")),
        out_specs=P(None, None, "pix"),
        check_vma=False,
    )
```

profile of v0, /device:TPU:0, one launch (start us, length us, event | category | flops | bytes accessed | tf_op | source)
XLA Modules:
  0.0 272.9 jit_solution(13894957902598750448)
XLA Ops:
  6.5 2.6 multiply_reduce_fusion
  9.7 3.2 %all-reduce.1 = (f32[128]{0:T(128)S(1)}, f32[]{:T(128)}) all-reduce(f32[128]{0:T(128)S(1)} %multiply_reduce_fusion, f32[]{:T(128)} %reduce_sum.631), channel_id=1, replica_groups=mesh['tm'=16,'pix'=2] {'pix'}, use_global_device_ids=true, to_apply=%region_1.0 | all-reduce | flops 129 | bytes 1032 | tf_op jit(solution)/shard_map/psum | solution.py:33
  13.6 2.7 broadcast_add_fusion
  16.3 1.9 copy-done
  20.4 5.8 %reshape.15 = f32[64,2,8192]{2,1,0:T(2,128)} reshape(f32[128,8192]{1,0:T(8,128)} %copy-done) | data formatting | bytes 8388608 | tf_op jit(solution)/shard_map/reshape | solution.py:18
  26.2 8.8 %reduce_sum.648 = f32[64,8192]{1,0:T(8,128)} reduce(f32[64,2,8192]{2,1,0:T(2,128)} %reshape.15, f32[]{:T(128)} %constant.4.clone.1), dimensions={1}, to_apply=%region_21.0 | reduce | flops 524288 | bytes 6291460 | tf_op jit(solution)/shard_map/reduce_sum | solution.py:18
  38.9 2.2 mul.278
  41.2 5.1 %reduce_sum.665 = f32[32,8192]{1,0:T(8,128)} reduce(f32[32,2,8192]{2,1,0:T(2,128)} %mul.278, f32[]{:T(128)} %constant.4.clone.1), dimensions={1}, to_apply=%region_39.0 | reduce | flops 262144 | bytes 3145732 | tf_op jit(solution)/shard_map/reduce_sum | solution.py:18
  51.5 3.3 %reduce_sum.682 = f32[16,8192]{1,0:T(8,128)} reduce(f32[16,2,8192]{2,1,0:T(2,128)} %mul.297, f32[]{:T(128)} %constant.4.clone.1), dimensions={1}, to_apply=%region_57.0 | reduce | flops 131072 | bytes 1572868 | tf_op jit(solution)/shard_map/reduce_sum | solution.py:18
  58.2 19.1 %fusion.46 = (f32[8192]{0:T(1024)S(1)}, f32[8192]{0:T(1024)S(1)}, f32[8192]{0:T(1024)S(1)}, f32[8192]{0:T(1024)S(1)}, f32[8192]{0:T(1024)S(1)}, /*index=5*/f32[8...) fusion(f32[128,8192]{1,0:T(8,128)} %copy-done, f32[16,8192]{1,0:T(8,128)} %collective-permute-done), kind=kLoop, calls=%fused_computation.107 | loop fusion | flops 28237824 | bytes 5013504 | tf_op jit(solution)/shard_map/reduce_sum | solution.py:24
  77.3 7.6 %fusion.23 = (f32[8192]{0:T(1024)S(1)}, f32[8192]{0:T(1024)S(1)}, f32[8192]{0:T(1024)S(1)}, f32[8192]{0:T(1024)}, f32[8192]{0:T(1024)}, /*index=5*/f32[8192]{0:T(1024)}, f32[8192]{0:T(1024)}, f32[8192]{0:T(1024)}) fusion(f32[128,8192]{1,0:T(8,128)S(1)} %copy-done.1, f32[16,8192]{1,0:T(8,128)} %collective-permute-done), kind=kLoop, calls=%fused_computation.83 | loop fusion | flops 23003136 | bytes 4980736 | tf_op jit(solution)/shard_map/reduce_sum | solution.py:24
  85.0 2.9 %stack.235 = f32[16,8192]{1,0:T(8,128)} concatenate(f32[1,8192]{1,0:T(1,128)} %bitcast.117, f32[1,8192]{1,0:T(1,128)} %bitcast.116, f32[1,8192]{1,0:T(1,128)} %bitcast.115, f32[1,8192]{1,0:T(1,128)} %bitcast.114, f32[1,8192]{1,0:T(1,128)S(1)} %bitcast.113, f32[1,8192]{1,0:T(1,128)S(1)} %bitcast.112, f32[1,8192]{1,0:T(1,128)S(1)} %bitcast.111, f32[1,8192]{1,0:T(1,128)S(1)} %bitcast.110, ...), dimensions={0} | concatenate | bytes 1048576 | tf_op jit(solution)/shard_map/stack | solution.py:22
  87.9 5.7 %fusion.93 = (f32[8192]{0:T(1024)S(1)}, f32[8192]{0:T(1024)S(1)}, f32[8192]{0:T(1024)S(1)}, f32[8192]{0:T(1024)S(1)}, f32[8192]{0:T(1024)S(1)}, /*index=5*/f32[8...) fusion(f32[64,8192]{1,0:T(8,128)S(1)} %broadcast_multiply_fusion, ...), kind=kLoop, calls=%fused_computation.214 | loop fusion | flops 14082048 | bytes 2916352 | tf_op jit(solution)/shard_map/reduce_sum | solution.py:24
  93.5 5.4 %fusion.70 = (f32[8192]{0:T(1024)S(1)}, f32[8192]{0:T(1024)S(1)}, f32[8192]{0:T(1024)S(1)}, f32[8192]{0:T(1024)}, f32[8192]{0:T(1024)}, /*index=5*/f32[8192]{0:T(1024)}, f32[8192]{0:T(1024)}) fusion(f32[64,8192]{1,0:T(8,128)S(1)} %broadcast_multiply_fusion, f32[16,8192]{1,0:T(8,128)} %collective-permute-done.1), kind=kLoop, calls=%fused_computation.190 | loop fusion | flops 10952704 | bytes 2850816 | tf_op jit(solution)/shard_map/reduce_sum | solution.py:24
  99.0 3.6 %fusion.117 = (f32[8192]{0:T(1024)S(1)}, f32[8192]{0:T(1024)S(1)}, f32[8192]{0:T(1024)S(1)}, f32[8192]{0:T(1024)S(1)}, f32[8192]{0:T(1024)S(1)}, /*index=5*/f32[8192]{0:T(1024)S(1)}, f32[8192]{0:T(1024)S(1)}) fusion(f32[32,8192]{1,0:T(8,128)S(1)} %broadcast_multiply_fusion.1, f32[16,8192]{1,0:T(8,128)} %collective-permute-done.2), kind=kLoop, calls=%fused_computation.240 | loop fusion | flops 5447680 | bytes 1802240 | tf_op jit(solution)/shard_map/reduce_sum | solution.py:24
  102.5 2.9 %stack.253 = f32[16,8192]{1,0:T(8,128)} concatenate(f32[1,8192]{1,0:T(1,128)} %bitcast.94, f32[1,8192]{1,0:T(1,128)} %bitcast.93, f32[1,8192]{1,0:T(1,128)} %bitcast.92, f32[1,8192]{1,0:T(1,128)} %bitcast.91, f32[1,8192]{1,0:T(1,128)S(1)} %bitcast.90, f32[1,8192]{1,0:T(1,128)S(1)} %bitcast.89, f32[1,8192]{1,0:T(1,128)S(1)} %bitcast.88, f32[1,8192]{1,0:T(1,128)S(1)} %bitcast.87, ...), dimensions={0} | concatenate | bytes 1048576 | tf_op jit(solution)/shard_map/stack | solution.py:22
  105.5 4.3 %fusion.140 = (f32[8192]{0:T(1024)S(1)}, f32[8192]{0:T(1024)S(1)}, f32[8192]{0:T(1024)S(1)}, f32[8192]{0:T(1024)S(1)}, f32[8192]{0:T(1024)S(1)}, /*index=5*/f32[...) fusion(f32[32,8192]{1,0:T(8,128)S(1)} %broadcast_multiply_fusion.1, ...), kind=kLoop, calls=%fused_computation.264 | loop fusion | flops 7004160 | bytes 1867776 | tf_op jit(solution)/shard_map/reduce_sum | solution.py:24
  109.8 2.2 stack.271
  112.0 4.4 %fusion.161 = (f32[8192]{0:T(1024)S(1)}, f32[8192]{0:T(1024)S(1)}, f32[8192]{0:T(1024)S(1)}, f32[8192]{0:T(1024)S(1)}, f32[8192]{0:T(1024)S(1)}, /*index=5*/f32[8192]{0:T(1024)S(1)}, f32[8192]{0:T(1024)S(1)}) fusion(f32[16,8192]{1,0:T(8,128)} %broadcast_multiply_fusion.2, f32[16,8192]{1,0:T(8,128)} %collective-permute-done.3, f32[16,8192]{1,0:T(8,128)S(1)} %copy-done.2), kind=kLoop, calls=%fused_computation.286 | loop fusion | flops 2695168 | bytes 1802240 | tf_op jit(solution)/shard_map/reduce_sum | solution.py:24
  116.4 5.8 %fusion.184 = (f32[8192]{0:T(1024)S(1)}, f32[8192]{0:T(1024)S(1)}, f32[8192]{0:T(1024)S(1)}, f32[8192]{0:T(1024)S(1)}, f32[8192]{0:T(1024)S(1)}, /*index=5*/f32[...) fusion(f32[16,8192]{1,0:T(8,128)} %broadcast_multiply_fusion.2, f32[16,8192]{1,0:T(8,128)} %collective-permute-done.3), kind=kLoop, calls=%fused_computation.310 | loop fusion | flops 3465216 | bytes 1343488 | tf_op jit(solution)/shard_map/reduce_sum | solution.py:24
  122.2 2.1 stack.289
  124.4 87.6 %psum.55 = f32[8192]{0:T(1024)S(1)} all-reduce(f32[8192]{0:T(1024)S(1)} %copy-done.4), channel_id=1, replica_groups=mesh['tm'=16,'pix'=2] {'tm'}, use_global_device_ids=true, to_apply=%region_76.0 | all-reduce | flops 8192 | bytes 65536 | tf_op jit(solution)/shard_map/psum | solution.py:45
  212.0 50.9 %all-reduce.4.cloned.1.call-done = (f32[1,16,8192]{2,1,0:T(8,128)}, f32[1,16,8192]{2,1,0:T(8,128)}, f32[1,16,8192]{2,1,0:T(8,128)}, f32[1,16,8192]{2,1,0:T(8,128)}) async-done(((f32[1,16,8192]{2,1,0:T(8,128)}, f32[1,16,8192]{2,1,0:T(8,128)}, f32[1,16,8192]{2,1,0:T(8,128)}, f32[1,16,8192]{2,1,0:T(8,128)}), (f32[1,16,8192]{2,1,0:T(8,128)}, f32[1,16,8192]{2,1,0:T(8,128)}, f32[1,16,8192]{2,1,0:T(8,128)}, ...) | async-done | bytes 2097168 | tf_op jit(solution)/shard_map/psum | solution.py:45
  262.8 3.2 %maximum_divide_fusion = f32[4,16,8192]{2,1,0:T(8,128)} fusion(f32[1,16,8192]{2,1,0:T(8,128)} %get-tuple-element.70, f32[1,16,8192]{2,1,0:T(8,128)} %get-tuple-element.71, f32[1,16,8192]{2,1,0:T(8,128)} %get-tuple-element.72, f32[1,16,8192]{2,1,0:T(8,128)} %get-tuple-element.73, f32[8192]{0:T(1024)S(1)} %multiply_multiply_fusion, f32[4,16]{1,0:T(4,128)S(1)} %copy-done.5), kind=kLoop, calls=%fused_computation.215 | loop fusion | flops 2621440 | bytes 4227328 | tf_op jit(solution)/shard_map/div | solution.py:58
  (31 shorter events, 16.0 us)
Async XLA Ops:
  6.5 2.6 copy-start.3
  6.5 256.3 %all-reduce.4.cloned.1.call-start = ((), (), s32[]{:S(2)}) async-start(), calls=%async_computation | async-start | bytes 4194304 | tf_op jit(solution)/shard_map/psum | solution.py:45
  16.3 1.9 copy-start
  19.1 39.1 %collective-permute-start = (f32[16,8192]{1,0:T(8,128)}, f32[16,8192]{1,0:T(8,128)}, u32[]{:S(2)}, u32[]{:S(2)}) collective-permute-start(f32[16,8192]{1,0:T(8,128)} %slice.264), channel_id=1, source_target_pairs={{2,0},{4,2},{6,4},{8,6},{10,8},{12,10},{14,12},{16,14},{18,16},{20... | collective-permute-start | bytes 1572872 | tf_op jit(solution)/shard_map/ppermute | solution.py:13
  37.6 50.2 %collective-permute-start.1 = (f32[16,8192]{1,0:T(8,128)}, f32[16,8192]{1,0:T(8,128)}, u32[]{:S(2)}, u32[]{:S(2)}) collective-permute-start(f32[16,8192]{1,0:T(8,128)} %slice.295), channel_id=1, source_target_pairs={{2,0},{4,2},{6,4},{8,6},{10,8},{12,10},{14,12},{16,14},{18,16},{20... | collective-permute-start | bytes 1572872 | tf_op jit(solution)/shard_map/ppermute | solution.py:13
  48.5 50.5 %collective-permute-start.2 = (f32[16,8192]{1,0:T(8,128)}, f32[16,8192]{1,0:T(8,128)}, u32[]{:S(2)}, u32[]{:S(2)}) collective-permute-start(f32[16,8192]{1,0:T(8,128)} %slice.326), channel_id=1, source_target_pairs={{2,0},{4,2},{6,4},{8,6},{10,8},{12,10},{14,12},{16,14},{18,16},{20... | collective-permute-start | bytes 1572872 | tf_op jit(solution)/shard_map/ppermute | solution.py:13
  56.7 20.6 %copy-start.1 = (f32[128,8192]{1,0:T(8,128)S(1)}, f32[128,8192]{1,0:T(8,128)}, u32[]{:S(2)}) copy-start(f32[128,8192]{1,0:T(8,128)} %copy-done) | copy-start | bytes 12582916
  56.7 55.3 %collective-permute-start.3 = (f32[16,8192]{1,0:T(8,128)}, f32[16,8192]{1,0:T(8,128)}, u32[]{:S(2)}, u32[]{:S(2)}) collective-permute-start(f32[16,8192]{1,0:T(8,128)} %broadcast_multiply_fusion.2), channel_id=1, source_target_pairs={{2,0},{4,2},{6,4},{8,6},{10,8},{12,10},{14,12},{16,14},{18,16},{20... | collective-permute-start | bytes 1572872 | tf_op jit(solution)/shard_map/ppermute | solution.py:13
  99.0 13.1 %copy-start.2 = (f32[16,8192]{1,0:T(8,128)S(1)}, f32[16,8192]{1,0:T(8,128)}, u32[]{:S(2)}) copy-start(f32[16,8192]{1,0:T(8,128)} %reduce_sum.682) | copy-start | bytes 1572868
  116.4 8.0 %copy-start.4 = (f32[8192]{0:T(1024)S(1)}, f32[8192]{0:T(1024)}, u32[]{:S(2)}) copy-start(f32[8192]{0:T(1024)} %get-tuple-element.21) | copy-start | bytes 98308
  116.4 146.4 %copy-start.5 = (f32[4,16]{1,0:T(4,128)S(1)}, f32[4,16]{1,0:T(4,128)}, u32[]{:S(2)}) copy-start(f32[4,16]{1,0:T(4,128)} %constant.3.clone) | copy-start | bytes 772
Sparse Core Ops, SparseCore 0:
  124.5 138.2 all-reduce.3
where the time goes:
time: 274 us; the launch traced here: 273 us
  blocking collectives  90.8 us (33%)
  other arithmetic  87.7 us (32%)
  waiting for transfers between devices  50.9 us (19%)
  local copies, waits for them, and re-layouts  24.4 us (9%)
  between operations  13.6 us (5%)
  starting transfers between devices  5.57 us (2%)
    psum x1, blocking collectives, on_device(): summed, column_all = lax.psum((partial_value, column_sum), 'tm')  87.6 us
    reduce_sum x8, other arithmetic, lag_sums(): jnp.sum(extended[:row_count] * extended[lag_index:lag_index + row_count],...  55.9 us
    psum x1, waiting for transfers between devices, on_device(): summed, column_all = lax.psum((partial_value, column_sum), 'tm')  50.9 us
    reduce_sum x3, other arithmetic, coarsen(): return series.reshape(half_rows, 2, series.shape[1]).sum(axis=1) * 0.5  17.2 us
    another operation x4, local copies, waits for them, and re-layouts, lag_sums(): jnp.stack([jnp.sum(extended[:row_count] * extended[lag_index:lag_index +...  10.2 us
    reshape x1, local copies, waits for them, and re-layouts, coarsen(): return series.reshape(half_rows, 2, series.shape[1]).sum(axis=1) * 0.5  5.82 us
    ppermute x4, starting transfers between devices, from_behind(): return lax.ppermute(block, axis, route)  5.56 us
  transfers between devices with their start and end apart: 5, of which 1 were waited for; matrix products, arithmetic and copies ran while one was open for 32% of the time, Pallas kernels for 0%

commit v1 on v0

v1 whole, which is shorter than its diff:
```python
import functools

import jax
import jax.numpy as jnp
from jax import lax
from jax.experimental import pallas as pl
from jax.experimental.pallas import tpu as pltpu
from jax.sharding import PartitionSpec as P

LEVELS = 4
LAGS = 16
SUB, LANE = 8, 128
GROUP = SUB * LANE
VMEM_LIMIT = 48 * 1024 * 1024


def stack_tile(x_ref, tall_ref, row_tiles):
    for i in range(row_tiles):
        for c in range(SUB):
            tall_ref[pl.ds(i * SUB * SUB + c, SUB, stride=SUB), :] = x_ref[
                i * SUB : (i + 1) * SUB, c * LANE : (c + 1) * LANE
            ]


def tile(ref, row):
    return ref[row * SUB : (row + 1) * SUB, :]


def edge_kernel(x_ref, w_ref, sums_ref, edge_ref, tall_ref, acc_ref):
    rows = x_ref.shape[0]

    @pl.when(pl.program_id(0) == 0)
    def _():
        acc_ref[...] = jnp.zeros_like(acc_ref)

    for c in range(SUB):
        weight = jnp.broadcast_to(w_ref[:, c * LANE : (c + 1) * LANE], (SUB, LANE))
        acc_ref[rows : rows + SUB, :] += weight
        for i in range(rows // SUB):
            part = slice(i * SUB, (i + 1) * SUB)
            acc_ref[part, :] += x_ref[part, c * LANE : (c + 1) * LANE] * weight
    stack_tile(x_ref, tall_ref, rows // SUB)
    edge_ref[0, : LAGS * SUB, :] = tall_ref[: LAGS * SUB, :]
    half = LAGS // 2
    for level in range(1, LEVELS):
        span = 1 << level
        for j in range(half):
            group = [tile(tall_ref, (half + j) * span + s) for s in range(span)]
            while len(group) > 1:
                group = [(a + b) * 0.5 for a, b in zip(group[::2], group[1::2])]
            row = LAGS + (level - 1) * half + j
            edge_ref[0, row * SUB : (row + 1) * SUB, :] = group[0]

    @pl.when(pl.program_id(0) == pl.num_programs(0) - 1)
    def _():
        sums_ref[...] = jnp.sum(acc_ref[...], axis=1, keepdims=True)


def lag_step(old, new, totals):
    out = list(totals)
    for k in range(1, LAGS + 1):
        terms = []
        for i in range(LAGS):
            if i + k < LAGS:
                terms.append(old[i] * old[i + k])
            elif new is not None:
                terms.append(old[i] * new[i + k - LAGS])
        if terms:
            total = terms[0]
            for term in terms[1:]:
                total = total + term
            out[k - 1] = out[k - 1] + total
    return out


def inner_kernel(mean_ref, x_ref, totals_ref, last_ref, sum_ref, series_ref):
    rows = x_ref.shape[0]
    stack_tile(x_ref, series_ref, rows // SUB)

    def add_mean(t, total):
        at = pl.ds(pl.multiple_of(t * SUB, SUB), SUB)
        value = series_ref[at, :] + mean_ref[t]
        series_ref[at, :] = value
        return total + value

    sum_ref[0] = lax.fori_loop(
        0, rows, add_mean, jnp.zeros((SUB, LANE), jnp.float32), unroll=8
    )
    zero = jnp.zeros((SUB, LANE), jnp.float32)
    for level in range(LEVELS):
        count = rows >> level
        chunks = count // LAGS

        def load(chunk):
            start = pl.multiple_of(chunk * LAGS * SUB, SUB)
            block = series_ref[pl.ds(start, LAGS * SUB), :]
            return [block[i * SUB : (i + 1) * SUB] for i in range(LAGS)]

        def body(chunk, totals):
            return tuple(lag_step(load(chunk), load(chunk + 1), totals))

        totals = tuple([zero] * LAGS)
        if chunks > 1:
            totals = lax.fori_loop(0, chunks - 1, body, totals)
        old = load(chunks - 1)
        totals = lag_step(old, None, totals)
        for i in range(LAGS):
            row = level * LAGS + i
            totals_ref[0, row * SUB : (row + 1) * SUB, :] = totals[i]
            last_ref[0, row * SUB : (row + 1) * SUB, :] = old[i]
        if level < LEVELS - 1:
            def coarsen(i, carry):
                start = pl.multiple_of(i * 2 * SUB, SUB)
                pair = series_ref[pl.ds(start, 2 * SUB), :]
                series_ref[pl.ds(pl.multiple_of(i * SUB, SUB), SUB), :] = (
                    pair[:SUB] + pair[SUB:]
                ) * 0.5
                return carry

            lax.fori_loop(0, count // 2, coarsen, 0, unroll=4)


def border_kernel(mean_ref, edge_ref, last_ref, totals_ref, out_ref):
    half = LAGS // 2
    means = [mean_ref[t] for t in range(LAGS << (LEVELS - 1))]
    new = None
    for level in range(LEVELS):
        if level == 0:
            new = [
                edge_ref[0, j * SUB : (j + 1) * SUB, :] + means[j] for j in range(LAGS)
            ]
        else:
            means = [(a + b) * 0.5 for a, b in zip(means[::2], means[1::2])]
            first = [(a + b) * 0.5 for a, b in zip(new[::2], new[1::2])]
            second = []
            for j in range(half):
                row = LAGS + (level - 1) * half + j
                second.append(edge_ref[0, row * SUB : (row + 1) * SUB, :] + means[half + j])
            new = first + second
        old = [
            last_ref[0, (level * LAGS + i) * SUB : (level * LAGS + i + 1) * SUB, :]
            for i in range(LAGS)
        ]
        for k in range(1, LAGS + 1):
            at = slice((level * LAGS + k - 1) * SUB, (level * LAGS + k) * SUB)
            total = totals_ref[0, at, :]
            for i in range(LAGS - k, LAGS):
                total = total + old[i] * new[i + k - LAGS]
            out_ref[0, at, :] = total


def finish_kernel(total_frames, totals_ref, sum_ref, out_ref):
    for c in range(SUB):
        mean = sum_ref[0, c : c + 1, :] / total_frames
        square = jnp.broadcast_to(mean * mean, (SUB, LANE))
        for level in range(LEVELS):
            for i in range(LAGS // SUB):
                lag = lax.broadcasted_iota(jnp.int32, (SUB, LANE), 0) + (i * SUB + 1)
                count = ((total_frames >> level) - lag).astype(jnp.float32)
                row = level * LAGS + i * SUB
                total = totals_ref[0, pl.ds(row * SUB + c, SUB, stride=SUB), :]
                out_ref[level, i * SUB : (i + 1) * SUB, c * LANE : (c + 1) * LANE] = (
                    total / (count * square)
                )


def params():
    return pltpu.CompilerParams(vmem_limit_bytes=VMEM_LIMIT)


def f32(*shape):
    return jax.ShapeDtypeStruct(shape, jnp.float32)


def by_group(rows):
    return pl.BlockSpec((1, rows * SUB, LANE), lambda g: (g, 0, 0))


SMEM = pl.BlockSpec(memory_space=pltpu.SMEM)
ROWS = LEVELS * LAGS
EDGE_ROWS = LAGS + (LEVELS - 1) * (LAGS // 2)


def swap(block, mask):
    size = lax.axis_size("tm")
    return lax.ppermute(block, "tm", [(i, i ^ mask) for i in range(size)])


def sum_parts(parts, orders):
    me = lax.axis_index("tm")
    count = len(parts)
    steps = len(orders[0])
    cur = [p[0] for p in parts]
    sums = [p[1] for p in parts]
    for s in range(steps):
        kept, sent = [], []
        for p in range(count):
            half = cur[p].shape[1] // 2
            upper = (me & orders[p][s]) != 0
            low, high = cur[p][:, :half], cur[p][:, half:]
            kept.append(jnp.where(upper, high, low))
            sent.append(
                jnp.concatenate([jnp.where(upper, low, high), sums[p]], axis=1)
            )
        for p in range(count):
            half = kept[p].shape[1]
            got = swap(sent[p], orders[p][s])
            cur[p] = kept[p] + got[:, :half]
            sums[p] = sums[p] + got[:, half:]
    for s in reversed(range(steps)):
        for p in range(count):
            upper = (me & orders[p][s]) != 0
            got = swap(cur[p], orders[p][s])
            cur[p] = jnp.concatenate(
                [jnp.where(upper, got, cur[p]), jnp.where(upper, cur[p], got)], axis=1
            )
    return cur, sums


def on_device(frames, ref_weight):
    rows, pixels = frames.shape
    groups = pixels // GROUP
    size = lax.axis_size("tm")
    total_frames = rows * size
    block = pl.BlockSpec((rows, GROUP), lambda g: (0, g))
    sums, edge = pl.pallas_call(
        edge_kernel,
        grid=(groups,),
        in_specs=[block, pl.BlockSpec((1, GROUP), lambda g: (0, g))],
        out_specs=[pl.BlockSpec((rows + SUB, 1), lambda g: (0, 0)), by_group(EDGE_ROWS)],
        out_shape=[f32(rows + SUB, 1), f32(groups, EDGE_ROWS * SUB, LANE)],
        scratch_shapes=[
            pltpu.VMEM((rows * SUB, LANE), jnp.float32),
            pltpu.VMEM((rows + SUB, LANE), jnp.float32),
        ],
        compiler_params=params(),
        name="edges",
    )(frames, ref_weight.reshape(1, pixels))
    back = [(i, i - 1) for i in range(1, size)]
    next_edge = lax.ppermute(edge, "tm", back)
    sums = lax.psum(sums[:, 0], "pix")
    mean = sums[:rows] / sums[rows]
    next_mean = lax.ppermute(mean, "tm", back)
    totals, last, pixel_sum = pl.pallas_call(
        inner_kernel,
        grid=(groups,),
        in_specs=[SMEM, block],
        out_specs=[by_group(ROWS), by_group(ROWS), by_group(1)],
        out_shape=[
            f32(groups, ROWS * SUB, LANE),
            f32(groups, ROWS * SUB, LANE),
            f32(groups, SUB, LANE),
        ],
        scratch_shapes=[pltpu.VMEM((rows * SUB, LANE), jnp.float32)],
        compiler_params=params(),
        name="inner",
    )(mean, frames)
    totals = pl.pallas_call(
        border_kernel,
        grid=(groups,),
        in_specs=[SMEM, by_group(EDGE_ROWS), by_group(ROWS), by_group(ROWS)],
        out_specs=by_group(ROWS),
        out_shape=f32(groups, ROWS * SUB, LANE),
        compiler_params=params(),
        name="border",
    )(next_mean, next_edge, last, totals)
    bits = [1 << b for b in range(size.bit_length() - 1)]
    turn = bits[:-1]
    orders = [turn + bits[-1:], turn[1:] + turn[:1] + bits[-1:]]
    cut = groups // 2
    parts = [(totals[:cut], pixel_sum[:cut]), (totals[cut:], pixel_sum[cut:])]
    cur, sums = sum_parts(parts, orders)
    totals = jnp.concatenate(cur, axis=0)
    pixel_sum = jnp.concatenate(sums, axis=0)
    return pl.pallas_call(
        functools.partial(finish_kernel, total_frames),
        grid=(groups,),
        in_specs=[by_group(ROWS), by_group(1)],
        out_specs=pl.BlockSpec((LEVELS, LAGS, GROUP), lambda g: (0, 0, g)),
        out_shape=f32(LEVELS, LAGS, pixels),
        compiler_params=params(),
        name="finish",
    )(totals, pixel_sum)


def solution(mesh):
    return jax.shard_map(
        on_device,
        mesh=mesh,
        in_specs=(P("tm", "pix"), P("pix")),
        out_specs=P(None, None, "pix"),
        check_vma=False,
    )
```

time: 274 us -> 122 us (0.45)
  blocking collectives: 90.8 us -> 2.59 us
  other arithmetic: 87.7 us -> 5.46 us
  Pallas kernels: 0 us -> 24.4 us
  starting transfers between devices: 5.57 us -> 23.4 us
  local copies, waits for them, and re-layouts: 24.4 us -> 7.71 us
  between operations: 13.6 us -> 0.36 us
  waiting for transfers between devices: 50.9 us -> 57.2 us
    psum x2 -> x1, blocking collectives: 90.8 us -> 2.59 us  [on_device(): sums = lax.psum(sums[:, 0], 'pix')]
    reduce_sum x13 -> x0, other arithmetic: 76.3 us -> none  [the longest x8 55.9 us: lag_sums(): jnp.sum(extended[:row_count] * extended[lag_index:lag_index + row_count],...]
    ppermute x4 -> x18, waiting for transfers between devices: 0.01 us -> 57.2 us  [the longest x16 47.3 us: swap(): return lax.ppermute(block, 'tm', [(i, i ^ mask) for i in range(size)])]
    psum x1 -> x0, waiting for transfers between devices: 50.9 us -> none  [on_device(): summed, column_all = lax.psum((partial_value, column_sum), 'tm')]
    pallas_call x0 -> x4, Pallas kernels: none -> 24.4 us  [the longest x1 14.6 us: on_device(): pl.pallas_call(inner_kernel, grid=(groups,), in_specs=[SMEM, block], out_...]
    ppermute x4 -> x18, starting transfers between devices: 5.56 us -> 23.4 us  [the longest x16 20.8 us: swap(): return lax.ppermute(block, 'tm', [(i, i ^ mask) for i in range(size)])]
    another operation x4 -> x0, local copies, waits for them, and re-layouts: 10.2 us -> none  [lag_sums(): jnp.stack([jnp.sum(extended[:row_count] * extended[lag_index:lag_index +...]
    reshape x1 -> x0, local copies, waits for them, and re-layouts: 5.82 us -> none  [coarsen(): return series.reshape(half_rows, 2, series.shape[1]).sum(axis=1) * 0.5]
  transfers between devices with their start and end apart: 5 -> 18, of which waited for: 1 -> 14; matrix products, arithmetic and copies ran while one was open for 32% -> 2% of each run, Pallas kernels for 0% -> 12%
where the time goes in v1:
time: 122 us; the launch traced here: 121 us
  waiting for transfers between devices  57.2 us (47%)
  Pallas kernels  24.4 us (20%)
  starting transfers between devices  23.4 us (19%)
  local copies, waits for them, and re-layouts  7.71 us (6%)
  other arithmetic  5.46 us (4%)
  blocking collectives  2.59 us (2%)
    ppermute x16, waiting for transfers between devices, swap(): return lax.ppermute(block, 'tm', [(i, i ^ mask) for i in range(size)])  47.3 us
    ppermute x16, starting transfers between devices, swap(): return lax.ppermute(block, 'tm', [(i, i ^ mask) for i in range(size)])  20.8 us
    pallas_call x1, Pallas kernels, on_device(): pl.pallas_call(inner_kernel, grid=(groups,), in_specs=[SMEM, block], out_...  14.6 us
    ppermute x1, waiting for transfers between devices, on_device(): next_mean = lax.ppermute(mean, 'tm', back)  9.91 us
    unnamed x10, local copies, waits for them, and re-layouts  7.19 us
    pallas_call x1, Pallas kernels, on_device(): pl.pallas_call(border_kernel, grid=(groups,), in_specs=[SMEM, by_group(ED...  4.92 us
    pallas_call x1, Pallas kernels, on_device(): pl.pallas_call(functools.partial(finish_kernel, total_frames), grid=(grou...  3.15 us
    psum x1, blocking collectives, on_device(): sums = lax.psum(sums[:, 0], 'pix')  2.59 us
  transfers between devices with their start and end apart: 18, of which 14 were waited for; matrix products, arithmetic and copies ran while one was open for 2% of the time, Pallas kernels for 12%

profile of v1, /device:TPU:0, one launch (start us, length us, event | category | flops | bytes accessed | tf_op | source)
XLA Modules:
  0.0 121.1 jit_solution(2833641945213602505)
XLA Ops:
  0.0 2.2 %copy-done = f32[128,8192]{1,0:T(8,128)S(1)} copy-done((f32[128,8192]{1,0:T(8,128)S(1)}, f32[128,8192]{1,0:T(8,128)}, u32[]{:S(2)}) %copy-start) | copy-done | bytes 4194328
  2.9 1.7 %edges.1 = (f32[136,1]{1,0:T(8,128)S(1)}, f32[8,320,128]{2,1,0:T(8,128)S(1)}) custom-call(f32[128,8192]{1,0:T(8,128)S(1)} %copy-done, f32[1,8192]{1,0:T(1,128)S(1)} %bitcast.2), custom_call_target="tpu_custom_call" | custom-call | tf_op jit(solution)/shard_map/edges/pallas_call | solution.py:226
  6.0 2.6 %psum.7 = f32[136]{0:T(256)S(1)} all-reduce(f32[136]{0:T(256)S(1)} %reduce), channel_id=1, replica_groups=mesh['tm'=16,'pix'=2] {'pix'}, use_global_device_ids=true, to_apply=%region_0.0 | all-reduce | flops 136 | bytes 1088 | tf_op jit(solution)/shard_map/psum | solution.py:241
  11.1 14.6 %inner.1 = (f32[8,512,128]{2,1,0:T(8,128)S(1)}, f32[8,512,128]{2,1,0:T(8,128)S(1)}, f32[8,8,128]{2,1,0:T(8,128)S(1)}) custom-call(f32[128]{0:T(128)S(1)} %slice_divide_fusion.mean_ref, f32[128,8192]{1,0:T(8,128)} %x_ref.3), custom_call_target="tpu_custom_call" | custom-call | tf_op jit(solution)/shard_map/inner/pallas_call | solution.py:244
  28.4 9.9 %collective-permute-done.mean_ref = f32[128]{0:T(128)S(1)} collective-permute-done((f32[128]{0:T(128)S(1)}, f32[128]{0:T(128)S(1)}, u32[]{:S(2)}, u32[]{:S(2)}) %collective-permute-start) | collective-permute-done | bytes 544 | tf_op jit(solution)/shard_map/ppermute | solution.py:243
  39.9 4.9 %border.1 = f32[8,512,128]{2,1,0:T(8,128)S(1)} custom-call(f32[128]{0:T(128)S(1)} %collective-permute-done.mean_ref, f32[8,320,128]{2,1,0:T(8,128)S(1)} %collective-permute-done.1.edge_ref, f32[8,512,128]{2,1,0:T(8,128)S(1)} %copy-done.3, f32[8,512,128]{2,1,0:T(8,128)} %copy-done.1), custom_call_target="tpu_custom_call" | custom-call | tf_op jit(solution)/shard_map/border/pallas_call | solution.py:258
  45.8 1.8 %collective-permute-start.10 = (f32[4,264,128]{2,1,0:T(8,128)}, f32[4,264,128]{2,1,0:T(8,128)S(1)}, u32[]{:S(2)}, u32[]{:S(2)}) collective-permute-start(f32[4,264,128]{2,1,0:T(8,128)} %pad_maximum_fusion.1), channel_id=1, source_target_pairs={{0,4},{2,6},{4,0},{6,2},{8,12},{10,14},{12,8},{14,10},{16,20},{18,... | collective-permute-start | bytes 1622024 | tf_op jit(solution)/shard_map/ppermute | solution.py:186
  48.4 3.3 %collective-permute-start.2 = (f32[4,264,128]{2,1,0:T(8,128)}, f32[4,264,128]{2,1,0:T(8,128)}, u32[]{:S(2)}, u32[]{:S(2)}) collective-permute-start(f32[4,264,128]{2,1,0:T(8,128)} %pad_maximum_fusion), channel_id=1, source_target_pairs={{0,2},{2,0},{4,6},{6,4},{8,10},{10,8},{12,14},{14,12},{16,18},{18,... | collective-permute-start | bytes 1622024 | tf_op jit(solution)/shard_map/ppermute | solution.py:186
  51.7 7.7 %collective-permute-done.10 = f32[4,264,128]{2,1,0:T(8,128)S(1)} collective-permute-done((f32[4,264,128]{2,1,0:T(8,128)}, f32[4,264,128]{2,1,0:T(8,128)S(1)}, u32[]{:S(2)}, u32[]{:S(2)}) %collective-permute-start.10) | collective-permute-done | bytes 540704 | tf_op jit(solution)/shard_map/ppermute | solution.py:186
  59.4 3.6 %collective-permute-done.2 = f32[4,264,128]{2,1,0:T(8,128)} collective-permute-done((f32[4,264,128]{2,1,0:T(8,128)}, f32[4,264,128]{2,1,0:T(8,128)}, u32[]{:S(2)}, u32[]{:S(2)}) %collective-permute-start.2) | collective-permute-done | bytes 540704 | tf_op jit(solution)/shard_map/ppermute | solution.py:186
  65.5 1.6 %collective-permute-start.11 = (f32[4,136,128]{2,1,0:T(8,128)S(1)}, f32[4,136,128]{2,1,0:T(8,128)S(1)}, u32[]{:S(2)}, u32[]{:S(2)}) collective-permute-start(f32[4,136,128]{2,1,0:T(8,128)S(1)} %pad_maximum_fusion.5), channel_id=1, source_target_pairs={{0,8},{2,10},{4,12},{6,14},{8,0},{10,2},{12,4},{14,6},{16,24},{18,... | collective-permute-start | bytes 835592 | tf_op jit(solution)/shard_map/ppermute | solution.py:186
  67.1 4.6 %collective-permute-done.3 = f32[4,136,128]{2,1,0:T(8,128)S(1)} collective-permute-done((f32[4,136,128]{2,1,0:T(8,128)S(1)}, f32[4,136,128]{2,1,0:T(8,128)S(1)}, u32[]{:S(2)}, u32[]{:S(2)}) %collective-permute-start.3) | collective-permute-done | bytes 278560 | tf_op jit(solution)/shard_map/ppermute | solution.py:186
  73.6 1.8 %collective-permute-start.12 = (f32[4,72,128]{2,1,0:T(8,128)S(1)}, f32[4,72,128]{2,1,0:T(8,128)S(1)}, u32[]{:S(2)}, u32[]{:S(2)}) collective-permute-start(f32[4,72,128]{2,1,0:T(8,128)S(1)} %pad_maximum_fusion.9), channel_id=1, source_target_pairs={{0,2},{2,0},{4,6},{6,4},{8,10},{10,8},{12,14},{14,12},{16,18},{18,... | collective-permute-start | bytes 442376 | tf_op jit(solution)/shard_map/ppermute | solution.py:186
  77.1 3.5 %collective-permute-start.5 = (f32[4,40,128]{2,1,0:T(8,128)S(1)}, f32[4,40,128]{2,1,0:T(8,128)S(1)}, u32[]{:S(2)}, u32[]{:S(2)}) collective-permute-start(f32[4,40,128]{2,1,0:T(8,128)S(1)} %pad_maximum_fusion.12), channel_id=1, source_target_pairs={{0,16},{2,18},{4,20},{6,22},{8,24},{10,26},{12,28},{14,30},{16,0},... | collective-permute-start | bytes 245768 | tf_op jit(solution)/shard_map/ppermute | solution.py:186
  80.9 4.9 %collective-permute-done.5 = f32[4,40,128]{2,1,0:T(8,128)S(1)} collective-permute-done((f32[4,40,128]{2,1,0:T(8,128)S(1)}, f32[4,40,128]{2,1,0:T(8,128)S(1)}, u32[]{:S(2)}, u32[]{:S(2)}) %collective-permute-start.5) | collective-permute-done | bytes 81952 | tf_op jit(solution)/shard_map/ppermute | solution.py:186
  88.9 2.1 %collective-permute-done.6 = f32[4,32,128]{2,1,0:T(8,128)S(1)} collective-permute-done((f32[4,32,128]{2,1,0:T(8,128)S(1)}, f32[4,32,128]{2,1,0:T(8,128)S(1)}, u32[]{:S(2)}, u32[]{:S(2)}) %collective-permute-start.6) | collective-permute-done | bytes 65568 | tf_op jit(solution)/shard_map/ppermute | solution.py:186
  91.1 2.3 %collective-permute-done.14 = f32[4,32,128]{2,1,0:T(8,128)S(1)} collective-permute-done((f32[4,32,128]{2,1,0:T(8,128)S(1)}, f32[4,32,128]{2,1,0:T(8,128)S(1)}, u32[]{:S(2)}, u32[]{:S(2)}) %collective-permute-start.14) | collective-permute-done | bytes 65568 | tf_op jit(solution)/shard_map/ppermute | solution.py:186
  93.5 1.8 %collective-permute-start.15 = (f32[4,64,128]{2,1,0:T(8,128)S(1)}, f32[4,64,128]{2,1,0:T(8,128)S(1)}, u32[]{:S(2)}, u32[]{:S(2)}) collective-permute-start(f32[4,64,128]{2,1,0:T(8,128)S(1)} %pad_maximum_fusion.11), channel_id=1, source_target_pairs={{0,2},{2,0},{4,6},{6,4},{8,10},{10,8},{12,14},{14,12},{16,18},{18,... | collective-permute-start | bytes 393224 | tf_op jit(solution)/shard_map/ppermute | solution.py:186
  95.3 2.1 %collective-permute-done.7 = f32[4,64,128]{2,1,0:T(8,128)S(1)} collective-permute-done((f32[4,64,128]{2,1,0:T(8,128)S(1)}, f32[4,64,128]{2,1,0:T(8,128)S(1)}, u32[]{:S(2)}, u32[]{:S(2)}) %collective-permute-start.7) | collective-permute-done | bytes 131104 | tf_op jit(solution)/shard_map/ppermute | solution.py:186
  100.0 6.6 %collective-permute-done.8 = f32[4,128,128]{2,1,0:T(8,128)S(1)} collective-permute-done((f32[4,128,128]{2,1,0:T(8,128)S(1)}, f32[4,128,128]{2,1,0:T(8,128)S(1)}, u32[]{:S(2)}, u32[]{:S(2)}) %collective-permute-start.8) | collective-permute-done | bytes 262176 | tf_op jit(solution)/shard_map/ppermute | solution.py:186
  106.7 1.7 %collective-permute-start.9 = (f32[4,256,128]{2,1,0:T(8,128)S(1)}, f32[4,256,128]{2,1,0:T(8,128)S(1)}, u32[]{:S(2)}, u32[]{:S(2)}) collective-permute-start(f32[4,256,128]{2,1,0:T(8,128)S(1)} %pad_maximum_fusion.2), channel_id=1, source_target_pairs={{0,2},{2,0},{4,6},{6,4},{8,10},{10,8},{12,14},{14,12},{16,18},{18,... | collective-permute-start | bytes 1572872 | tf_op jit(solution)/shard_map/ppermute | solution.py:186
  108.5 7.4 %collective-permute-done.9 = f32[4,256,128]{2,1,0:T(8,128)S(1)} collective-permute-done((f32[4,256,128]{2,1,0:T(8,128)S(1)}, f32[4,256,128]{2,1,0:T(8,128)S(1)}, u32[]{:S(2)}, u32[]{:S(2)}) %collective-permute-start.9) | collective-permute-done | bytes 524320 | tf_op jit(solution)/shard_map/ppermute | solution.py:186
  116.0 1.7 %collective-permute-done.17 = f32[4,256,128]{2,1,0:T(8,128)S(1)} collective-permute-done((f32[4,256,128]{2,1,0:T(8,128)S(1)}, f32[4,256,128]{2,1,0:T(8,128)S(1)}, u32[]{:S(2)}, u32[]{:S(2)}) %collective-permute-start.17) | collective-permute-done | bytes 524320 | tf_op jit(solution)/shard_map/ppermute | solution.py:186
  117.9 3.1 %finish.1 = f32[4,16,8192]{2,1,0:T(8,128)} custom-call(f32[8,512,128]{2,1,0:T(8,128)S(1)} %maximum_maximum_fusion.totals_ref, f32[8,8,128]{2,1,0:T(8,128)S(1)} %pad_maximum_fusion.14.sum_ref), custom_call_target="tpu_custom_call" | custom-call | tf_op jit(solution)/shard_map/finish/pallas_call | solution.py:275
  (76 shorter events, 23.0 us)
Async XLA Ops:
  0.0 2.2 %copy-start = (f32[128,8192]{1,0:T(8,128)S(1)}, f32[128,8192]{1,0:T(8,128)}, u32[]{:S(2)}) copy-start(f32[128,8192]{1,0:T(8,128)} %x_ref.3) | copy-start | bytes 12582916
  2.2 0.8 copy-start.4
  4.6 33.7 %collective-permute-start.1 = (f32[8,320,128]{2,1,0:T(8,128)S(1)}, f32[8,320,128]{2,1,0:T(8,128)S(1)}, u32[]{:S(2)}, u32[]{:S(2)}) collective-permute-start(f32[8,320,128]{2,1,0:T(8,128)S(1)} %get-tuple-element.11), channel_id=1, source_target_pairs={{2,0},{4,2},{6,4},{8,6},{10,8},{12,10},{14,12},{16,14},{18,16},{20... | collective-permute-start | bytes 3932168 | tf_op jit(solution)/shard_map/ppermute | solution.py:240
  9.8 28.5 %collective-permute-start = (f32[128]{0:T(128)S(1)}, f32[128]{0:T(128)S(1)}, u32[]{:S(2)}, u32[]{:S(2)}) collective-permute-start(f32[128]{0:T(128)S(1)} %slice_divide_fusion.mean_ref), channel_id=1, source_target_pairs={{2,0},{4,2},{6,4},{8,6},{10,8},{12,10},{14,12},{16,14},{18,16},{20... | collective-permute-start | bytes 1544 | tf_op jit(solution)/shard_map/ppermute | solution.py:243
  25.7 1.3 %copy-start.1 = (f32[8,512,128]{2,1,0:T(8,128)}, f32[8,512,128]{2,1,0:T(8,128)S(1)}, u32[]{:S(2)}) copy-start(f32[8,512,128]{2,1,0:T(8,128)S(1)} %get-tuple-element.13.totals_ref) | copy-start | bytes 6291460
  27.1 1.3 %copy-start.2 = (f32[8,512,128]{2,1,0:T(8,128)}, f32[8,512,128]{2,1,0:T(8,128)S(1)}, u32[]{:S(2)}) copy-start(f32[8,512,128]{2,1,0:T(8,128)S(1)} %get-tuple-element.12.last_ref) | copy-start | bytes 6291460
  38.3 1.6 %copy-start.3 = (f32[8,512,128]{2,1,0:T(8,128)S(1)}, f32[8,512,128]{2,1,0:T(8,128)}, u32[]{:S(2)}) copy-start(f32[8,512,128]{2,1,0:T(8,128)} %copy-done.2) | copy-start | bytes 6291460
  45.8 13.6 %collective-permute-start.10 = (f32[4,264,128]{2,1,0:T(8,128)}, f32[4,264,128]{2,1,0:T(8,128)S(1)}, u32[]{:S(2)}, u32[]{:S(2)}) collective-permute-start(f32[4,264,128]{2,1,0:T(8,128)} %pad_maximum_fusion.1), channel_id=1, source_target_pairs={{0,4},{2,6},{4,0},{6,2},{8,12},{10,14},{12,8},{14,10},{16,20},{18,... | collective-permute-start | bytes 1622024 | tf_op jit(solution)/shard_map/ppermute | solution.py:186
  48.4 14.7 %collective-permute-start.2 = (f32[4,264,128]{2,1,0:T(8,128)}, f32[4,264,128]{2,1,0:T(8,128)}, u32[]{:S(2)}, u32[]{:S(2)}) collective-permute-start(f32[4,264,128]{2,1,0:T(8,128)} %pad_maximum_fusion), channel_id=1, source_target_pairs={{0,2},{2,0},{4,6},{6,4},{8,10},{10,8},{12,14},{14,12},{16,18},{18,... | collective-permute-start | bytes 1622024 | tf_op jit(solution)/shard_map/ppermute | solution.py:186
  65.1 6.6 %collective-permute-start.3 = (f32[4,136,128]{2,1,0:T(8,128)S(1)}, f32[4,136,128]{2,1,0:T(8,128)S(1)}, u32[]{:S(2)}, u32[]{:S(2)}) collective-permute-start(f32[4,136,128]{2,1,0:T(8,128)S(1)} %pad_maximum_fusion.4), channel_id=1, source_target_pairs={{0,4},{2,6},{4,0},{6,2},{8,12},{10,14},{12,8},{14,10},{16,20},{18,... | collective-permute-start | bytes 835592 | tf_op jit(solution)/shard_map/ppermute | solution.py:186
  65.5 8.0 %collective-permute-start.11 = (f32[4,136,128]{2,1,0:T(8,128)S(1)}, f32[4,136,128]{2,1,0:T(8,128)S(1)}, u32[]{:S(2)}, u32[]{:S(2)}) collective-permute-start(f32[4,136,128]{2,1,0:T(8,128)S(1)} %pad_maximum_fusion.5), channel_id=1, source_target_pairs={{0,8},{2,10},{4,12},{6,14},{8,0},{10,2},{12,4},{14,6},{16,24},{18,... | collective-permute-start | bytes 835592 | tf_op jit(solution)/shard_map/ppermute | solution.py:186
  71.8 5.2 %collective-permute-start.4 = (f32[4,72,128]{2,1,0:T(8,128)S(1)}, f32[4,72,128]{2,1,0:T(8,128)S(1)}, u32[]{:S(2)}, u32[]{:S(2)}) collective-permute-start(f32[4,72,128]{2,1,0:T(8,128)S(1)} %pad_maximum_fusion.8), channel_id=1, source_target_pairs={{0,8},{2,10},{4,12},{6,14},{8,0},{10,2},{12,4},{14,6},{16,24},{18,... | collective-permute-start | bytes 442376 | tf_op jit(solution)/shard_map/ppermute | solution.py:186
  73.6 7.1 %collective-permute-start.12 = (f32[4,72,128]{2,1,0:T(8,128)S(1)}, f32[4,72,128]{2,1,0:T(8,128)S(1)}, u32[]{:S(2)}, u32[]{:S(2)}) collective-permute-start(f32[4,72,128]{2,1,0:T(8,128)S(1)} %pad_maximum_fusion.9), channel_id=1, source_target_pairs={{0,2},{2,0},{4,6},{6,4},{8,10},{10,8},{12,14},{14,12},{16,18},{18,... | collective-permute-start | bytes 442376 | tf_op jit(solution)/shard_map/ppermute | solution.py:186
  77.1 8.7 %collective-permute-start.5 = (f32[4,40,128]{2,1,0:T(8,128)S(1)}, f32[4,40,128]{2,1,0:T(8,128)S(1)}, u32[]{:S(2)}, u32[]{:S(2)}) collective-permute-start(f32[4,40,128]{2,1,0:T(8,128)S(1)} %pad_maximum_fusion.12), channel_id=1, source_target_pairs={{0,16},{2,18},{4,20},{6,22},{8,24},{10,26},{12,28},{14,30},{16,0},... | collective-permute-start | bytes 245768 | tf_op jit(solution)/shard_map/ppermute | solution.py:186
  80.7 7.1 %collective-permute-start.13 = (f32[4,40,128]{2,1,0:T(8,128)S(1)}, f32[4,40,128]{2,1,0:T(8,128)S(1)}, u32[]{:S(2)}, u32[]{:S(2)}) collective-permute-start(f32[4,40,128]{2,1,0:T(8,128)S(1)} %pad_maximum_fusion.13), channel_id=1, source_target_pairs={{0,16},{2,18},{4,20},{6,22},{8,24},{10,26},{12,28},{14,30},{16,0},... | collective-permute-start | bytes 245768 | tf_op jit(solution)/shard_map/ppermute | solution.py:186
  85.8 5.2 %collective-permute-start.6 = (f32[4,32,128]{2,1,0:T(8,128)S(1)}, f32[4,32,128]{2,1,0:T(8,128)S(1)}, u32[]{:S(2)}, u32[]{:S(2)}) collective-permute-start(f32[4,32,128]{2,1,0:T(8,128)S(1)} %slice_add_fusion.7), channel_id=1, source_target_pairs={{0,16},{2,18},{4,20},{6,22},{8,24},{10,26},{12,28},{14,30},{16,0},... | collective-permute-start | bytes 196616 | tf_op jit(solution)/shard_map/ppermute | solution.py:186
  87.8 5.7 %collective-permute-start.14 = (f32[4,32,128]{2,1,0:T(8,128)S(1)}, f32[4,32,128]{2,1,0:T(8,128)S(1)}, u32[]{:S(2)}, u32[]{:S(2)}) collective-permute-start(f32[4,32,128]{2,1,0:T(8,128)S(1)} %slice_add_fusion.6), channel_id=1, source_target_pairs={{0,16},{2,18},{4,20},{6,22},{8,24},{10,26},{12,28},{14,30},{16,0},... | collective-permute-start | bytes 196616 | tf_op jit(solution)/shard_map/ppermute | solution.py:186
  91.0 6.4 %collective-permute-start.7 = (f32[4,64,128]{2,1,0:T(8,128)S(1)}, f32[4,64,128]{2,1,0:T(8,128)S(1)}, u32[]{:S(2)}, u32[]{:S(2)}) collective-permute-start(f32[4,64,128]{2,1,0:T(8,128)S(1)} %pad_maximum_fusion.10), channel_id=1, source_target_pairs={{0,8},{2,10},{4,12},{6,14},{8,0},{10,2},{12,4},{14,6},{16,24},{18,... | collective-permute-start | bytes 393224 | tf_op jit(solution)/shard_map/ppermute | solution.py:186
  93.5 5.7 %collective-permute-start.15 = (f32[4,64,128]{2,1,0:T(8,128)S(1)}, f32[4,64,128]{2,1,0:T(8,128)S(1)}, u32[]{:S(2)}, u32[]{:S(2)}) collective-permute-start(f32[4,64,128]{2,1,0:T(8,128)S(1)} %pad_maximum_fusion.11), channel_id=1, source_target_pairs={{0,2},{2,0},{4,6},{6,4},{8,10},{10,8},{12,14},{14,12},{16,18},{18,... | collective-permute-start | bytes 393224 | tf_op jit(solution)/shard_map/ppermute | solution.py:186
  97.5 9.1 %collective-permute-start.8 = (f32[4,128,128]{2,1,0:T(8,128)S(1)}, f32[4,128,128]{2,1,0:T(8,128)S(1)}, u32[]{:S(2)}, u32[]{:S(2)}) collective-permute-start(f32[4,128,128]{2,1,0:T(8,128)S(1)} %pad_maximum_fusion.6), channel_id=1, source_target_pairs={{0,4},{2,6},{4,0},{6,2},{8,12},{10,14},{12,8},{14,10},{16,20},{18,... | collective-permute-start | bytes 786440 | tf_op jit(solution)/shard_map/ppermute | solution.py:186
  99.2 9.1 %collective-permute-start.16 = (f32[4,128,128]{2,1,0:T(8,128)S(1)}, f32[4,128,128]{2,1,0:T(8,128)S(1)}, u32[]{:S(2)}, u32[]{:S(2)}) collective-permute-start(f32[4,128,128]{2,1,0:T(8,128)S(1)} %pad_maximum_fusion.7), channel_id=1, source_target_pairs={{0,8},{2,10},{4,12},{6,14},{8,0},{10,2},{12,4},{14,6},{16,24},{18,... | collective-permute-start | bytes 786440 | tf_op jit(solution)/shard_map/ppermute | solution.py:186
  106.7 9.2 %collective-permute-start.9 = (f32[4,256,128]{2,1,0:T(8,128)S(1)}, f32[4,256,128]{2,1,0:T(8,128)S(1)}, u32[]{:S(2)}, u32[]{:S(2)}) collective-permute-start(f32[4,256,128]{2,1,0:T(8,128)S(1)} %pad_maximum_fusion.2), channel_id=1, source_target_pairs={{0,2},{2,0},{4,6},{6,4},{8,10},{10,8},{12,14},{14,12},{16,18},{18,... | collective-permute-start | bytes 1572872 | tf_op jit(solution)/shard_map/ppermute | solution.py:186
  108.4 9.2 %collective-permute-start.17 = (f32[4,256,128]{2,1,0:T(8,128)S(1)}, f32[4,256,128]{2,1,0:T(8,128)S(1)}, u32[]{:S(2)}, u32[]{:S(2)}) collective-permute-start(f32[4,256,128]{2,1,0:T(8,128)S(1)} %pad_maximum_fusion.3), channel_id=1, source_target_pairs={{0,4},{2,6},{4,0},{6,2},{8,12},{10,14},{12,8},{14,10},{16,20},{18,... | collective-permute-start | bytes 1572872 | tf_op jit(solution)/shard_map/ppermute | solution.py:186

commit v2 on v1

v2 whole, which is shorter than its diff:
```python
import functools

import jax
import jax.numpy as jnp
from jax import lax
from jax.experimental import pallas as pl
from jax.experimental.pallas import tpu as pltpu
from jax.sharding import PartitionSpec as P

LEVELS = 4
LAGS = 16
SUB, LANE = 8, 128
GROUP = SUB * LANE
VMEM_LIMIT = 16 * 1024 * 1024


def stack_tile(x_ref, tall_ref, row_tiles):
    for i in range(row_tiles):
        for c in range(SUB):
            tall_ref[pl.ds(i * SUB * SUB + c, SUB, stride=SUB), :] = x_ref[
                i * SUB : (i + 1) * SUB, c * LANE : (c + 1) * LANE
            ]


def tile(ref, row):
    return ref[row * SUB : (row + 1) * SUB, :]


def edge_kernel(x_hbm, w_hbm, sums_ref, edge_ref, x_ref, w_ref, tall_ref, acc_ref, sem, w_sem):
    groups, rows, _ = x_ref.shape
    half = LAGS // 2

    def fetch(g):
        at = pl.ds(pl.multiple_of(g * GROUP, GROUP), GROUP)
        return pltpu.make_async_copy(x_hbm.at[:, at], x_ref.at[g], sem.at[g])

    weights = pltpu.make_async_copy(w_hbm, w_ref, w_sem)
    weights.start()
    for g in range(groups):
        fetch(g).start()
    acc_ref[...] = jnp.zeros_like(acc_ref)
    weights.wait()

    def one_group(g, carry):
        fetch(g).wait()
        for c in range(SUB):
            at = pl.ds(pl.multiple_of(g * GROUP + c * LANE, LANE), LANE)
            weight = jnp.broadcast_to(w_ref[:, at], (SUB, LANE))
            acc_ref[rows : rows + SUB, :] += weight
            for i in range(rows // SUB):
                part = slice(i * SUB, (i + 1) * SUB)
                value = x_ref[g, part, c * LANE : (c + 1) * LANE]
                acc_ref[part, :] += value * weight
                tall_ref[pl.ds(i * SUB * SUB + c, SUB, stride=SUB), :] = value
        edge_ref[g, : LAGS * SUB, :] = tall_ref[: LAGS * SUB, :]
        for level in range(1, LEVELS):
            span = 1 << level
            for j in range(half):
                group = [tile(tall_ref, (half + j) * span + s) for s in range(span)]
                while len(group) > 1:
                    group = [(a + b) * 0.5 for a, b in zip(group[::2], group[1::2])]
                row = LAGS + (level - 1) * half + j
                edge_ref[g, row * SUB : (row + 1) * SUB, :] = group[0]
        return carry

    lax.fori_loop(0, groups, one_group, 0)
    sums_ref[...] = jnp.sum(acc_ref[...], axis=1, keepdims=True)


def lag_step(old, new, totals):
    out = list(totals)
    for k in range(1, LAGS + 1):
        terms = []
        for i in range(LAGS):
            if i + k < LAGS:
                terms.append(old[i] * old[i + k])
            elif new is not None:
                terms.append(old[i] * new[i + k - LAGS])
        if terms:
            total = terms[0]
            for term in terms[1:]:
                total = total + term
            out[k - 1] = out[k - 1] + total
    return out


def inner_kernel(mean_ref, x_ref, totals_ref, last_ref, sum_ref, series_ref):
    rows = x_ref.shape[0]
    stack_tile(x_ref, series_ref, rows // SUB)

    def add_mean(t, total):
        at = pl.ds(pl.multiple_of(t * SUB, SUB), SUB)
        value = series_ref[at, :] + mean_ref[t]
        series_ref[at, :] = value
        return total + value

    sum_ref[0] = lax.fori_loop(
        0, rows, add_mean, jnp.zeros((SUB, LANE), jnp.float32), unroll=8
    )
    zero = jnp.zeros((SUB, LANE), jnp.float32)
    for level in range(LEVELS):
        count = rows >> level
        chunks = count // LAGS

        def load(chunk):
            start = pl.multiple_of(chunk * LAGS * SUB, SUB)
            block = series_ref[pl.ds(start, LAGS * SUB), :]
            return [block[i * SUB : (i + 1) * SUB] for i in range(LAGS)]

        def body(chunk, totals):
            return tuple(lag_step(load(chunk), load(chunk + 1), totals))

        totals = tuple([zero] * LAGS)
        if chunks > 1:
            totals = lax.fori_loop(0, chunks - 1, body, totals)
        old = load(chunks - 1)
        totals = lag_step(old, None, totals)
        for i in range(LAGS):
            row = level * LAGS + i
            totals_ref[0, row * SUB : (row + 1) * SUB, :] = totals[i]
            last_ref[0, row * SUB : (row + 1) * SUB, :] = old[i]
        if level < LEVELS - 1:
            def coarsen(i, carry):
                start = pl.multiple_of(i * 2 * SUB, SUB)
                pair = series_ref[pl.ds(start, 2 * SUB), :]
                series_ref[pl.ds(pl.multiple_of(i * SUB, SUB), SUB), :] = (
                    pair[:SUB] + pair[SUB:]
                ) * 0.5
                return carry

            lax.fori_loop(0, count // 2, coarsen, 0, unroll=4)


def border_kernel(first, mean_ref, side_ref, edge_ref, last_ref, totals_ref,
                  sum_ref, kept_ref, sent_ref, level_mean_ref):
    half = LAGS // 2
    split = LEVELS // 2
    side = side_ref[0]
    groups = kept_ref.shape[0]
    for j in range(LAGS):
        level_mean_ref[j] = mean_ref[j]
    for level in range(1, LEVELS):
        span = 1 << level
        for j in range(half):
            group = [mean_ref[(half + j) * span + s] for s in range(span)]
            while len(group) > 1:
                group = [(a + b) * 0.5 for a, b in zip(group[::2], group[1::2])]
            level_mean_ref[LAGS + (level - 1) * half + j] = group[0]

    def one_group(slot, carry):
        g = slot + first
        sent_ref[slot, ROWS // 2 * SUB :, :] = sum_ref[slot]
        new = [
            edge_ref[g, j * SUB : (j + 1) * SUB, :] + level_mean_ref[j]
            for j in range(LAGS)
        ]
        for level in range(LEVELS):
            if level > 0:
                fresh = [(a + b) * 0.5 for a, b in zip(new[::2], new[1::2])]
                for j in range(half):
                    row = LAGS + (level - 1) * half + j
                    fresh.append(
                        edge_ref[g, row * SUB : (row + 1) * SUB, :] + level_mean_ref[row]
                    )
                new = fresh
            base = level * LAGS
            old = [
                last_ref[slot, (base + i) * SUB : (base + i + 1) * SUB, :]
                for i in range(LAGS)
            ]
            totals = []
            for k in range(1, LAGS + 1):
                row = base + k - 1
                total = totals_ref[slot, row * SUB : (row + 1) * SUB, :]
                for i in range(LAGS - k, LAGS):
                    total = total + old[i] * new[i + k - LAGS]
                totals.append(total)
            upper, base = level // split, (level % split) * LAGS

            def put(ref, totals=totals, base=base):
                for i, total in enumerate(totals):
                    ref[slot, (base + i) * SUB : (base + i + 1) * SUB, :] = total

            pl.when(side == upper)(functools.partial(put, kept_ref))
            pl.when(side != upper)(functools.partial(put, sent_ref))
        return carry

    lax.fori_loop(0, groups, one_group, 0)


def finish_kernel(total_frames, side_ref, mine_ref, got_ref, sum_ref, *refs):
    out_ref = refs[-1]
    split = LEVELS // 2
    g = pl.program_id(0)
    side = side_ref[0]
    for c in range(SUB):
        mean = sum_ref[g, c : c + 1, :] / total_frames
        square = jnp.broadcast_to(mean * mean, (SUB, LANE))
        for level in range(LEVELS):
            own = side == level // split
            for i in range(LAGS // SUB):
                lag = lax.broadcasted_iota(jnp.int32, (SUB, LANE), 0) + (i * SUB + 1)
                count = ((total_frames >> level) - lag).astype(jnp.float32)
                row = (level % split) * LAGS + i * SUB
                at = pl.ds(row * SUB + c, SUB, stride=SUB)
                total = jnp.where(own, mine_ref[g, at, :], got_ref[g, at, :])
                out_ref[level, i * SUB : (i + 1) * SUB, c * LANE : (c + 1) * LANE] = (
                    total / (count * square)
                )


ROWS = LEVELS * LAGS
EDGE_ROWS = LAGS + (LEVELS - 1) * (LAGS // 2)
SMEM = pl.BlockSpec(memory_space=pltpu.SMEM)
VMEM = pl.BlockSpec(memory_space=pltpu.VMEM)


def params():
    return pltpu.CompilerParams(vmem_limit_bytes=VMEM_LIMIT)


def in_hbm(value):
    return pltpu.with_memory_space_constraint(value, pltpu.HBM)


def f32(*shape):
    return jax.ShapeDtypeStruct(shape, jnp.float32)


def by_group(rows):
    return pl.BlockSpec((1, rows * SUB, LANE), lambda g: (g, 0, 0))


def swap(block, mask):
    size = lax.axis_size("tm")
    return lax.ppermute(block, "tm", [(i, i ^ mask) for i in range(size)])


class Part:
    def __init__(self, order, uppers, kept, sent):
        self.order = order
        self.uppers = uppers
        self.step = 0
        self.kept, self.sent = kept, sent
        self.sums = sent[:, kept.shape[1] :]

    def send(self):
        mask = self.order[self.step]
        last = self.step == len(self.order) - 1
        if self.step > 0:
            if last:
                self.kept, self.sent = self.cur, self.cur
            else:
                half = self.cur.shape[1] // 2
                upper = self.uppers[mask]
                low, high = self.cur[:, :half], self.cur[:, half:]
                self.kept = jnp.where(upper, high, low)
                self.sent = jnp.where(upper, low, high)
            self.sent = jnp.concatenate([self.sent, self.sums], axis=1)
        self.got = swap(self.sent, mask)

    def receive(self):
        rows = self.kept.shape[1]
        self.cur = self.kept + self.got[:, :rows]
        self.sums = self.sums + self.got[:, rows:]
        self.step += 1

    def send_back(self, step):
        self.got = swap(self.cur, self.order[step])

    def receive_back(self, step):
        upper = self.uppers[self.order[step]]
        low = jnp.where(upper, self.got, self.cur)
        high = jnp.where(upper, self.cur, self.got)
        self.cur = jnp.concatenate([low, high], axis=1)


def on_device(frames, ref_weight):
    rows, pixels = frames.shape
    groups = pixels // GROUP
    size = lax.axis_size("tm")
    total_frames = rows * size
    bits = [1 << b for b in range(size.bit_length() - 1)]
    me = lax.axis_index("tm")
    uppers = {bit: (me & bit) != 0 for bit in bits}
    sides = {bit: uppers[bit].astype(jnp.int32).reshape(1) for bit in bits[:2]}
    ref_weight, uppers, sides = lax.optimization_barrier((ref_weight, uppers, sides))
    stored = in_hbm(frames)
    back = [(i, i - 1) for i in range(1, size)]
    sums, edge = pl.pallas_call(
        edge_kernel,
        in_specs=[pl.BlockSpec(memory_space=pl.ANY)] * 2,
        out_specs=[VMEM, VMEM],
        out_shape=[f32(rows + SUB, 1), f32(groups, EDGE_ROWS * SUB, LANE)],
        scratch_shapes=[
            pltpu.VMEM((groups, rows, GROUP), jnp.float32),
            pltpu.VMEM((1, pixels), jnp.float32),
            pltpu.VMEM((rows * SUB, LANE), jnp.float32),
            pltpu.VMEM((rows + SUB, LANE), jnp.float32),
            pltpu.SemaphoreType.DMA((groups,)),
            pltpu.SemaphoreType.DMA,
        ],
        compiler_params=params(),
        name="edges",
    )(stored, in_hbm(ref_weight.reshape(1, pixels)))
    next_edge = lax.ppermute(edge, "tm", back)
    sums = lax.psum(sums[:, 0], "pix")
    mean = sums[:rows] / sums[rows]
    next_mean = lax.ppermute(mean, "tm", back)
    orders = [
        bits[:1] + bits[2:3] + bits[1:2] + bits[3:],
        bits[1:2] + bits[:1] + bits[2:],
    ]
    count = groups // 2
    inner = []
    for p in range(len(orders)):
        sums = pl.pallas_call(
            inner_kernel,
            grid=(count,),
            in_specs=[
                SMEM,
                pl.BlockSpec((rows, GROUP), lambda g, first=p * count: (0, g + first)),
            ],
            out_specs=[by_group(ROWS), by_group(ROWS), by_group(1)],
            out_shape=[
                f32(count, ROWS * SUB, LANE),
                f32(count, ROWS * SUB, LANE),
                f32(count, SUB, LANE),
            ],
            scratch_shapes=[pltpu.VMEM((rows * SUB, LANE), jnp.float32)],
            compiler_params=params(),
            name=f"inner_{p}",
        )(mean, stored)
        inner.append(sums)
    next_edge, inner = lax.optimization_barrier((next_edge, inner))
    parts = []
    for p, order in enumerate(orders):
        totals, last, pixel_sum = inner[p]
        kept, sent = pl.pallas_call(
            functools.partial(border_kernel, p * count),
            in_specs=[SMEM, SMEM] + [VMEM] * 4,
            out_specs=[VMEM, VMEM],
            out_shape=[
                f32(count, ROWS // 2 * SUB, LANE),
                f32(count, (ROWS // 2 + 1) * SUB, LANE),
            ],
            scratch_shapes=[
                pltpu.SMEM((LAGS + EDGE_ROWS,), jnp.float32),
            ],
            compiler_params=params(),
            name=f"border_{p}",
        )(
            next_mean,
            sides[order[0]],
            next_edge,
            last,
            totals,
            pixel_sum,
        )
        parts.append(Part(order, uppers, kept, sent))
    steps = len(bits)
    for part in parts:
        part.send()
    for step in range(1, steps + 1):
        for part in parts:
            part.receive()
            if step < steps:
                part.send()
            else:
                part.send_back(steps - 2)
    for step in reversed(range(1, steps - 1)):
        for part in parts:
            part.receive_back(step)
            part.send_back(step - 1)
    out = None
    for p, part in enumerate(parts):
        first = p * count
        held = [] if out is None else [out]
        out = pl.pallas_call(
            functools.partial(finish_kernel, total_frames),
            grid=(count,),
            in_specs=[SMEM, VMEM, VMEM, VMEM]
            + [pl.BlockSpec(memory_space=pl.ANY)] * len(held),
            out_specs=pl.BlockSpec(
                (LEVELS, LAGS, GROUP), lambda g, first=first: (0, 0, g + first)
            ),
            out_shape=f32(LEVELS, LAGS, pixels),
            input_output_aliases={4: 0} if held else {},
            compiler_params=params(),
            name=f"finish_{p}",
        )(sides[part.order[0]], part.cur, part.got, part.sums, *held)
    return out


def solution(mesh):
    return jax.shard_map(
        on_device,
        mesh=mesh,
        in_specs=(P("tm", "pix"), P("pix")),
        out_specs=P(None, None, "pix"),
        check_vma=False,
    )
```

time: 122 us -> 107 us (0.88)
  local copies, waits for them, and re-layouts: 7.71 us -> 0.52 us
  waiting for transfers between devices: 57.2 us -> 51.9 us
  other arithmetic: 5.46 us -> 1.51 us
    ppermute x1, waiting for transfers between devices: 0.01 us -> 11.4 us  [on_device(): next_edge = lax.ppermute(edge, 'tm', back)]
    ppermute x1, waiting for transfers between devices: 9.91 us -> 0.06 us  [on_device(): next_mean = lax.ppermute(mean, 'tm', back)]
    unnamed x10 -> x0, local copies, waits for them, and re-layouts: 7.19 us -> none
    ppermute x16 -> x14, waiting for transfers between devices: 47.3 us -> 40.4 us  [swap(): return lax.ppermute(block, 'tm', [(i, i ^ mask) for i in range(size)])]
    concatenate x16 -> x10, other arithmetic: 2.05 us -> 0.2 us  [the longest x4 0.11 us: receive_back(): self.cur = jnp.concatenate([low, high], axis=1)]
    add x14 -> x16, other arithmetic: 2.14 us -> 0.35 us  [the longest x8 0.3 us: receive(): self.cur = self.kept + self.got[:, :rows]]
    pallas_call x4 -> x7, Pallas kernels: 24.4 us -> 25.5 us  [the longest x2 15.7 us: on_device(): pl.pallas_call(inner_kernel, grid=(count,), in_specs=[SMEM, pl.BlockSpec(...]
    ppermute x16 -> x14, starting transfers between devices: 20.8 us -> 21.6 us  [swap(): return lax.ppermute(block, 'tm', [(i, i ^ mask) for i in range(size)])]
  transfers between devices with their start and end apart: 18 -> 16, of which waited for: 14 -> 15; matrix products, arithmetic and copies ran while one was open for 2% -> 2% of each run, Pallas kernels for 12% -> 18%
where the time goes in v2:
time: 107 us
  waiting for transfers between devices  51.9 us (49%)
  Pallas kernels  25.5 us (24%)
  starting transfers between devices  24.2 us (23%)
  blocking collectives  2.59 us (2%)
  other arithmetic  1.51 us (1%)
    ppermute x14, waiting for transfers between devices, swap(): return lax.ppermute(block, 'tm', [(i, i ^ mask) for i in range(size)])  40.4 us
    ppermute x14, starting transfers between devices, swap(): return lax.ppermute(block, 'tm', [(i, i ^ mask) for i in range(size)])  21.6 us
    pallas_call x2, Pallas kernels, on_device(): pl.pallas_call(inner_kernel, grid=(count,), in_specs=[SMEM, pl.BlockSpec(...  15.7 us
    ppermute x1, waiting for transfers between devices, on_device(): next_edge = lax.ppermute(edge, 'tm', back)  11.4 us
    pallas_call x1, Pallas kernels, on_device(): pl.pallas_call(edge_kernel, in_specs=[pl.BlockSpec(memory_space=pl.ANY)]...  3.4 us
    pallas_call x2, Pallas kernels, on_device(): pl.pallas_call(functools.partial(finish_kernel, total_frames), grid=(coun...  3.21 us
    pallas_call x2, Pallas kernels, on_device(): pl.pallas_call(functools.partial(border_kernel, p * count), in_specs=[SME...  3.2 us
    psum x1, blocking collectives, on_device(): sums = lax.psum(sums[:, 0], 'pix')  2.59 us
  transfers between devices with their start and end apart: 16, of which 15 were waited for; matrix products, arithmetic and copies ran while one was open for 2% of the time, Pallas kernels for 18%

profile of v2, /device:TPU:0, one launch (start us, length us, event | category | flops | bytes accessed | tf_op | source)
XLA Modules:
  0.0 106.5 jit_solution(9018385412360744694)
XLA Ops:
  0.0 3.4 %edges.1 = (f32[136,1]{1,0:T(8,128)S(1)}, f32[8,320,128]{2,1,0:T(8,128)S(1)}) custom-call(f32[128,8192]{1,0:T(8,128)} %x_ref.3, f32[1,8192]{1,0:T(1,128)} %bitcast.4), custom_call_target="tpu_custom_call" | custom-call | tf_op jit(solution)/shard_map/edges/pallas_call | solution.py:290
  4.8 2.6 %psum.7 = f32[136]{0:T(256)S(1)} all-reduce(f32[136]{0:T(256)S(1)} %reduce), channel_id=1, replica_groups=mesh['tm'=16,'pix'=2] {'pix'}, use_global_device_ids=true, to_apply=%region_0.0 | all-reduce | flops 136 | bytes 1088 | tf_op jit(solution)/shard_map/psum | solution.py:307
  9.9 7.8 %inner_1.1 = (f32[4,512,128]{2,1,0:T(8,128)S(1)}, f32[4,512,128]{2,1,0:T(8,128)S(1)}, f32[4,8,128]{2,1,0:T(8,128)S(1)}) custom-call(f32[128]{0:T(128)S(1)} %slice_divide_fusion.mean_ref, f32[128,8192]{1,0:T(8,128)} %x_ref.3), custom_call_target="tpu_custom_call" | custom-call | tf_op jit(solution)/shard_map/inner_1/pallas_call | solution.py:317
  17.7 7.8 %inner_0.1 = (f32[4,512,128]{2,1,0:T(8,128)S(1)}, f32[4,512,128]{2,1,0:T(8,128)S(1)}, f32[4,8,128]{2,1,0:T(8,128)S(1)}) custom-call(f32[128]{0:T(128)S(1)} %slice_divide_fusion.mean_ref, f32[128,8192]{1,0:T(8,128)} %x_ref.3), custom_call_target="tpu_custom_call" | custom-call | tf_op jit(solution)/shard_map/inner_0/pallas_call | solution.py:317
  25.6 11.4 %collective-permute-done.1.edge_ref = f32[8,320,128]{2,1,0:T(8,128)S(1)} collective-permute-done((f32[8,320,128]{2,1,0:T(8,128)S(1)}, f32[8,320,128]{2,1,0:T(8,128)S(1)}, u32[]{:S(2)}, u32[]{:S(2)}) %collective-permute-start.1) | collective-permute-done | bytes 1310752 | tf_op jit(solution)/shard_map/ppermute | solution.py:306
  38.7 1.8 %collective-permute-start.2 = (f32[4,264,128]{2,1,0:T(8,128)S(1)}, f32[4,264,128]{2,1,0:T(8,128)S(1)}, u32[]{:S(2)}, u32[]{:S(2)}) collective-permute-start(f32[4,264,128]{2,1,0:T(8,128)S(1)} %get-tuple-element.47), channel_id=1, source_target_pairs={{0,4},{2,6},{4,0},{6,2},{8,12},{10,14},{12,8},{14,10},{16,20},{18,... | collective-permute-start | bytes 1622024 | tf_op jit(solution)/shard_map/ppermute | solution.py:236
  42.1 3.4 %collective-permute-start.9 = (f32[4,264,128]{2,1,0:T(8,128)S(1)}, f32[4,264,128]{2,1,0:T(8,128)S(1)}, u32[]{:S(2)}, u32[]{:S(2)}) collective-permute-start(f32[4,264,128]{2,1,0:T(8,128)S(1)} %get-tuple-element.54), channel_id=1, source_target_pairs={{0,2},{2,0},{4,6},{6,4},{8,10},{10,8},{12,14},{14,12},{16,18},{18,... | collective-permute-start | bytes 1622024 | tf_op jit(solution)/shard_map/ppermute | solution.py:236
  45.5 6.7 %collective-permute-done.2 = f32[4,264,128]{2,1,0:T(8,128)S(1)} collective-permute-done((f32[4,264,128]{2,1,0:T(8,128)S(1)}, f32[4,264,128]{2,1,0:T(8,128)S(1)}, u32[]{:S(2)}, u32[]{:S(2)}) %collective-permute-start.2) | collective-permute-done | bytes 540704 | tf_op jit(solution)/shard_map/ppermute | solution.py:236
  52.3 3.1 %collective-permute-start.3 = (f32[4,136,128]{2,1,0:T(8,128)S(1)}, f32[4,136,128]{2,1,0:T(8,128)S(1)}, u32[]{:S(2)}, u32[]{:S(2)}) collective-permute-start(f32[4,136,128]{2,1,0:T(8,128)S(1)} %pad_maximum_fusion.2), channel_id=1, source_target_pairs={{0,2},{2,0},{4,6},{6,4},{8,10},{10,8},{12,14},{14,12},{16,18},{18,... | collective-permute-start | bytes 835592 | tf_op jit(solution)/shard_map/ppermute | solution.py:236
  55.4 3.2 %collective-permute-done.9 = f32[4,264,128]{2,1,0:T(8,128)S(1)} collective-permute-done((f32[4,264,128]{2,1,0:T(8,128)S(1)}, f32[4,264,128]{2,1,0:T(8,128)S(1)}, u32[]{:S(2)}, u32[]{:S(2)}) %collective-permute-start.9) | collective-permute-done | bytes 540704 | tf_op jit(solution)/shard_map/ppermute | solution.py:236
  58.7 1.6 %collective-permute-start.10 = (f32[4,136,128]{2,1,0:T(8,128)S(1)}, f32[4,136,128]{2,1,0:T(8,128)S(1)}, u32[]{:S(2)}, u32[]{:S(2)}) collective-permute-start(f32[4,136,128]{2,1,0:T(8,128)S(1)} %pad_maximum_fusion.3), channel_id=1, source_target_pairs={{0,8},{2,10},{4,12},{6,14},{8,0},{10,2},{12,4},{14,6},{16,24},{18,... | collective-permute-start | bytes 835592 | tf_op jit(solution)/shard_map/ppermute | solution.py:236
  60.3 2.2 %collective-permute-done.3 = f32[4,136,128]{2,1,0:T(8,128)S(1)} collective-permute-done((f32[4,136,128]{2,1,0:T(8,128)S(1)}, f32[4,136,128]{2,1,0:T(8,128)S(1)}, u32[]{:S(2)}, u32[]{:S(2)}) %collective-permute-start.3) | collective-permute-done | bytes 278560 | tf_op jit(solution)/shard_map/ppermute | solution.py:236
  62.6 4.3 %collective-permute-done.10 = f32[4,136,128]{2,1,0:T(8,128)S(1)} collective-permute-done((f32[4,136,128]{2,1,0:T(8,128)S(1)}, f32[4,136,128]{2,1,0:T(8,128)S(1)}, u32[]{:S(2)}, u32[]{:S(2)}) %collective-permute-start.10) | collective-permute-done | bytes 278560 | tf_op jit(solution)/shard_map/ppermute | solution.py:236
  67.1 1.6 %collective-permute-start.4 = (f32[4,72,128]{2,1,0:T(8,128)S(1)}, f32[4,72,128]{2,1,0:T(8,128)S(1)}, u32[]{:S(2)}, u32[]{:S(2)}) collective-permute-start(f32[4,72,128]{2,1,0:T(8,128)S(1)} %pad_maximum_fusion.6), channel_id=1, source_target_pairs={{0,8},{2,10},{4,12},{6,14},{8,0},{10,2},{12,4},{14,6},{16,24},{18,... | collective-permute-start | bytes 442376 | tf_op jit(solution)/shard_map/ppermute | solution.py:236
  68.7 3.5 %collective-permute-done.11 = f32[4,72,128]{2,1,0:T(8,128)S(1)} collective-permute-done((f32[4,72,128]{2,1,0:T(8,128)S(1)}, f32[4,72,128]{2,1,0:T(8,128)S(1)}, u32[]{:S(2)}, u32[]{:S(2)}) %collective-permute-start.11) | collective-permute-done | bytes 147488 | tf_op jit(solution)/shard_map/ppermute | solution.py:236
  72.2 2.7 %collective-permute-start.12 = (f32[4,72,128]{2,1,0:T(8,128)S(1)}, f32[4,72,128]{2,1,0:T(8,128)S(1)}, u32[]{:S(2)}, u32[]{:S(2)}) collective-permute-start(f32[4,72,128]{2,1,0:T(8,128)S(1)} %pad_maximum_fusion.9), channel_id=1, source_target_pairs={{0,16},{2,18},{4,20},{6,22},{8,24},{10,26},{12,28},{14,30},{16,0},... | collective-permute-start | bytes 442376 | tf_op jit(solution)/shard_map/ppermute | solution.py:236
  75.4 4.2 %collective-permute-done.12 = f32[4,72,128]{2,1,0:T(8,128)S(1)} collective-permute-done((f32[4,72,128]{2,1,0:T(8,128)S(1)}, f32[4,72,128]{2,1,0:T(8,128)S(1)}, u32[]{:S(2)}, u32[]{:S(2)}) %collective-permute-start.12) | collective-permute-done | bytes 147488 | tf_op jit(solution)/shard_map/ppermute | solution.py:236
  80.0 2.8 %collective-permute-done.5 = f32[4,72,128]{2,1,0:T(8,128)S(1)} collective-permute-done((f32[4,72,128]{2,1,0:T(8,128)S(1)}, f32[4,72,128]{2,1,0:T(8,128)S(1)}, u32[]{:S(2)}, u32[]{:S(2)}) %collective-permute-start.5) | collective-permute-done | bytes 147488 | tf_op jit(solution)/shard_map/ppermute | solution.py:236
  85.9 1.9 %collective-permute-done.6 = f32[4,64,128]{2,1,0:T(8,128)S(1)} collective-permute-done((f32[4,64,128]{2,1,0:T(8,128)S(1)}, f32[4,64,128]{2,1,0:T(8,128)S(1)}, u32[]{:S(2)}, u32[]{:S(2)}) %collective-permute-start.6) | collective-permute-done | bytes 131104 | tf_op jit(solution)/shard_map/ppermute | solution.py:236
  87.9 1.7 %collective-permute-start.7 = (f32[4,128,128]{2,1,0:T(8,128)S(1)}, f32[4,128,128]{2,1,0:T(8,128)S(1)}, u32[]{:S(2)}, u32[]{:S(2)}) collective-permute-start(f32[4,128,128]{2,1,0:T(8,128)S(1)} %pad_maximum_fusion.4), channel_id=1, source_target_pairs={{0,2},{2,0},{4,6},{6,4},{8,10},{10,8},{12,14},{14,12},{16,18},{18,... | collective-permute-start | bytes 786440 | tf_op jit(solution)/shard_map/ppermute | solution.py:236
  92.8 2.7 %collective-permute-done.7 = f32[4,128,128]{2,1,0:T(8,128)S(1)} collective-permute-done((f32[4,128,128]{2,1,0:T(8,128)S(1)}, f32[4,128,128]{2,1,0:T(8,128)S(1)}, u32[]{:S(2)}, u32[]{:S(2)}) %collective-permute-start.7) | collective-permute-done | bytes 262176 | tf_op jit(solution)/shard_map/ppermute | solution.py:236
  96.4 4.8 %collective-permute-done.15.got_ref = f32[4,256,128]{2,1,0:T(8,128)S(1)} collective-permute-done((f32[4,256,128]{2,1,0:T(8,128)S(1)}, f32[4,256,128]{2,1,0:T(8,128)S(1)}, u32[]{:S(2)}, u32[]{:S(2)}) %collective-permute-start.15) | collective-permute-done | bytes 524320 | tf_op jit(solution)/shard_map/ppermute | solution.py:236
  101.2 1.6 %finish_0.1.refs_0_ = f32[4,16,8192]{2,1,0:T(8,128)} custom-call(s32[1]{0:T(128)} %bitcast.side_ref, f32[4,256,128]{2,1,0:T(8,128)S(1)} %pad_maximum_fusion.1.mine_ref, f32[4,256,128]{2,1,0:T(8,128)S(1)} %collective-permute-done.15.got_ref, f32[4,8,128]{2,1,0:T(8,128)S(1)} %slice_add_fusion.8.sum_ref), custom_call_target="tpu_custom_call" | custom-call | tf_op jit(solution)/shard_map/finish_0/pallas_call | solution.py:379
  102.8 2.1 %collective-permute-done.8.got_ref = f32[4,256,128]{2,1,0:T(8,128)S(1)} collective-permute-done((f32[4,256,128]{2,1,0:T(8,128)S(1)}, f32[4,256,128]{2,1,0:T(8,128)S(1)}, u32[]{:S(2)}, u32[]{:S(2)}) %collective-permute-start.8) | collective-permute-done | bytes 524320 | tf_op jit(solution)/shard_map/ppermute | solution.py:236
  (53 shorter events, 17.4 us)
Async XLA Ops:
  3.4 33.6 %collective-permute-start.1 = (f32[8,320,128]{2,1,0:T(8,128)S(1)}, f32[8,320,128]{2,1,0:T(8,128)S(1)}, u32[]{:S(2)}, u32[]{:S(2)}) collective-permute-start(f32[8,320,128]{2,1,0:T(8,128)S(1)} %get-tuple-element.35), channel_id=1, source_target_pairs={{2,0},{4,2},{6,4},{8,6},{10,8},{12,10},{14,12},{16,14},{18,16},{20... | collective-permute-start | bytes 3932168 | tf_op jit(solution)/shard_map/ppermute | solution.py:306
  8.6 28.5 %collective-permute-start = (f32[128]{0:T(128)S(1)}, f32[128]{0:T(128)S(1)}, u32[]{:S(2)}, u32[]{:S(2)}) collective-permute-start(f32[128]{0:T(128)S(1)} %slice_divide_fusion.mean_ref), channel_id=1, source_target_pairs={{2,0},{4,2},{6,4},{8,6},{10,8},{12,10},{14,12},{16,14},{18,16},{20... | collective-permute-start | bytes 1544 | tf_op jit(solution)/shard_map/ppermute | solution.py:309
  38.7 13.5 %collective-permute-start.2 = (f32[4,264,128]{2,1,0:T(8,128)S(1)}, f32[4,264,128]{2,1,0:T(8,128)S(1)}, u32[]{:S(2)}, u32[]{:S(2)}) collective-permute-start(f32[4,264,128]{2,1,0:T(8,128)S(1)} %get-tuple-element.47), channel_id=1, source_target_pairs={{0,4},{2,6},{4,0},{6,2},{8,12},{10,14},{12,8},{14,10},{16,20},{18,... | collective-permute-start | bytes 1622024 | tf_op jit(solution)/shard_map/ppermute | solution.py:236
  42.1 16.4 %collective-permute-start.9 = (f32[4,264,128]{2,1,0:T(8,128)S(1)}, f32[4,264,128]{2,1,0:T(8,128)S(1)}, u32[]{:S(2)}, u32[]{:S(2)}) collective-permute-start(f32[4,264,128]{2,1,0:T(8,128)S(1)} %get-tuple-element.54), channel_id=1, source_target_pairs={{0,2},{2,0},{4,6},{6,4},{8,10},{10,8},{12,14},{14,12},{16,18},{18,... | collective-permute-start | bytes 1622024 | tf_op jit(solution)/shard_map/ppermute | solution.py:236
  52.3 10.2 %collective-permute-start.3 = (f32[4,136,128]{2,1,0:T(8,128)S(1)}, f32[4,136,128]{2,1,0:T(8,128)S(1)}, u32[]{:S(2)}, u32[]{:S(2)}) collective-permute-start(f32[4,136,128]{2,1,0:T(8,128)S(1)} %pad_maximum_fusion.2), channel_id=1, source_target_pairs={{0,2},{2,0},{4,6},{6,4},{8,10},{10,8},{12,14},{14,12},{16,18},{18,... | collective-permute-start | bytes 835592 | tf_op jit(solution)/shard_map/ppermute | solution.py:236
  58.7 8.2 %collective-permute-start.10 = (f32[4,136,128]{2,1,0:T(8,128)S(1)}, f32[4,136,128]{2,1,0:T(8,128)S(1)}, u32[]{:S(2)}, u32[]{:S(2)}) collective-permute-start(f32[4,136,128]{2,1,0:T(8,128)S(1)} %pad_maximum_fusion.3), channel_id=1, source_target_pairs={{0,8},{2,10},{4,12},{6,14},{8,0},{10,2},{12,4},{14,6},{16,24},{18,... | collective-permute-start | bytes 835592 | tf_op jit(solution)/shard_map/ppermute | solution.py:236
  67.0 5.2 %collective-permute-start.11 = (f32[4,72,128]{2,1,0:T(8,128)S(1)}, f32[4,72,128]{2,1,0:T(8,128)S(1)}, u32[]{:S(2)}, u32[]{:S(2)}) collective-permute-start(f32[4,72,128]{2,1,0:T(8,128)S(1)} %pad_maximum_fusion.8), channel_id=1, source_target_pairs={{0,4},{2,6},{4,0},{6,2},{8,12},{10,14},{12,8},{14,10},{16,20},{18,... | collective-permute-start | bytes 442376 | tf_op jit(solution)/shard_map/ppermute | solution.py:236
  67.1 7.8 %collective-permute-start.4 = (f32[4,72,128]{2,1,0:T(8,128)S(1)}, f32[4,72,128]{2,1,0:T(8,128)S(1)}, u32[]{:S(2)}, u32[]{:S(2)}) collective-permute-start(f32[4,72,128]{2,1,0:T(8,128)S(1)} %pad_maximum_fusion.6), channel_id=1, source_target_pairs={{0,8},{2,10},{4,12},{6,14},{8,0},{10,2},{12,4},{14,6},{16,24},{18,... | collective-permute-start | bytes 442376 | tf_op jit(solution)/shard_map/ppermute | solution.py:236
  72.2 7.4 %collective-permute-start.12 = (f32[4,72,128]{2,1,0:T(8,128)S(1)}, f32[4,72,128]{2,1,0:T(8,128)S(1)}, u32[]{:S(2)}, u32[]{:S(2)}) collective-permute-start(f32[4,72,128]{2,1,0:T(8,128)S(1)} %pad_maximum_fusion.9), channel_id=1, source_target_pairs={{0,16},{2,18},{4,20},{6,22},{8,24},{10,26},{12,28},{14,30},{16,0},... | collective-permute-start | bytes 442376 | tf_op jit(solution)/shard_map/ppermute | solution.py:236
  74.9 7.8 %collective-permute-start.5 = (f32[4,72,128]{2,1,0:T(8,128)S(1)}, f32[4,72,128]{2,1,0:T(8,128)S(1)}, u32[]{:S(2)}, u32[]{:S(2)}) collective-permute-start(f32[4,72,128]{2,1,0:T(8,128)S(1)} %pad_maximum_fusion.7), channel_id=1, source_target_pairs={{0,16},{2,18},{4,20},{6,22},{8,24},{10,26},{12,28},{14,30},{16,0},... | collective-permute-start | bytes 442376 | tf_op jit(solution)/shard_map/ppermute | solution.py:236
  79.6 5.0 %collective-permute-start.13 = (f32[4,64,128]{2,1,0:T(8,128)S(1)}, f32[4,64,128]{2,1,0:T(8,128)S(1)}, u32[]{:S(2)}, u32[]{:S(2)}) collective-permute-start(f32[4,64,128]{2,1,0:T(8,128)S(1)} %slice_add_fusion.4), channel_id=1, source_target_pairs={{0,4},{2,6},{4,0},{6,2},{8,12},{10,14},{12,8},{14,10},{16,20},{18,... | collective-permute-start | bytes 393224 | tf_op jit(solution)/shard_map/ppermute | solution.py:236
  82.8 5.0 %collective-permute-start.6 = (f32[4,64,128]{2,1,0:T(8,128)S(1)}, f32[4,64,128]{2,1,0:T(8,128)S(1)}, u32[]{:S(2)}, u32[]{:S(2)}) collective-permute-start(f32[4,64,128]{2,1,0:T(8,128)S(1)} %slice_add_fusion.6), channel_id=1, source_target_pairs={{0,8},{2,10},{4,12},{6,14},{8,0},{10,2},{12,4},{14,6},{16,24},{18,... | collective-permute-start | bytes 393224 | tf_op jit(solution)/shard_map/ppermute | solution.py:236
  84.7 6.4 %collective-permute-start.14 = (f32[4,128,128]{2,1,0:T(8,128)S(1)}, f32[4,128,128]{2,1,0:T(8,128)S(1)}, u32[]{:S(2)}, u32[]{:S(2)}) collective-permute-start(f32[4,128,128]{2,1,0:T(8,128)S(1)} %pad_maximum_fusion.5), channel_id=1, source_target_pairs={{0,8},{2,10},{4,12},{6,14},{8,0},{10,2},{12,4},{14,6},{16,24},{18,... | collective-permute-start | bytes 786440 | tf_op jit(solution)/shard_map/ppermute | solution.py:236
  87.9 7.7 %collective-permute-start.7 = (f32[4,128,128]{2,1,0:T(8,128)S(1)}, f32[4,128,128]{2,1,0:T(8,128)S(1)}, u32[]{:S(2)}, u32[]{:S(2)}) collective-permute-start(f32[4,128,128]{2,1,0:T(8,128)S(1)} %pad_maximum_fusion.4), channel_id=1, source_target_pairs={{0,2},{2,0},{4,6},{6,4},{8,10},{10,8},{12,14},{14,12},{16,18},{18,... | collective-permute-start | bytes 786440 | tf_op jit(solution)/shard_map/ppermute | solution.py:236
  91.2 10.0 %collective-permute-start.15 = (f32[4,256,128]{2,1,0:T(8,128)S(1)}, f32[4,256,128]{2,1,0:T(8,128)S(1)}, u32[]{:S(2)}, u32[]{:S(2)}) collective-permute-start(f32[4,256,128]{2,1,0:T(8,128)S(1)} %pad_maximum_fusion.1.mine_ref), channel_id=1, source_target_pairs={{0,2},{2,0},{4,6},{6,4},{8,10},{10,8},{12,14},{14,12},{16,18},{18,... | collective-permute-start | bytes 1572872 | tf_op jit(solution)/shard_map/ppermute | solution.py:236
  95.7 9.2 %collective-permute-start.8 = (f32[4,256,128]{2,1,0:T(8,128)S(1)}, f32[4,256,128]{2,1,0:T(8,128)S(1)}, u32[]{:S(2)}, u32[]{:S(2)}) collective-permute-start(f32[4,256,128]{2,1,0:T(8,128)S(1)} %pad_maximum_fusion.mine_ref), channel_id=1, source_target_pairs={{0,4},{2,6},{4,0},{6,2},{8,12},{10,14},{12,8},{14,10},{16,20},{18,... | collective-permute-start | bytes 1572872 | tf_op jit(solution)/shard_map/ppermute | solution.py:236

commit v3 on v2

v3 whole, which is shorter than its diff:
```python
import functools

import jax
import jax.numpy as jnp
from jax import lax
from jax.experimental import pallas as pl
from jax.experimental.pallas import tpu as pltpu
from jax.sharding import PartitionSpec as P

LEVELS = 4
LAGS = 16
SUB, LANE = 8, 128
GROUP = SUB * LANE
VMEM_LIMIT = 16 * 1024 * 1024


def tile(ref, row):
    return ref[row * SUB : (row + 1) * SUB, :]


def edge_kernel(spans, x_hbm, w_hbm, sums_ref, *refs):
    edge_refs, refs = refs[: len(spans)], refs[len(spans) :]
    x_ref, w_ref, tall_ref, acc_ref, sem, w_sem = refs
    groups, rows, _ = x_ref.shape
    half = LAGS // 2

    def fetch(g):
        at = pl.ds(pl.multiple_of(g * GROUP, GROUP), GROUP)
        return pltpu.make_async_copy(x_hbm.at[:, at], x_ref.at[g], sem.at[g])

    weights = pltpu.make_async_copy(w_hbm, w_ref, w_sem)
    weights.start()
    for g in range(groups):
        fetch(g).start()
    acc_ref[...] = jnp.zeros_like(acc_ref)
    weights.wait()

    def one_group(first, edge_ref, slot, carry):
        g = slot + first
        fetch(g).wait()
        for c in range(SUB):
            at = pl.ds(pl.multiple_of(g * GROUP + c * LANE, LANE), LANE)
            weight = jnp.broadcast_to(w_ref[:, at], (SUB, LANE))
            acc_ref[rows : rows + SUB, :] += weight
            for i in range(rows // SUB):
                part = slice(i * SUB, (i + 1) * SUB)
                value = x_ref[g, part, c * LANE : (c + 1) * LANE]
                acc_ref[part, :] += value * weight
                tall_ref[pl.ds(i * SUB * SUB + c, SUB, stride=SUB), :] = value
        edge_ref[slot, : LAGS * SUB, :] = tall_ref[: LAGS * SUB, :]
        for level in range(1, LEVELS):
            span = 1 << level
            for j in range(half):
                group = [tile(tall_ref, (half + j) * span + s) for s in range(span)]
                while len(group) > 1:
                    group = [(a + b) * 0.5 for a, b in zip(group[::2], group[1::2])]
                row = LAGS + (level - 1) * half + j
                edge_ref[slot, row * SUB : (row + 1) * SUB, :] = group[0]
        return carry

    for (first, count), edge_ref in zip(spans, edge_refs):
        lax.fori_loop(0, count, functools.partial(one_group, first, edge_ref), 0)
    sums_ref[...] = jnp.sum(acc_ref[...], axis=1, keepdims=True)


def lag_step(read, near, far, totals):
    window = [read(i) for i in range(LAGS)]
    out = list(totals)
    for i in range(near):
        for k in range(1, LAGS + 1):
            if i + k < far:
                if i + k == len(window):
                    window.append(read(i + k))
                out[k - 1] = out[k - 1] + window[i] * window[i + k]
    return out


def inner_kernel(mean_ref, x_ref, totals_ref, last_ref, sum_ref, series_ref, wide_ref):
    rows = x_ref.shape[0]

    @pl.when(pl.program_id(0) == 0)
    def _():
        for t in range(rows):
            wide_ref[t : t + 1, :] = jnp.full((1, LANE), mean_ref[t], jnp.float32)

    for c in range(SUB):
        total = None
        for i in range(rows // SUB):
            part = slice(i * SUB, (i + 1) * SUB)
            value = x_ref[part, c * LANE : (c + 1) * LANE] + wide_ref[part, :]
            series_ref[pl.ds(i * SUB * SUB + c, SUB, stride=SUB), :] = value
            total = value if total is None else total + value
        sum_ref[0, c : c + 1, :] = jnp.sum(total, axis=0, keepdims=True)
    zero = jnp.zeros((SUB, LANE), jnp.float32)
    for level in range(LEVELS):
        count = rows >> level
        chunks = count // LAGS

        def reader(chunk):
            start = chunk * (LAGS * SUB)

            def read(i):
                return series_ref[pl.ds(pl.multiple_of(start + i * SUB, SUB), SUB), :]

            return read

        def body(chunk, totals):
            return tuple(lag_step(reader(chunk), LAGS, 2 * LAGS, totals))

        totals = tuple([zero] * LAGS)
        if chunks > 1:
            totals = lax.fori_loop(0, chunks - 1, body, totals)
        read = reader(chunks - 1)
        totals = lag_step(read, LAGS, LAGS, totals)
        old = [read(i) for i in range(LAGS)]
        for i in range(LAGS):
            row = level * LAGS + i
            totals_ref[0, row * SUB : (row + 1) * SUB, :] = totals[i]
            last_ref[0, row * SUB : (row + 1) * SUB, :] = old[i]
        if level < LEVELS - 1:
            for i in range(count // 2):
                pair = tile(series_ref, 2 * i) + tile(series_ref, 2 * i + 1)
                series_ref[i * SUB : (i + 1) * SUB, :] = pair * 0.5


def border_kernel(offset, mean_ref, side_ref, edge_ref, last_ref, totals_ref,
                  sum_ref, kept_ref, sent_ref, level_mean_ref):
    half = LAGS // 2
    split = LEVELS // 2
    side = side_ref[0]
    groups = kept_ref.shape[0]
    for j in range(LAGS):
        level_mean_ref[j] = mean_ref[j]
    for level in range(1, LEVELS):
        span = 1 << level
        for j in range(half):
            group = [mean_ref[(half + j) * span + s] for s in range(span)]
            while len(group) > 1:
                group = [(a + b) * 0.5 for a, b in zip(group[::2], group[1::2])]
            level_mean_ref[LAGS + (level - 1) * half + j] = group[0]

    def one_group(slot, carry):
        sent_ref[slot, ROWS // 2 * SUB :, :] = sum_ref[slot]
        new = [
            edge_ref[slot + offset, j * SUB : (j + 1) * SUB, :] + level_mean_ref[j]
            for j in range(LAGS)
        ]
        for level in range(LEVELS):
            if level > 0:
                fresh = [(a + b) * 0.5 for a, b in zip(new[::2], new[1::2])]
                for j in range(half):
                    row = LAGS + (level - 1) * half + j
                    fresh.append(
                        edge_ref[slot + offset, row * SUB : (row + 1) * SUB, :]
                        + level_mean_ref[row]
                    )
                new = fresh
            base = level * LAGS
            old = [
                last_ref[slot, (base + i) * SUB : (base + i + 1) * SUB, :]
                for i in range(LAGS)
            ]
            totals = []
            for k in range(1, LAGS + 1):
                row = base + k - 1
                total = totals_ref[slot, row * SUB : (row + 1) * SUB, :]
                for i in range(LAGS - k, LAGS):
                    total = total + old[i] * new[i + k - LAGS]
                totals.append(total)
            upper, base = level // split, (level % split) * LAGS

            def put(ref, totals=totals, base=base):
                for i, total in enumerate(totals):
                    ref[slot, (base + i) * SUB : (base + i + 1) * SUB, :] = total

            pl.when(side == upper)(functools.partial(put, kept_ref))
            pl.when(side != upper)(functools.partial(put, sent_ref))
        return carry

    lax.fori_loop(0, groups, one_group, 0)


def finish_kernel(total_frames, side_ref, mine_ref, got_ref, sum_ref, *refs):
    out_ref = refs[-1]
    split = LEVELS // 2
    g = pl.program_id(0)
    side = side_ref[0]
    for c in range(SUB):
        mean = sum_ref[g, c : c + 1, :] / total_frames
        square = jnp.broadcast_to(mean * mean, (SUB, LANE))
        for level in range(LEVELS):
            own = side == level // split
            for i in range(LAGS // SUB):
                lag = lax.broadcasted_iota(jnp.int32, (SUB, LANE), 0) + (i * SUB + 1)
                count = ((total_frames >> level) - lag).astype(jnp.float32)
                row = (level % split) * LAGS + i * SUB
                at = pl.ds(row * SUB + c, SUB, stride=SUB)
                total = jnp.where(own, mine_ref[g, at, :], got_ref[g, at, :])
                out_ref[level, i * SUB : (i + 1) * SUB, c * LANE : (c + 1) * LANE] = (
                    total / (count * square)
                )


ROWS = LEVELS * LAGS
EDGE_ROWS = LAGS + (LEVELS - 1) * (LAGS // 2)
SMEM = pl.BlockSpec(memory_space=pltpu.SMEM)
VMEM = pl.BlockSpec(memory_space=pltpu.VMEM)


def params():
    return pltpu.CompilerParams(vmem_limit_bytes=VMEM_LIMIT)


def in_hbm(value):
    return pltpu.with_memory_space_constraint(value, pltpu.HBM)


def f32(*shape):
    return jax.ShapeDtypeStruct(shape, jnp.float32)


def by_group(rows):
    return pl.BlockSpec((1, rows * SUB, LANE), lambda g: (g, 0, 0))


def swap(block, mask):
    size = lax.axis_size("tm")
    return lax.ppermute(block, "tm", [(i, i ^ mask) for i in range(size)])


def after(value, token):
    return lax.optimization_barrier((value, token))[0]


class Part:
    def __init__(self, order, uppers, kept, sent):
        self.order = order
        self.uppers = uppers
        self.kept, self.sent = kept, sent
        self.sums = sent[:, kept.shape[1] :]
        steps = len(order)
        self.route = list(range(steps)) + list(reversed(range(steps - 1)))
        self.at = 0
        self.got = swap(sent, order[0])

    def finished(self):
        return self.at == len(self.route) - 1

    def advance(self, token):
        steps = len(self.order)
        got = after(self.got, token)
        if self.at < steps:
            rows = self.kept.shape[1]
            self.cur = self.kept + got[:, :rows]
            self.sums = self.sums + got[:, rows:]
        else:
            upper = self.uppers[self.order[self.route[self.at]]]
            low = jnp.where(upper, got, self.cur)
            high = jnp.where(upper, self.cur, got)
            self.cur = jnp.concatenate([low, high], axis=1)
        self.at += 1
        mask = self.order[self.route[self.at]]
        if self.at < steps:
            if self.at == steps - 1:
                self.kept = self.sent = self.cur
            else:
                half = self.cur.shape[1] // 2
                low, high = self.cur[:, :half], self.cur[:, half:]
                self.kept = jnp.where(self.uppers[mask], high, low)
                self.sent = jnp.where(self.uppers[mask], low, high)
            self.sent = jnp.concatenate([self.sent, self.sums], axis=1)
        else:
            self.sent = self.cur
        self.got = swap(self.sent, mask)
        return self.sent


def plan(groups, bits):
    x, y, z = (bits + bits[-1:] * 2)[:3]
    tail = bits[3:]
    cuts = [groups * i // 8 for i in CUTS]
    orders = [[z, y, x] + tail, [y, x, z] + tail, [x, z, y] + tail]
    orders = [o[: len(bits)] for o in orders]
    return [(a, b - a, o) for a, b, o in zip(cuts, cuts[1:], orders)]


CUTS = (0, 3, 6, 8)


def on_device(frames, ref_weight):
    rows, pixels = frames.shape
    groups = pixels // GROUP
    size = lax.axis_size("tm")
    total_frames = rows * size
    bits = [1 << b for b in range(size.bit_length() - 1)]
    parts = plan(groups, bits)
    me = lax.axis_index("tm")
    uppers = {bit: (me & bit) != 0 for bit in bits}
    sides = {o[0]: uppers[o[0]].astype(jnp.int32).reshape(1) for _, _, o in parts}
    ref_weight, uppers, sides = lax.optimization_barrier((ref_weight, uppers, sides))
    stored = in_hbm(frames)
    head = parts[0][1]
    spans = [(0, head), (head, groups - head)]
    back = [(i, i - 1) for i in range(1, size)]
    sums, *edges = pl.pallas_call(
        functools.partial(edge_kernel, spans),
        in_specs=[pl.BlockSpec(memory_space=pl.ANY)] * 2,
        out_specs=[VMEM] * (1 + len(spans)),
        out_shape=[f32(rows + SUB, 1)]
        + [f32(count, EDGE_ROWS * SUB, LANE) for _, count in spans],
        scratch_shapes=[
            pltpu.VMEM((groups, rows, GROUP), jnp.float32),
            pltpu.VMEM((1, pixels), jnp.float32),
            pltpu.VMEM((rows * SUB, LANE), jnp.float32),
            pltpu.VMEM((rows + SUB, LANE), jnp.float32),
            pltpu.SemaphoreType.DMA((groups,)),
            pltpu.SemaphoreType.DMA,
        ],
        compiler_params=params(),
        name="edges",
    )(stored, in_hbm(ref_weight.reshape(1, pixels)))
    next_edges = [lax.ppermute(edges[0], "tm", back)]
    sums = lax.psum(sums[:, 0], "pix")
    mean = sums[:rows] / sums[rows]
    next_mean = lax.ppermute(mean, "tm", back)
    for edge in edges[1:]:
        next_edges.append(lax.ppermute(after(edge, mean), "tm", back))

    def inner(p, token):
        first, count, _ = parts[p]
        return pl.pallas_call(
            inner_kernel,
            grid=(count,),
            in_specs=[
                SMEM,
                pl.BlockSpec((rows, GROUP), lambda g: (0, g + first)),
            ],
            out_specs=[by_group(ROWS), by_group(ROWS), by_group(1)],
            out_shape=[
                f32(count, ROWS * SUB, LANE),
                f32(count, ROWS * SUB, LANE),
                f32(count, SUB, LANE),
            ],
            scratch_shapes=[
                pltpu.VMEM((rows * SUB, LANE), jnp.float32),
                pltpu.VMEM((rows, LANE), jnp.float32),
            ],
            compiler_params=params(),
            name=f"inner_{p}",
        )(after(mean, token), stored)

    def border(p, sums, token):
        first, count, order = parts[p]
        totals, last, pixel_sum = sums
        kept, sent = pl.pallas_call(
            functools.partial(border_kernel, first - spans[p > 0][0]),
            in_specs=[SMEM, SMEM] + [VMEM] * 4,
            out_specs=[VMEM, VMEM],
            out_shape=[
                f32(count, ROWS // 2 * SUB, LANE),
                f32(count, (ROWS // 2 + 1) * SUB, LANE),
            ],
            scratch_shapes=[pltpu.SMEM((EDGE_ROWS,), jnp.float32)],
            compiler_params=params(),
            name=f"border_{p}",
        )(next_mean, sides[order[0]], after(next_edges[p > 0], token), last, totals, pixel_sum)
        return Part(order, uppers, kept, sent)

    sums = []
    token = mean
    local = []
    for p in range(len(parts)):
        local.append(inner(p, token))
        token = local[p][2]
    for p in range(len(parts)):
        sums.append(border(p, local[p], token))
        token = sums[p].sent
    while not all(part.finished() for part in sums):
        for part in sums:
            if not part.finished():
                token = part.advance(token)
    out = None
    for p, (first, count, order) in enumerate(parts):
        held = [] if out is None else [out]
        part = sums[p]
        out = pl.pallas_call(
            functools.partial(finish_kernel, total_frames),
            grid=(count,),
            in_specs=[SMEM, VMEM, VMEM, VMEM]
            + [pl.BlockSpec(memory_space=pl.ANY)] * len(held),
            out_specs=pl.BlockSpec(
                (LEVELS, LAGS, GROUP), lambda g, first=first: (0, 0, g + first)
            ),
            out_shape=f32(LEVELS, LAGS, pixels),
            input_output_aliases={4: 0} if held else {},
            compiler_params=params(),
            name=f"finish_{p}",
        )(sides[order[0]], part.cur, part.got, part.sums, *held)
    return out


def solution(mesh):
    return jax.shard_map(
        on_device,
        mesh=mesh,
        in_specs=(P("tm", "pix"), P("pix")),
        out_specs=P(None, None, "pix"),
        check_vma=False,
    )
```

time: 107 us -> 98.9 us (0.924)
  waiting for transfers between devices: 51.9 us -> 28.4 us
  starting transfers between devices: 24.2 us -> 41 us
  Pallas kernels: 25.5 us -> 24.1 us
    ppermute x14 -> x21, waiting for transfers between devices: 40.4 us -> 15.5 us  [swap(): return lax.ppermute(block, 'tm', [(i, i ^ mask) for i in range(size)])]
    ppermute x14 -> x21, starting transfers between devices: 21.6 us -> 37.2 us  [swap(): return lax.ppermute(block, 'tm', [(i, i ^ mask) for i in range(size)])]
    ppermute x1, waiting for transfers between devices: 0.06 us -> 12.9 us  [on_device(): next_mean = lax.ppermute(mean, 'tm', back)]
    ppermute x1 -> x2, waiting for transfers between devices: 11.4 us -> 0.01 us  [the longest x1 0.01 us: on_device(): next_edges = [lax.ppermute(edges[0], 'tm', back)]]
    pallas_call x5 -> x7, Pallas kernels: 22.3 us -> 20.2 us  [the longest x3 13 us: inner(): pl.pallas_call(inner_kernel, grid=(count,), in_specs=[SMEM, pl.BlockSpec(...]
    ppermute x1 -> x2, starting transfers between devices: 1.29 us -> 2.58 us  [the longest x1 1.29 us: on_device(): next_edges = [lax.ppermute(edges[0], 'tm', back)]]
    pallas_call x2 -> x3, Pallas kernels: 3.21 us -> 3.89 us  [on_device(): pl.pallas_call(functools.partial(finish_kernel, total_frames), grid=(coun...]
  transfers between devices with their start and end apart: 16 -> 24, of which waited for: 15 -> 13; matrix products, arithmetic and copies ran while one was open for 2% -> 2% of each run, Pallas kernels for 18% -> 20%
where the time goes in v3:
time: 98.9 us; the launch traced here: 98.6 us
  starting transfers between devices  41 us (41%)
  waiting for transfers between devices  28.4 us (29%)
  Pallas kernels  24.1 us (24%)
  blocking collectives  2.59 us (3%)
  other arithmetic  1.64 us (2%)
    ppermute x21, starting transfers between devices, swap(): return lax.ppermute(block, 'tm', [(i, i ^ mask) for i in range(size)])  37.2 us
    ppermute x21, waiting for transfers between devices, swap(): return lax.ppermute(block, 'tm', [(i, i ^ mask) for i in range(size)])  15.5 us
    pallas_call x3, Pallas kernels, inner(): pl.pallas_call(inner_kernel, grid=(count,), in_specs=[SMEM, pl.BlockSpec(...  13 us
    ppermute x1, waiting for transfers between devices, on_device(): next_mean = lax.ppermute(mean, 'tm', back)  12.9 us
    pallas_call x3, Pallas kernels, on_device(): pl.pallas_call(functools.partial(finish_kernel, total_frames), grid=(coun...  3.89 us
    pallas_call x3, Pallas kernels, border(): pl.pallas_call(functools.partial(border_kernel, first - spans[p > 0][0]),...  3.83 us
    pallas_call x1, Pallas kernels, on_device(): pl.pallas_call(functools.partial(edge_kernel, spans), in_specs=[pl.BlockS...  3.4 us
    psum x1, blocking collectives, on_device(): sums = lax.psum(sums[:, 0], 'pix')  2.59 us
  transfers between devices with their start and end apart: 24, of which 13 were waited for; matrix products, arithmetic and copies ran while one was open for 2% of the time, Pallas kernels for 20%

profile of v3, /device:TPU:0, one launch (start us, length us, event | category | flops | bytes accessed | tf_op | source)
XLA Modules:
  0.0 98.6 jit_solution(6556286689846392706)
XLA Ops:
  0.0 3.4 %edges.1 = (f32[136,1]{1,0:T(8,128)S(1)}, f32[3,320,128]{2,1,0:T(8,128)S(1)}, f32[5,320,128]{2,1,0:T(8,128)S(1)}) custom-call(f32[128,8192]{1,0:T(8,128)} %x_ref.5, f32[1,8192]{1,0:T(1,128)} %bitcast.5), custom_call_target="tpu_custom_call" | custom-call | tf_op jit(solution)/shard_map/edges/pallas_call | solution.py:305
  4.8 2.6 %psum.7 = f32[136]{0:T(256)S(1)} all-reduce(f32[136]{0:T(256)S(1)} %reduce), channel_id=1, replica_groups=mesh['tm'=16,'pix'=2] {'pix'}, use_global_device_ids=true, to_apply=%region_0.0 | all-reduce | flops 136 | bytes 1088 | tf_op jit(solution)/shard_map/psum | solution.py:323
  11.2 4.7 %inner_0.1 = (f32[3,512,128]{2,1,0:T(8,128)S(1)}, f32[3,512,128]{2,1,0:T(8,128)S(1)}, f32[3,8,128]{2,1,0:T(8,128)S(1)}) custom-call(f32[128]{0:T(128)S(1)} %slice_divide_fusion.mean_ref, f32[128,8192]{1,0:T(8,128)} %x_ref.5), custom_call_target="tpu_custom_call" | custom-call | tf_op jit(solution)/shard_map/inner_0/pallas_call | solution.py:331
  15.9 4.7 %inner_1.1 = (f32[3,512,128]{2,1,0:T(8,128)S(1)}, f32[3,512,128]{2,1,0:T(8,128)S(1)}, f32[3,8,128]{2,1,0:T(8,128)S(1)}) custom-call(f32[128]{0:T(128)S(1)} %slice_divide_fusion.mean_ref, f32[128,8192]{1,0:T(8,128)} %x_ref.5), custom_call_target="tpu_custom_call" | custom-call | tf_op jit(solution)/shard_map/inner_1/pallas_call | solution.py:331
  20.6 3.5 %inner_2.1 = (f32[2,512,128]{2,1,0:T(8,128)S(1)}, f32[2,512,128]{2,1,0:T(8,128)S(1)}, f32[2,8,128]{2,1,0:T(8,128)S(1)}) custom-call(f32[128]{0:T(128)S(1)} %slice_divide_fusion.mean_ref, f32[128,8192]{1,0:T(8,128)} %x_ref.5), custom_call_target="tpu_custom_call" | custom-call | tf_op jit(solution)/shard_map/inner_2/pallas_call | solution.py:331
  24.2 12.9 %collective-permute-done.mean_ref = f32[128]{0:T(128)S(1)} collective-permute-done((f32[128]{0:T(128)S(1)}, f32[128]{0:T(128)S(1)}, u32[]{:S(2)}, u32[]{:S(2)}) %collective-permute-start) | collective-permute-done | bytes 544 | tf_op jit(solution)/shard_map/ppermute | solution.py:325
  38.5 1.9 %collective-permute-start.5 = (f32[3,264,128]{2,1,0:T(8,128)S(1)}, f32[3,264,128]{2,1,0:T(8,128)S(1)}, u32[]{:S(2)}, u32[]{:S(2)}) collective-permute-start(f32[3,264,128]{2,1,0:T(8,128)S(1)} %get-tuple-element.74), channel_id=1, source_target_pairs={{0,8},{2,10},{4,12},{6,14},{8,0},{10,2},{12,4},{14,6},{16,24},{18,... | collective-permute-start | bytes 1216520 | tf_op jit(solution)/shard_map/ppermute | solution.py:228
  41.7 1.6 %collective-permute-start.4 = (f32[3,264,128]{2,1,0:T(8,128)S(1)}, f32[3,264,128]{2,1,0:T(8,128)S(1)}, u32[]{:S(2)}, u32[]{:S(2)}) collective-permute-start(f32[3,264,128]{2,1,0:T(8,128)S(1)} %get-tuple-element.78), channel_id=1, source_target_pairs={{0,4},{2,6},{4,0},{6,2},{8,12},{10,14},{12,8},{14,10},{16,20},{18,... | collective-permute-start | bytes 1216520 | tf_op jit(solution)/shard_map/ppermute | solution.py:228
  44.4 3.4 %collective-permute-start.3 = (f32[2,264,128]{2,1,0:T(8,128)S(1)}, f32[2,264,128]{2,1,0:T(8,128)S(1)}, u32[]{:S(2)}, u32[]{:S(2)}) collective-permute-start(f32[2,264,128]{2,1,0:T(8,128)S(1)} %get-tuple-element.83), channel_id=1, source_target_pairs={{0,2},{2,0},{4,6},{6,4},{8,10},{10,8},{12,14},{14,12},{16,18},{18,... | collective-permute-start | bytes 811016 | tf_op jit(solution)/shard_map/ppermute | solution.py:228
  50.7 2.5 %collective-permute-done.4 = f32[3,264,128]{2,1,0:T(8,128)S(1)} collective-permute-done((f32[3,264,128]{2,1,0:T(8,128)S(1)}, f32[3,264,128]{2,1,0:T(8,128)S(1)}, u32[]{:S(2)}, u32[]{:S(2)}) %collective-permute-start.4) | collective-permute-done | bytes 405536 | tf_op jit(solution)/shard_map/ppermute | solution.py:228
  53.3 3.5 %collective-permute-start.7 = (f32[3,136,128]{2,1,0:T(8,128)S(1)}, f32[3,136,128]{2,1,0:T(8,128)S(1)}, u32[]{:S(2)}, u32[]{:S(2)}) collective-permute-start(f32[3,136,128]{2,1,0:T(8,128)S(1)} %pad_maximum_fusion.4), channel_id=1, source_target_pairs={{0,2},{2,0},{4,6},{6,4},{8,10},{10,8},{12,14},{14,12},{16,18},{18,... | collective-permute-start | bytes 626696 | tf_op jit(solution)/shard_map/ppermute | solution.py:228
  57.1 2.3 %collective-permute-start.11 = (f32[3,72,128]{2,1,0:T(8,128)S(1)}, f32[3,72,128]{2,1,0:T(8,128)S(1)}, u32[]{:S(2)}, u32[]{:S(2)}) collective-permute-start(f32[3,72,128]{2,1,0:T(8,128)S(1)} %pad_maximum_fusion.9), channel_id=1, source_target_pairs={{0,2},{2,0},{4,6},{6,4},{8,10},{10,8},{12,14},{14,12},{16,18},{18,... | collective-permute-start | bytes 331784 | tf_op jit(solution)/shard_map/ppermute | solution.py:228
  59.4 2.4 %collective-permute-done.7 = f32[3,136,128]{2,1,0:T(8,128)S(1)} collective-permute-done((f32[3,136,128]{2,1,0:T(8,128)S(1)}, f32[3,136,128]{2,1,0:T(8,128)S(1)}, u32[]{:S(2)}, u32[]{:S(2)}) %collective-permute-start.7) | collective-permute-done | bytes 208928 | tf_op jit(solution)/shard_map/ppermute | solution.py:228
  63.3 1.7 %collective-permute-start.9 = (f32[2,72,128]{2,1,0:T(8,128)S(1)}, f32[2,72,128]{2,1,0:T(8,128)S(1)}, u32[]{:S(2)}, u32[]{:S(2)}) collective-permute-start(f32[2,72,128]{2,1,0:T(8,128)S(1)} %pad_maximum_fusion.13), channel_id=1, source_target_pairs={{0,4},{2,6},{4,0},{6,2},{8,12},{10,14},{12,8},{14,10},{16,20},{18,... | collective-permute-start | bytes 221192 | tf_op jit(solution)/shard_map/ppermute | solution.py:228
  65.1 2.9 %collective-permute-start.14 = (f32[3,72,128]{2,1,0:T(8,128)S(1)}, f32[3,72,128]{2,1,0:T(8,128)S(1)}, u32[]{:S(2)}, u32[]{:S(2)}) collective-permute-start(f32[3,72,128]{2,1,0:T(8,128)S(1)} %pad_maximum_fusion.11), channel_id=1, source_target_pairs={{0,16},{2,18},{4,20},{6,22},{8,24},{10,26},{12,28},{14,30},{16,0},... | collective-permute-start | bytes 331784 | tf_op jit(solution)/shard_map/ppermute | solution.py:228
  68.0 1.6 %collective-permute-done.10 = f32[3,72,128]{2,1,0:T(8,128)S(1)} collective-permute-done((f32[3,72,128]{2,1,0:T(8,128)S(1)}, f32[3,72,128]{2,1,0:T(8,128)S(1)}, u32[]{:S(2)}, u32[]{:S(2)}) %collective-permute-start.10) | collective-permute-done | bytes 110624 | tf_op jit(solution)/shard_map/ppermute | solution.py:228
  70.5 2.2 %collective-permute-start.12 = (f32[2,72,128]{2,1,0:T(8,128)S(1)}, f32[2,72,128]{2,1,0:T(8,128)S(1)}, u32[]{:S(2)}, u32[]{:S(2)}) collective-permute-start(f32[2,72,128]{2,1,0:T(8,128)S(1)} %pad_maximum_fusion.14), channel_id=1, source_target_pairs={{0,16},{2,18},{4,20},{6,22},{8,24},{10,26},{12,28},{14,30},{16,0},... | collective-permute-start | bytes 221192 | tf_op jit(solution)/shard_map/ppermute | solution.py:228
  73.4 2.8 %collective-permute-start.17 = (f32[3,64,128]{2,1,0:T(8,128)S(1)}, f32[3,64,128]{2,1,0:T(8,128)S(1)}, u32[]{:S(2)}, u32[]{:S(2)}) collective-permute-start(f32[3,64,128]{2,1,0:T(8,128)S(1)} %slice_add_fusion.7), channel_id=1, source_target_pairs={{0,2},{2,0},{4,6},{6,4},{8,10},{10,8},{12,14},{14,12},{16,18},{18,... | collective-permute-start | bytes 294920 | tf_op jit(solution)/shard_map/ppermute | solution.py:228
  77.3 1.8 %collective-permute-start.15 = (f32[2,64,128]{2,1,0:T(8,128)S(1)}, f32[2,64,128]{2,1,0:T(8,128)S(1)}, u32[]{:S(2)}, u32[]{:S(2)}) collective-permute-start(f32[2,64,128]{2,1,0:T(8,128)S(1)} %slice_add_fusion.10), channel_id=1, source_target_pairs={{0,4},{2,6},{4,0},{6,2},{8,12},{10,14},{12,8},{14,10},{16,20},{18,... | collective-permute-start | bytes 196616 | tf_op jit(solution)/shard_map/ppermute | solution.py:228
  80.9 2.7 %collective-permute-start.19 = (f32[3,128,128]{2,1,0:T(8,128)S(1)}, f32[3,128,128]{2,1,0:T(8,128)S(1)}, u32[]{:S(2)}, u32[]{:S(2)}) collective-permute-start(f32[3,128,128]{2,1,0:T(8,128)S(1)} %pad_maximum_fusion.6), channel_id=1, source_target_pairs={{0,2},{2,0},{4,6},{6,4},{8,10},{10,8},{12,14},{14,12},{16,18},{18,... | collective-permute-start | bytes 589832 | tf_op jit(solution)/shard_map/ppermute | solution.py:228
  83.7 1.5 %collective-permute-done.20 = f32[3,128,128]{2,1,0:T(8,128)S(1)} collective-permute-done((f32[3,128,128]{2,1,0:T(8,128)S(1)}, f32[3,128,128]{2,1,0:T(8,128)S(1)}, u32[]{:S(2)}, u32[]{:S(2)}) %collective-permute-start.20) | collective-permute-done | bytes 196640 | tf_op jit(solution)/shard_map/ppermute | solution.py:228
  88.4 1.9 %collective-permute-start.22 = (f32[3,256,128]{2,1,0:T(8,128)S(1)}, f32[3,256,128]{2,1,0:T(8,128)S(1)}, u32[]{:S(2)}, u32[]{:S(2)}) collective-permute-start(f32[3,256,128]{2,1,0:T(8,128)S(1)} %pad_maximum_fusion.1.mine_ref), channel_id=1, source_target_pairs={{0,4},{2,6},{4,0},{6,2},{8,12},{10,14},{12,8},{14,10},{16,20},{18,... | collective-permute-start | bytes 1179656 | tf_op jit(solution)/shard_map/ppermute | solution.py:228
  90.4 2.5 %collective-permute-start.21 = (f32[2,256,128]{2,1,0:T(8,128)S(1)}, f32[2,256,128]{2,1,0:T(8,128)S(1)}, u32[]{:S(2)}, u32[]{:S(2)}) collective-permute-start(f32[2,256,128]{2,1,0:T(8,128)S(1)} %pad_maximum_fusion.2.mine_ref), channel_id=1, source_target_pairs={{0,2},{2,0},{4,6},{6,4},{8,10},{10,8},{12,14},{14,12},{16,18},{18,... | collective-permute-start | bytes 786440 | tf_op jit(solution)/shard_map/ppermute | solution.py:228
  94.7 1.6 %collective-permute-done.22.got_ref = f32[3,256,128]{2,1,0:T(8,128)S(1)} collective-permute-done((f32[3,256,128]{2,1,0:T(8,128)S(1)}, f32[3,256,128]{2,1,0:T(8,128)S(1)}, u32[]{:S(2)}, u32[]{:S(2)}) %collective-permute-start.22) | collective-permute-done | bytes 393248 | tf_op jit(solution)/shard_map/ppermute | solution.py:228
  (89 shorter events, 25.5 us)
Async XLA Ops:
  3.4 20.7 %collective-permute-start.2 = (f32[3,320,128]{2,1,0:T(8,128)S(1)}, f32[3,320,128]{2,1,0:T(8,128)S(1)}, u32[]{:S(2)}, u32[]{:S(2)}) collective-permute-start(f32[3,320,128]{2,1,0:T(8,128)S(1)} %get-tuple-element.64), channel_id=1, source_target_pairs={{2,0},{4,2},{6,4},{8,6},{10,8},{12,10},{14,12},{16,14},{18,16},{20... | collective-permute-start | bytes 1474568 | tf_op jit(solution)/shard_map/ppermute | solution.py:322
  8.6 31.8 %collective-permute-start.1 = (f32[5,320,128]{2,1,0:T(8,128)S(1)}, f32[5,320,128]{2,1,0:T(8,128)S(1)}, u32[]{:S(2)}, u32[]{:S(2)}) collective-permute-start(f32[5,320,128]{2,1,0:T(8,128)S(1)} %get-tuple-element.61), channel_id=1, source_target_pairs={{2,0},{4,2},{6,4},{8,6},{10,8},{12,10},{14,12},{16,14},{18,16},{20... | collective-permute-start | bytes 2457608 | tf_op jit(solution)/shard_map/ppermute | solution.py:327
  9.9 27.2 %collective-permute-start = (f32[128]{0:T(128)S(1)}, f32[128]{0:T(128)S(1)}, u32[]{:S(2)}, u32[]{:S(2)}) collective-permute-start(f32[128]{0:T(128)S(1)} %slice_divide_fusion.mean_ref), channel_id=1, source_target_pairs={{2,0},{4,2},{6,4},{8,6},{10,8},{12,10},{14,12},{16,14},{18,16},{20... | collective-permute-start | bytes 1544 | tf_op jit(solution)/shard_map/ppermute | solution.py:325
  38.5 10.6 %collective-permute-start.5 = (f32[3,264,128]{2,1,0:T(8,128)S(1)}, f32[3,264,128]{2,1,0:T(8,128)S(1)}, u32[]{:S(2)}, u32[]{:S(2)}) collective-permute-start(f32[3,264,128]{2,1,0:T(8,128)S(1)} %get-tuple-element.74), channel_id=1, source_target_pairs={{0,8},{2,10},{4,12},{6,14},{8,0},{10,2},{12,4},{14,6},{16,24},{18,... | collective-permute-start | bytes 1216520 | tf_op jit(solution)/shard_map/ppermute | solution.py:228
  41.7 11.5 %collective-permute-start.4 = (f32[3,264,128]{2,1,0:T(8,128)S(1)}, f32[3,264,128]{2,1,0:T(8,128)S(1)}, u32[]{:S(2)}, u32[]{:S(2)}) collective-permute-start(f32[3,264,128]{2,1,0:T(8,128)S(1)} %get-tuple-element.78), channel_id=1, source_target_pairs={{0,4},{2,6},{4,0},{6,2},{8,12},{10,14},{12,8},{14,10},{16,20},{18,... | collective-permute-start | bytes 1216520 | tf_op jit(solution)/shard_map/ppermute | solution.py:228
  44.4 12.4 %collective-permute-start.3 = (f32[2,264,128]{2,1,0:T(8,128)S(1)}, f32[2,264,128]{2,1,0:T(8,128)S(1)}, u32[]{:S(2)}, u32[]{:S(2)}) collective-permute-start(f32[2,264,128]{2,1,0:T(8,128)S(1)} %get-tuple-element.83), channel_id=1, source_target_pairs={{0,2},{2,0},{4,6},{6,4},{8,10},{10,8},{12,14},{14,12},{16,18},{18,... | collective-permute-start | bytes 811016 | tf_op jit(solution)/shard_map/ppermute | solution.py:228
  49.2 7.8 %collective-permute-start.8 = (f32[3,136,128]{2,1,0:T(8,128)S(1)}, f32[3,136,128]{2,1,0:T(8,128)S(1)}, u32[]{:S(2)}, u32[]{:S(2)}) collective-permute-start(f32[3,136,128]{2,1,0:T(8,128)S(1)} %pad_maximum_fusion.3), channel_id=1, source_target_pairs={{0,4},{2,6},{4,0},{6,2},{8,12},{10,14},{12,8},{14,10},{16,20},{18,... | collective-permute-start | bytes 626696 | tf_op jit(solution)/shard_map/ppermute | solution.py:228
  53.3 8.5 %collective-permute-start.7 = (f32[3,136,128]{2,1,0:T(8,128)S(1)}, f32[3,136,128]{2,1,0:T(8,128)S(1)}, u32[]{:S(2)}, u32[]{:S(2)}) collective-permute-start(f32[3,136,128]{2,1,0:T(8,128)S(1)} %pad_maximum_fusion.4), channel_id=1, source_target_pairs={{0,2},{2,0},{4,6},{6,4},{8,10},{10,8},{12,14},{14,12},{16,18},{18,... | collective-permute-start | bytes 626696 | tf_op jit(solution)/shard_map/ppermute | solution.py:228
  56.9 5.9 %collective-permute-start.6 = (f32[2,136,128]{2,1,0:T(8,128)S(1)}, f32[2,136,128]{2,1,0:T(8,128)S(1)}, u32[]{:S(2)}, u32[]{:S(2)}) collective-permute-start(f32[2,136,128]{2,1,0:T(8,128)S(1)} %pad_maximum_fusion.7), channel_id=1, source_target_pairs={{0,8},{2,10},{4,12},{6,14},{8,0},{10,2},{12,4},{14,6},{16,24},{18,... | collective-permute-start | bytes 417800 | tf_op jit(solution)/shard_map/ppermute | solution.py:228
  57.1 7.9 %collective-permute-start.11 = (f32[3,72,128]{2,1,0:T(8,128)S(1)}, f32[3,72,128]{2,1,0:T(8,128)S(1)}, u32[]{:S(2)}, u32[]{:S(2)}) collective-permute-start(f32[3,72,128]{2,1,0:T(8,128)S(1)} %pad_maximum_fusion.9), channel_id=1, source_target_pairs={{0,2},{2,0},{4,6},{6,4},{8,10},{10,8},{12,14},{14,12},{16,18},{18,... | collective-permute-start | bytes 331784 | tf_op jit(solution)/shard_map/ppermute | solution.py:228
  62.8 6.8 %collective-permute-start.10 = (f32[3,72,128]{2,1,0:T(8,128)S(1)}, f32[3,72,128]{2,1,0:T(8,128)S(1)}, u32[]{:S(2)}, u32[]{:S(2)}) collective-permute-start(f32[3,72,128]{2,1,0:T(8,128)S(1)} %pad_maximum_fusion.10), channel_id=1, source_target_pairs={{0,8},{2,10},{4,12},{6,14},{8,0},{10,2},{12,4},{14,6},{16,24},{18,... | collective-permute-start | bytes 331784 | tf_op jit(solution)/shard_map/ppermute | solution.py:228
  63.3 6.3 %collective-permute-start.9 = (f32[2,72,128]{2,1,0:T(8,128)S(1)}, f32[2,72,128]{2,1,0:T(8,128)S(1)}, u32[]{:S(2)}, u32[]{:S(2)}) collective-permute-start(f32[2,72,128]{2,1,0:T(8,128)S(1)} %pad_maximum_fusion.13), channel_id=1, source_target_pairs={{0,4},{2,6},{4,0},{6,2},{8,12},{10,14},{12,8},{14,10},{16,20},{18,... | collective-permute-start | bytes 221192 | tf_op jit(solution)/shard_map/ppermute | solution.py:228
  65.1 8.3 %collective-permute-start.14 = (f32[3,72,128]{2,1,0:T(8,128)S(1)}, f32[3,72,128]{2,1,0:T(8,128)S(1)}, u32[]{:S(2)}, u32[]{:S(2)}) collective-permute-start(f32[3,72,128]{2,1,0:T(8,128)S(1)} %pad_maximum_fusion.11), channel_id=1, source_target_pairs={{0,16},{2,18},{4,20},{6,22},{8,24},{10,26},{12,28},{14,30},{16,0},... | collective-permute-start | bytes 331784 | tf_op jit(solution)/shard_map/ppermute | solution.py:228
  69.7 6.4 %collective-permute-start.13 = (f32[3,72,128]{2,1,0:T(8,128)S(1)}, f32[3,72,128]{2,1,0:T(8,128)S(1)}, u32[]{:S(2)}, u32[]{:S(2)}) collective-permute-start(f32[3,72,128]{2,1,0:T(8,128)S(1)} %pad_maximum_fusion.12), channel_id=1, source_target_pairs={{0,16},{2,18},{4,20},{6,22},{8,24},{10,26},{12,28},{14,30},{16,0},... | collective-permute-start | bytes 331784 | tf_op jit(solution)/shard_map/ppermute | solution.py:228
  70.5 6.8 %collective-permute-start.12 = (f32[2,72,128]{2,1,0:T(8,128)S(1)}, f32[2,72,128]{2,1,0:T(8,128)S(1)}, u32[]{:S(2)}, u32[]{:S(2)}) collective-permute-start(f32[2,72,128]{2,1,0:T(8,128)S(1)} %pad_maximum_fusion.14), channel_id=1, source_target_pairs={{0,16},{2,18},{4,20},{6,22},{8,24},{10,26},{12,28},{14,30},{16,0},... | collective-permute-start | bytes 221192 | tf_op jit(solution)/shard_map/ppermute | solution.py:228
  73.4 5.8 %collective-permute-start.17 = (f32[3,64,128]{2,1,0:T(8,128)S(1)}, f32[3,64,128]{2,1,0:T(8,128)S(1)}, u32[]{:S(2)}, u32[]{:S(2)}) collective-permute-start(f32[3,64,128]{2,1,0:T(8,128)S(1)} %slice_add_fusion.7), channel_id=1, source_target_pairs={{0,2},{2,0},{4,6},{6,4},{8,10},{10,8},{12,14},{14,12},{16,18},{18,... | collective-permute-start | bytes 294920 | tf_op jit(solution)/shard_map/ppermute | solution.py:228
  76.1 4.7 %collective-permute-start.16 = (f32[3,64,128]{2,1,0:T(8,128)S(1)}, f32[3,64,128]{2,1,0:T(8,128)S(1)}, u32[]{:S(2)}, u32[]{:S(2)}) collective-permute-start(f32[3,64,128]{2,1,0:T(8,128)S(1)} %slice_add_fusion.6), channel_id=1, source_target_pairs={{0,8},{2,10},{4,12},{6,14},{8,0},{10,2},{12,4},{14,6},{16,24},{18,... | collective-permute-start | bytes 294920 | tf_op jit(solution)/shard_map/ppermute | solution.py:228
  77.3 6.3 %collective-permute-start.15 = (f32[2,64,128]{2,1,0:T(8,128)S(1)}, f32[2,64,128]{2,1,0:T(8,128)S(1)}, u32[]{:S(2)}, u32[]{:S(2)}) collective-permute-start(f32[2,64,128]{2,1,0:T(8,128)S(1)} %slice_add_fusion.10), channel_id=1, source_target_pairs={{0,4},{2,6},{4,0},{6,2},{8,12},{10,14},{12,8},{14,10},{16,20},{18,... | collective-permute-start | bytes 196616 | tf_op jit(solution)/shard_map/ppermute | solution.py:228
  79.2 6.0 %collective-permute-start.20 = (f32[3,128,128]{2,1,0:T(8,128)S(1)}, f32[3,128,128]{2,1,0:T(8,128)S(1)}, u32[]{:S(2)}, u32[]{:S(2)}) collective-permute-start(f32[3,128,128]{2,1,0:T(8,128)S(1)} %pad_maximum_fusion.5), channel_id=1, source_target_pairs={{0,4},{2,6},{4,0},{6,2},{8,12},{10,14},{12,8},{14,10},{16,20},{18,... | collective-permute-start | bytes 589832 | tf_op jit(solution)/shard_map/ppermute | solution.py:228
  80.9 7.5 %collective-permute-start.19 = (f32[3,128,128]{2,1,0:T(8,128)S(1)}, f32[3,128,128]{2,1,0:T(8,128)S(1)}, u32[]{:S(2)}, u32[]{:S(2)}) collective-permute-start(f32[3,128,128]{2,1,0:T(8,128)S(1)} %pad_maximum_fusion.6), channel_id=1, source_target_pairs={{0,2},{2,0},{4,6},{6,4},{8,10},{10,8},{12,14},{14,12},{16,18},{18,... | collective-permute-start | bytes 589832 | tf_op jit(solution)/shard_map/ppermute | solution.py:228
  83.6 6.7 %collective-permute-start.18 = (f32[2,128,128]{2,1,0:T(8,128)S(1)}, f32[2,128,128]{2,1,0:T(8,128)S(1)}, u32[]{:S(2)}, u32[]{:S(2)}) collective-permute-start(f32[2,128,128]{2,1,0:T(8,128)S(1)} %pad_maximum_fusion.8), channel_id=1, source_target_pairs={{0,8},{2,10},{4,12},{6,14},{8,0},{10,2},{12,4},{14,6},{16,24},{18,... | collective-permute-start | bytes 393224 | tf_op jit(solution)/shard_map/ppermute | solution.py:228
  85.3 7.8 %collective-permute-start.23 = (f32[3,256,128]{2,1,0:T(8,128)S(1)}, f32[3,256,128]{2,1,0:T(8,128)S(1)}, u32[]{:S(2)}, u32[]{:S(2)}) collective-permute-start(f32[3,256,128]{2,1,0:T(8,128)S(1)} %pad_maximum_fusion.mine_ref), channel_id=1, source_target_pairs={{0,8},{2,10},{4,12},{6,14},{8,0},{10,2},{12,4},{14,6},{16,24},{18,... | collective-permute-start | bytes 1179656 | tf_op jit(solution)/shard_map/ppermute | solution.py:228
  88.4 7.8 %collective-permute-start.22 = (f32[3,256,128]{2,1,0:T(8,128)S(1)}, f32[3,256,128]{2,1,0:T(8,128)S(1)}, u32[]{:S(2)}, u32[]{:S(2)}) collective-permute-start(f32[3,256,128]{2,1,0:T(8,128)S(1)} %pad_maximum_fusion.1.mine_ref), channel_id=1, source_target_pairs={{0,4},{2,6},{4,0},{6,2},{8,12},{10,14},{12,8},{14,10},{16,20},{18,... | collective-permute-start | bytes 1179656 | tf_op jit(solution)/shard_map/ppermute | solution.py:228
  90.4 7.4 %collective-permute-start.21 = (f32[2,256,128]{2,1,0:T(8,128)S(1)}, f32[2,256,128]{2,1,0:T(8,128)S(1)}, u32[]{:S(2)}, u32[]{:S(2)}) collective-permute-start(f32[2,256,128]{2,1,0:T(8,128)S(1)} %pad_maximum_fusion.2.mine_ref), channel_id=1, source_target_pairs={{0,2},{2,0},{4,6},{6,4},{8,10},{10,8},{12,14},{14,12},{16,18},{18,... | collective-permute-start | bytes 786440 | tf_op jit(solution)/shard_map/ppermute | solution.py:228

commit v4 on v3

--- a/solution.py
+++ b/solution.py
@@ -180,25 +180,34 @@
     lax.fori_loop(0, groups, one_group, 0)
 
 
-def finish_kernel(total_frames, side_ref, mine_ref, got_ref, sum_ref, *refs):
-    out_ref = refs[-1]
+def finish_kernel(first, total_frames, side_ref, mine_ref, got_ref, sum_ref, *refs):
+    out_hbm, out_ref, sem = refs[-3:]
     split = LEVELS // 2
-    g = pl.program_id(0)
+    groups = mine_ref.shape[0]
     side = side_ref[0]
-    for c in range(SUB):
-        mean = sum_ref[g, c : c + 1, :] / total_frames
-        square = jnp.broadcast_to(mean * mean, (SUB, LANE))
-        for level in range(LEVELS):
-            own = side == level // split
-            for i in range(LAGS // SUB):
-                lag = lax.broadcasted_iota(jnp.int32, (SUB, LANE), 0) + (i * SUB + 1)
-                count = ((total_frames >> level) - lag).astype(jnp.float32)
-                row = (level % split) * LAGS + i * SUB
-                at = pl.ds(row * SUB + c, SUB, stride=SUB)
-                total = jnp.where(own, mine_ref[g, at, :], got_ref[g, at, :])
-                out_ref[level, i * SUB : (i + 1) * SUB, c * LANE : (c + 1) * LANE] = (
-                    total / (count * square)
-                )
+
+    def put(g):
+        at = pl.ds((first + g) * GROUP, GROUP)
+        return pltpu.make_async_copy(out_ref.at[g], out_hbm.at[:, :, at], sem.at[g])
+
+    for g in range(groups):
+        for c in range(SUB):
+            mean = sum_ref[g, c : c + 1, :] / total_frames
+            square = jnp.broadcast_to(mean * mean, (SUB, LANE))
+            for level in range(LEVELS):
+                own = side == level // split
+                for i in range(LAGS // SUB):
+                    lag = lax.broadcasted_iota(jnp.int32, (SUB, LANE), 0) + (i * SUB + 1)
+                    count = ((total_frames >> level) - lag).astype(jnp.float32)
+                    row = (level % split) * LAGS + i * SUB
+                    at = pl.ds(row * SUB + c, SUB, stride=SUB)
+                    total = jnp.where(own, mine_ref[g, at, :], got_ref[g, at, :])
+                    out_ref[
+                        g, level, i * SUB : (i + 1) * SUB, c * LANE : (c + 1) * LANE
+                    ] = total / (count * square)
+        put(g).start()
+    for g in range(groups):
+        put(g).wait()
 
 
 ROWS = LEVELS * LAGS
@@ -223,9 +232,14 @@
     return pl.BlockSpec((1, rows * SUB, LANE), lambda g: (g, 0, 0))
 
 
-def swap(block, mask):
-    size = lax.axis_size("tm")
-    return lax.ppermute(block, "tm", [(i, i ^ mask) for i in range(size)])
+def swap(block, masks):
+    size, cores = lax.axis_size("tm"), lax.axis_size("pix")
+    route = [
+        (i * cores + c, (i ^ masks[c % 2]) * cores + c)
+        for i in range(size)
+        for c in range(cores)
+    ]
+    return lax.ppermute(block, ("tm", "pix"), route)
 
 
 def after(value, token):
@@ -277,9 +291,10 @@
 
 def plan(groups, bits):
     x, y, z = (bits + bits[-1:] * 2)[:3]
-    tail = bits[3:]
     cuts = [groups * i // 8 for i in CUTS]
-    orders = [[z, y, x] + tail, [y, x, z] + tail, [x, z, y] + tail]
+    even = [[y, z, x], [x, y, z], [z, x, y]]
+    odd = [[x, y, z], [z, x, y], [y, z, x]]
+    orders = [list(zip(e + bits[3:], o + bits[3:])) for e, o in zip(even, odd)]
     orders = [o[: len(bits)] for o in orders]
     return [(a, b - a, o) for a, b, o in zip(cuts, cuts[1:], orders)]
 
@@ -295,7 +310,12 @@
     bits = [1 << b for b in range(size.bit_length() - 1)]
     parts = plan(groups, bits)
     me = lax.axis_index("tm")
-    uppers = {bit: (me & bit) != 0 for bit in bits}
+    odd = lax.axis_index("pix") % 2 == 1
+    uppers = {
+        masks: (me & jnp.where(odd, masks[1], masks[0])) != 0
+        for _, _, order in parts
+        for masks in order
+    }
     sides = {o[0]: uppers[o[0]].astype(jnp.int32).reshape(1) for _, _, o in parts}
     ref_weight, uppers, sides = lax.optimization_barrier((ref_weight, uppers, sides))
     stored = in_hbm(frames)
@@ -384,14 +404,15 @@
         held = [] if out is None else [out]
         part = sums[p]
         out = pl.pallas_call(
-            functools.partial(finish_kernel, total_frames),
-            grid=(count,),
+            functools.partial(finish_kernel, first, total_frames),
             in_specs=[SMEM, VMEM, VMEM, VMEM]
             + [pl.BlockSpec(memory_space=pl.ANY)] * len(held),
-            out_specs=pl.BlockSpec(
-                (LEVELS, LAGS, GROUP), lambda g, first=first: (0, 0, g + first)
-            ),
+            out_specs=pl.BlockSpec(memory_space=pl.ANY),
             out_shape=f32(LEVELS, LAGS, pixels),
+            scratch_shapes=[
+                pltpu.VMEM((count, LEVELS, LAGS, GROUP), jnp.float32),
+                pltpu.SemaphoreType.DMA((count,)),
+            ],
             input_output_aliases={4: 0} if held else {},
             compiler_params=params(),
             name=f"finish_{p}",

time: 98.9 us -> 96.3 us (0.974)
  waiting for transfers between devices: 28.4 us -> 27.2 us
  Pallas kernels: 24.1 us -> 23 us
    ppermute x21, waiting for transfers between devices: 15.5 us -> 14.2 us  [swap(): return lax.ppermute(block, ('tm', 'pix'), route)]
    pallas_call x3, Pallas kernels: 3.89 us -> 2.8 us  [on_device(): pl.pallas_call(functools.partial(finish_kernel, first, total_frames), in_...]
  transfers between devices with their start and end apart: 24 -> 24, of which waited for: 13 -> 12; matrix products, arithmetic and copies ran while one was open for 2% -> 2% of each run, Pallas kernels for 20% -> 19%
where the time goes in v4:
time: 96.3 us; the launch traced here: 96 us
  starting transfers between devices  40.7 us (42%)
  waiting for transfers between devices  27.2 us (28%)
  Pallas kernels  23 us (24%)
  blocking collectives  2.59 us (3%)
  other arithmetic  1.64 us (2%)
    ppermute x21, starting transfers between devices, swap(): return lax.ppermute(block, ('tm', 'pix'), route)  36.8 us
    ppermute x21, waiting for transfers between devices, swap(): return lax.ppermute(block, ('tm', 'pix'), route)  14.2 us
    pallas_call x3, Pallas kernels, inner(): pl.pallas_call(inner_kernel, grid=(count,), in_specs=[SMEM, pl.BlockSpec(...  13 us
    ppermute x1, waiting for transfers between devices, on_device(): next_mean = lax.ppermute(mean, 'tm', back)  12.9 us
    pallas_call x3, Pallas kernels, border(): pl.pallas_call(functools.partial(border_kernel, first - spans[p > 0][0]),...  3.83 us
    pallas_call x1, Pallas kernels, on_device(): pl.pallas_call(functools.partial(edge_kernel, spans), in_specs=[pl.BlockS...  3.4 us
    pallas_call x3, Pallas kernels, on_device(): pl.pallas_call(functools.partial(finish_kernel, first, total_frames), in_...  2.8 us
    psum x1, blocking collectives, on_device(): sums = lax.psum(sums[:, 0], 'pix')  2.59 us
  transfers between devices with their start and end apart: 24, of which 12 were waited for; matrix products, arithmetic and copies ran while one was open for 2% of the time, Pallas kernels for 19%

profile of v4, /device:TPU:0, one launch (start us, length us, event | category | flops | bytes accessed | tf_op | source)
XLA Modules:
  0.0 96.0 jit_solution(5895303662309328692)
XLA Ops:
  0.0 3.4 %edges.1 = (f32[136,1]{1,0:T(8,128)S(1)}, f32[3,320,128]{2,1,0:T(8,128)S(1)}, f32[5,320,128]{2,1,0:T(8,128)S(1)}) custom-call(f32[128,8192]{1,0:T(8,128)} %x_ref.5, f32[1,8192]{1,0:T(1,128)} %bitcast.5), custom_call_target="tpu_custom_call" | custom-call | tf_op jit(solution)/shard_map/edges/pallas_call | solution.py:325
  4.8 2.6 %psum.7 = f32[136]{0:T(256)S(1)} all-reduce(f32[136]{0:T(256)S(1)} %reduce), channel_id=1, replica_groups=mesh['tm'=16,'pix'=2] {'pix'}, use_global_device_ids=true, to_apply=%region_0.1 | all-reduce | flops 136 | bytes 1088 | tf_op jit(solution)/shard_map/psum | solution.py:343
  11.2 4.7 %inner_0.1 = (f32[3,512,128]{2,1,0:T(8,128)S(1)}, f32[3,512,128]{2,1,0:T(8,128)S(1)}, f32[3,8,128]{2,1,0:T(8,128)S(1)}) custom-call(f32[128]{0:T(128)S(1)} %slice_divide_fusion.mean_ref, f32[128,8192]{1,0:T(8,128)} %x_ref.5), custom_call_target="tpu_custom_call" | custom-call | tf_op jit(solution)/shard_map/inner_0/pallas_call | solution.py:351
  15.9 4.7 %inner_1.1 = (f32[3,512,128]{2,1,0:T(8,128)S(1)}, f32[3,512,128]{2,1,0:T(8,128)S(1)}, f32[3,8,128]{2,1,0:T(8,128)S(1)}) custom-call(f32[128]{0:T(128)S(1)} %slice_divide_fusion.mean_ref, f32[128,8192]{1,0:T(8,128)} %x_ref.5), custom_call_target="tpu_custom_call" | custom-call | tf_op jit(solution)/shard_map/inner_1/pallas_call | solution.py:351
  20.6 3.5 %inner_2.1 = (f32[2,512,128]{2,1,0:T(8,128)S(1)}, f32[2,512,128]{2,1,0:T(8,128)S(1)}, f32[2,8,128]{2,1,0:T(8,128)S(1)}) custom-call(f32[128]{0:T(128)S(1)} %slice_divide_fusion.mean_ref, f32[128,8192]{1,0:T(8,128)} %x_ref.5), custom_call_target="tpu_custom_call" | custom-call | tf_op jit(solution)/shard_map/inner_2/pallas_call | solution.py:351
  24.2 12.9 %collective-permute-done.mean_ref = f32[128]{0:T(128)S(1)} collective-permute-done((f32[128]{0:T(128)S(1)}, f32[128]{0:T(128)S(1)}, u32[]{:S(2)}, u32[]{:S(2)}) %collective-permute-start) | collective-permute-done | bytes 544 | tf_op jit(solution)/shard_map/ppermute | solution.py:345
  37.1 1.4 %border_0.1 = (f32[3,256,128]{2,1,0:T(8,128)S(1)}, f32[3,264,128]{2,1,0:T(8,128)S(1)}) custom-call(f32[128]{0:T(128)S(1)} %collective-permute-done.mean_ref, s32[1]{0:T(128)} %bitcast.1.side_ref, f32[3,320,128]{2,1,0:T(8,128)S(1)} %collective-permute-done.2.edge_ref, f32[3,512,128]{2,1,0:T(8,128)S(1)} %get-tuple-element.72.last_ref, ...), custom_call_target="tpu_custom_call" | custom-call | tf_op jit(solution)/shard_map/border_0/pallas_call | solution.py:375
  38.5 1.8 %collective-permute-start.5 = (f32[3,264,128]{2,1,0:T(8,128)S(1)}, f32[3,264,128]{2,1,0:T(8,128)S(1)}, u32[]{:S(2)}, u32[]{:S(2)}) collective-permute-start(f32[3,264,128]{2,1,0:T(8,128)S(1)} %get-tuple-element.74), channel_id=1, source_target_pairs={{0,4},{1,3},{2,6},{3,1},{4,0},{5,7},{6,2},{7,5},{8,12},{9,11},{10,... | collective-permute-start | bytes 1216520 | tf_op jit(solution)/shard_map/ppermute | solution.py:242
  40.3 1.4 %border_1.1 = (f32[3,256,128]{2,1,0:T(8,128)S(1)}, f32[3,264,128]{2,1,0:T(8,128)S(1)}) custom-call(f32[128]{0:T(128)S(1)} %collective-permute-done.mean_ref, s32[1]{0:T(128)} %bitcast.side_ref, f32[5,320,128]{2,1,0:T(8,128)S(1)} %collective-permute-done.1.edge_ref, f32[3,512,128]{2,1,0:T(8,128)S(1)} %get-tuple-element.76.last_ref, ...), custom_call_target="tpu_custom_call" | custom-call | tf_op jit(solution)/shard_map/border_1/pallas_call | solution.py:375
  41.7 3.4 %collective-permute-start.4 = (f32[3,264,128]{2,1,0:T(8,128)S(1)}, f32[3,264,128]{2,1,0:T(8,128)S(1)}, u32[]{:S(2)}, u32[]{:S(2)}) collective-permute-start(f32[3,264,128]{2,1,0:T(8,128)S(1)} %get-tuple-element.78), channel_id=1, source_target_pairs={{0,2},{1,9},{2,0},{3,11},{4,6},{5,13},{6,4},{7,15},{8,10},{9,1},{1... | collective-permute-start | bytes 1216520 | tf_op jit(solution)/shard_map/ppermute | solution.py:242
  46.1 1.6 %collective-permute-start.3 = (f32[2,264,128]{2,1,0:T(8,128)S(1)}, f32[2,264,128]{2,1,0:T(8,128)S(1)}, u32[]{:S(2)}, u32[]{:S(2)}) collective-permute-start(f32[2,264,128]{2,1,0:T(8,128)S(1)} %get-tuple-element.83), channel_id=1, source_target_pairs={{0,8},{1,5},{2,10},{3,7},{4,12},{5,1},{6,14},{7,3},{8,0},{9,13},{1... | collective-permute-start | bytes 811016 | tf_op jit(solution)/shard_map/ppermute | solution.py:242
  49.2 1.7 %collective-permute-done.4 = f32[3,264,128]{2,1,0:T(8,128)S(1)} collective-permute-done((f32[3,264,128]{2,1,0:T(8,128)S(1)}, f32[3,264,128]{2,1,0:T(8,128)S(1)}, u32[]{:S(2)}, u32[]{:S(2)}) %collective-permute-start.4) | collective-permute-done | bytes 405536 | tf_op jit(solution)/shard_map/ppermute | solution.py:242
  52.8 4.5 %collective-permute-start.6 = (f32[2,136,128]{2,1,0:T(8,128)S(1)}, f32[2,136,128]{2,1,0:T(8,128)S(1)}, u32[]{:S(2)}, u32[]{:S(2)}) collective-permute-start(f32[2,136,128]{2,1,0:T(8,128)S(1)} %pad_maximum_fusion.7), channel_id=1, source_target_pairs={{0,2},{1,9},{2,0},{3,11},{4,6},{5,13},{6,4},{7,15},{8,10},{9,1},{1... | collective-permute-start | bytes 417800 | tf_op jit(solution)/shard_map/ppermute | solution.py:242
  57.3 3.0 %collective-permute-start.11 = (f32[3,72,128]{2,1,0:T(8,128)S(1)}, f32[3,72,128]{2,1,0:T(8,128)S(1)}, u32[]{:S(2)}, u32[]{:S(2)}) collective-permute-start(f32[3,72,128]{2,1,0:T(8,128)S(1)} %pad_maximum_fusion.9), channel_id=1, source_target_pairs={{0,2},{1,9},{2,0},{3,11},{4,6},{5,13},{6,4},{7,15},{8,10},{9,1},{1... | collective-permute-start | bytes 331784 | tf_op jit(solution)/shard_map/ppermute | solution.py:242
  61.9 2.4 %collective-permute-start.9 = (f32[2,72,128]{2,1,0:T(8,128)S(1)}, f32[2,72,128]{2,1,0:T(8,128)S(1)}, u32[]{:S(2)}, u32[]{:S(2)}) collective-permute-start(f32[2,72,128]{2,1,0:T(8,128)S(1)} %pad_maximum_fusion.13), channel_id=1, source_target_pairs={{0,4},{1,3},{2,6},{3,1},{4,0},{5,7},{6,2},{7,5},{8,12},{9,11},{10,... | collective-permute-start | bytes 221192 | tf_op jit(solution)/shard_map/ppermute | solution.py:242
  64.4 1.3 %collective-permute-start.14 = (f32[3,72,128]{2,1,0:T(8,128)S(1)}, f32[3,72,128]{2,1,0:T(8,128)S(1)}, u32[]{:S(2)}, u32[]{:S(2)}) collective-permute-start(f32[3,72,128]{2,1,0:T(8,128)S(1)} %pad_maximum_fusion.11), channel_id=1, source_target_pairs={{0,16},{1,17},{2,18},{3,19},{4,20},{5,21},{6,22},{7,23},{8,24},{9,... | collective-permute-start | bytes 331784 | tf_op jit(solution)/shard_map/ppermute | solution.py:242
  66.7 2.1 %collective-permute-start.13 = (f32[3,72,128]{2,1,0:T(8,128)S(1)}, f32[3,72,128]{2,1,0:T(8,128)S(1)}, u32[]{:S(2)}, u32[]{:S(2)}) collective-permute-start(f32[3,72,128]{2,1,0:T(8,128)S(1)} %pad_maximum_fusion.12), channel_id=1, source_target_pairs={{0,16},{1,17},{2,18},{3,19},{4,20},{5,21},{6,22},{7,23},{8,24},{9,... | collective-permute-start | bytes 331784 | tf_op jit(solution)/shard_map/ppermute | solution.py:242
  69.7 1.5 %collective-permute-done.14 = f32[3,72,128]{2,1,0:T(8,128)S(1)} collective-permute-done((f32[3,72,128]{2,1,0:T(8,128)S(1)}, f32[3,72,128]{2,1,0:T(8,128)S(1)}, u32[]{:S(2)}, u32[]{:S(2)}) %collective-permute-start.14) | collective-permute-done | bytes 110624 | tf_op jit(solution)/shard_map/ppermute | solution.py:242
  74.6 2.8 %collective-permute-start.15 = (f32[2,64,128]{2,1,0:T(8,128)S(1)}, f32[2,64,128]{2,1,0:T(8,128)S(1)}, u32[]{:S(2)}, u32[]{:S(2)}) collective-permute-start(f32[2,64,128]{2,1,0:T(8,128)S(1)} %slice_add_fusion.10), channel_id=1, source_target_pairs={{0,4},{1,3},{2,6},{3,1},{4,0},{5,7},{6,2},{7,5},{8,12},{9,11},{10,... | collective-permute-start | bytes 196616 | tf_op jit(solution)/shard_map/ppermute | solution.py:242
  78.5 1.9 %collective-permute-start.19 = (f32[3,128,128]{2,1,0:T(8,128)S(1)}, f32[3,128,128]{2,1,0:T(8,128)S(1)}, u32[]{:S(2)}, u32[]{:S(2)}) collective-permute-start(f32[3,128,128]{2,1,0:T(8,128)S(1)} %pad_maximum_fusion.6), channel_id=1, source_target_pairs={{0,4},{1,3},{2,6},{3,1},{4,0},{5,7},{6,2},{7,5},{8,12},{9,11},{10,... | collective-permute-start | bytes 589832 | tf_op jit(solution)/shard_map/ppermute | solution.py:242
  80.5 1.5 %collective-permute-start.18 = (f32[2,128,128]{2,1,0:T(8,128)S(1)}, f32[2,128,128]{2,1,0:T(8,128)S(1)}, u32[]{:S(2)}, u32[]{:S(2)}) collective-permute-start(f32[2,128,128]{2,1,0:T(8,128)S(1)} %pad_maximum_fusion.8), channel_id=1, source_target_pairs={{0,2},{1,9},{2,0},{3,11},{4,6},{5,13},{6,4},{7,15},{8,10},{9,1},{1... | collective-permute-start | bytes 393224 | tf_op jit(solution)/shard_map/ppermute | solution.py:242
  82.0 3.3 %collective-permute-done.20 = f32[3,128,128]{2,1,0:T(8,128)S(1)} collective-permute-done((f32[3,128,128]{2,1,0:T(8,128)S(1)}, f32[3,128,128]{2,1,0:T(8,128)S(1)}, u32[]{:S(2)}, u32[]{:S(2)}) %collective-permute-start.20) | collective-permute-done | bytes 196640 | tf_op jit(solution)/shard_map/ppermute | solution.py:242
  85.6 2.1 %collective-permute-start.22 = (f32[3,256,128]{2,1,0:T(8,128)S(1)}, f32[3,256,128]{2,1,0:T(8,128)S(1)}, u32[]{:S(2)}, u32[]{:S(2)}) collective-permute-start(f32[3,256,128]{2,1,0:T(8,128)S(1)} %pad_maximum_fusion.1.mine_ref), channel_id=1, source_target_pairs={{0,2},{1,9},{2,0},{3,11},{4,6},{5,13},{6,4},{7,15},{8,10},{9,1},{1... | collective-permute-start | bytes 1179656 | tf_op jit(solution)/shard_map/ppermute | solution.py:242
  88.8 4.4 %collective-permute-done.23.got_ref = f32[3,256,128]{2,1,0:T(8,128)S(1)} collective-permute-done((f32[3,256,128]{2,1,0:T(8,128)S(1)}, f32[3,256,128]{2,1,0:T(8,128)S(1)}, u32[]{:S(2)}, u32[]{:S(2)}) %collective-permute-start.23) | collective-permute-done | bytes 393248 | tf_op jit(solution)/shard_map/ppermute | solution.py:242
  (89 shorter events, 21.8 us)
Async XLA Ops:
  3.4 20.7 %collective-permute-start.2 = (f32[3,320,128]{2,1,0:T(8,128)S(1)}, f32[3,320,128]{2,1,0:T(8,128)S(1)}, u32[]{:S(2)}, u32[]{:S(2)}) collective-permute-start(f32[3,320,128]{2,1,0:T(8,128)S(1)} %get-tuple-element.64), channel_id=1, source_target_pairs={{2,0},{4,2},{6,4},{8,6},{10,8},{12,10},{14,12},{16,14},{18,16},{20... | collective-permute-start | bytes 1474568 | tf_op jit(solution)/shard_map/ppermute | solution.py:342
  8.6 31.7 %collective-permute-start.1 = (f32[5,320,128]{2,1,0:T(8,128)S(1)}, f32[5,320,128]{2,1,0:T(8,128)S(1)}, u32[]{:S(2)}, u32[]{:S(2)}) collective-permute-start(f32[5,320,128]{2,1,0:T(8,128)S(1)} %get-tuple-element.61), channel_id=1, source_target_pairs={{2,0},{4,2},{6,4},{8,6},{10,8},{12,10},{14,12},{16,14},{18,16},{20... | collective-permute-start | bytes 2457608 | tf_op jit(solution)/shard_map/ppermute | solution.py:347
  9.9 27.2 %collective-permute-start = (f32[128]{0:T(128)S(1)}, f32[128]{0:T(128)S(1)}, u32[]{:S(2)}, u32[]{:S(2)}) collective-permute-start(f32[128]{0:T(128)S(1)} %slice_divide_fusion.mean_ref), channel_id=1, source_target_pairs={{2,0},{4,2},{6,4},{8,6},{10,8},{12,10},{14,12},{16,14},{18,16},{20... | collective-permute-start | bytes 1544 | tf_op jit(solution)/shard_map/ppermute | solution.py:345
  38.5 9.3 %collective-permute-start.5 = (f32[3,264,128]{2,1,0:T(8,128)S(1)}, f32[3,264,128]{2,1,0:T(8,128)S(1)}, u32[]{:S(2)}, u32[]{:S(2)}) collective-permute-start(f32[3,264,128]{2,1,0:T(8,128)S(1)} %get-tuple-element.74), channel_id=1, source_target_pairs={{0,4},{1,3},{2,6},{3,1},{4,0},{5,7},{6,2},{7,5},{8,12},{9,11},{10,... | collective-permute-start | bytes 1216520 | tf_op jit(solution)/shard_map/ppermute | solution.py:242
  41.7 9.2 %collective-permute-start.4 = (f32[3,264,128]{2,1,0:T(8,128)S(1)}, f32[3,264,128]{2,1,0:T(8,128)S(1)}, u32[]{:S(2)}, u32[]{:S(2)}) collective-permute-start(f32[3,264,128]{2,1,0:T(8,128)S(1)} %get-tuple-element.78), channel_id=1, source_target_pairs={{0,2},{1,9},{2,0},{3,11},{4,6},{5,13},{6,4},{7,15},{8,10},{9,1},{1... | collective-permute-start | bytes 1216520 | tf_op jit(solution)/shard_map/ppermute | solution.py:242
  46.1 6.5 %collective-permute-start.3 = (f32[2,264,128]{2,1,0:T(8,128)S(1)}, f32[2,264,128]{2,1,0:T(8,128)S(1)}, u32[]{:S(2)}, u32[]{:S(2)}) collective-permute-start(f32[2,264,128]{2,1,0:T(8,128)S(1)} %get-tuple-element.83), channel_id=1, source_target_pairs={{0,8},{1,5},{2,10},{3,7},{4,12},{5,1},{6,14},{7,3},{8,0},{9,13},{1... | collective-permute-start | bytes 811016 | tf_op jit(solution)/shard_map/ppermute | solution.py:242
  47.9 9.3 %collective-permute-start.8 = (f32[3,136,128]{2,1,0:T(8,128)S(1)}, f32[3,136,128]{2,1,0:T(8,128)S(1)}, u32[]{:S(2)}, u32[]{:S(2)}) collective-permute-start(f32[3,136,128]{2,1,0:T(8,128)S(1)} %pad_maximum_fusion.3), channel_id=1, source_target_pairs={{0,8},{1,5},{2,10},{3,7},{4,12},{5,1},{6,14},{7,3},{8,0},{9,13},{1... | collective-permute-start | bytes 626696 | tf_op jit(solution)/shard_map/ppermute | solution.py:242
  51.0 9.3 %collective-permute-start.7 = (f32[3,136,128]{2,1,0:T(8,128)S(1)}, f32[3,136,128]{2,1,0:T(8,128)S(1)}, u32[]{:S(2)}, u32[]{:S(2)}) collective-permute-start(f32[3,136,128]{2,1,0:T(8,128)S(1)} %pad_maximum_fusion.4), channel_id=1, source_target_pairs={{0,4},{1,3},{2,6},{3,1},{4,0},{5,7},{6,2},{7,5},{8,12},{9,11},{10,... | collective-permute-start | bytes 626696 | tf_op jit(solution)/shard_map/ppermute | solution.py:242
  52.8 7.9 %collective-permute-start.6 = (f32[2,136,128]{2,1,0:T(8,128)S(1)}, f32[2,136,128]{2,1,0:T(8,128)S(1)}, u32[]{:S(2)}, u32[]{:S(2)}) collective-permute-start(f32[2,136,128]{2,1,0:T(8,128)S(1)} %pad_maximum_fusion.7), channel_id=1, source_target_pairs={{0,2},{1,9},{2,0},{3,11},{4,6},{5,13},{6,4},{7,15},{8,10},{9,1},{1... | collective-permute-start | bytes 417800 | tf_op jit(solution)/shard_map/ppermute | solution.py:242
  57.3 7.0 %collective-permute-start.11 = (f32[3,72,128]{2,1,0:T(8,128)S(1)}, f32[3,72,128]{2,1,0:T(8,128)S(1)}, u32[]{:S(2)}, u32[]{:S(2)}) collective-permute-start(f32[3,72,128]{2,1,0:T(8,128)S(1)} %pad_maximum_fusion.9), channel_id=1, source_target_pairs={{0,2},{1,9},{2,0},{3,11},{4,6},{5,13},{6,4},{7,15},{8,10},{9,1},{1... | collective-permute-start | bytes 331784 | tf_op jit(solution)/shard_map/ppermute | solution.py:242
  60.7 5.5 %collective-permute-start.10 = (f32[3,72,128]{2,1,0:T(8,128)S(1)}, f32[3,72,128]{2,1,0:T(8,128)S(1)}, u32[]{:S(2)}, u32[]{:S(2)}) collective-permute-start(f32[3,72,128]{2,1,0:T(8,128)S(1)} %pad_maximum_fusion.10), channel_id=1, source_target_pairs={{0,8},{1,5},{2,10},{3,7},{4,12},{5,1},{6,14},{7,3},{8,0},{9,13},{1... | collective-permute-start | bytes 331784 | tf_op jit(solution)/shard_map/ppermute | solution.py:242
  61.9 4.7 %collective-permute-start.9 = (f32[2,72,128]{2,1,0:T(8,128)S(1)}, f32[2,72,128]{2,1,0:T(8,128)S(1)}, u32[]{:S(2)}, u32[]{:S(2)}) collective-permute-start(f32[2,72,128]{2,1,0:T(8,128)S(1)} %pad_maximum_fusion.13), channel_id=1, source_target_pairs={{0,4},{1,3},{2,6},{3,1},{4,0},{5,7},{6,2},{7,5},{8,12},{9,11},{10,... | collective-permute-start | bytes 221192 | tf_op jit(solution)/shard_map/ppermute | solution.py:242
  64.4 6.8 %collective-permute-start.14 = (f32[3,72,128]{2,1,0:T(8,128)S(1)}, f32[3,72,128]{2,1,0:T(8,128)S(1)}, u32[]{:S(2)}, u32[]{:S(2)}) collective-permute-start(f32[3,72,128]{2,1,0:T(8,128)S(1)} %pad_maximum_fusion.11), channel_id=1, source_target_pairs={{0,16},{1,17},{2,18},{3,19},{4,20},{5,21},{6,22},{7,23},{8,24},{9,... | collective-permute-start | bytes 331784 | tf_op jit(solution)/shard_map/ppermute | solution.py:242
  66.7 6.9 %collective-permute-start.13 = (f32[3,72,128]{2,1,0:T(8,128)S(1)}, f32[3,72,128]{2,1,0:T(8,128)S(1)}, u32[]{:S(2)}, u32[]{:S(2)}) collective-permute-start(f32[3,72,128]{2,1,0:T(8,128)S(1)} %pad_maximum_fusion.12), channel_id=1, source_target_pairs={{0,16},{1,17},{2,18},{3,19},{4,20},{5,21},{6,22},{7,23},{8,24},{9,... | collective-permute-start | bytes 331784 | tf_op jit(solution)/shard_map/ppermute | solution.py:242
  68.8 5.8 %collective-permute-start.12 = (f32[2,72,128]{2,1,0:T(8,128)S(1)}, f32[2,72,128]{2,1,0:T(8,128)S(1)}, u32[]{:S(2)}, u32[]{:S(2)}) collective-permute-start(f32[2,72,128]{2,1,0:T(8,128)S(1)} %pad_maximum_fusion.14), channel_id=1, source_target_pairs={{0,16},{1,17},{2,18},{3,19},{4,20},{5,21},{6,22},{7,23},{8,24},{9,... | collective-permute-start | bytes 221192 | tf_op jit(solution)/shard_map/ppermute | solution.py:242
  71.2 6.2 %collective-permute-start.17 = (f32[3,64,128]{2,1,0:T(8,128)S(1)}, f32[3,64,128]{2,1,0:T(8,128)S(1)}, u32[]{:S(2)}, u32[]{:S(2)}) collective-permute-start(f32[3,64,128]{2,1,0:T(8,128)S(1)} %slice_add_fusion.7), channel_id=1, source_target_pairs={{0,2},{1,9},{2,0},{3,11},{4,6},{5,13},{6,4},{7,15},{8,10},{9,1},{1... | collective-permute-start | bytes 294920 | tf_op jit(solution)/shard_map/ppermute | solution.py:242
  73.6 4.8 %collective-permute-start.16 = (f32[3,64,128]{2,1,0:T(8,128)S(1)}, f32[3,64,128]{2,1,0:T(8,128)S(1)}, u32[]{:S(2)}, u32[]{:S(2)}) collective-permute-start(f32[3,64,128]{2,1,0:T(8,128)S(1)} %slice_add_fusion.6), channel_id=1, source_target_pairs={{0,8},{1,5},{2,10},{3,7},{4,12},{5,1},{6,14},{7,3},{8,0},{9,13},{1... | collective-permute-start | bytes 294920 | tf_op jit(solution)/shard_map/ppermute | solution.py:242
  74.6 5.8 %collective-permute-start.15 = (f32[2,64,128]{2,1,0:T(8,128)S(1)}, f32[2,64,128]{2,1,0:T(8,128)S(1)}, u32[]{:S(2)}, u32[]{:S(2)}) collective-permute-start(f32[2,64,128]{2,1,0:T(8,128)S(1)} %slice_add_fusion.10), channel_id=1, source_target_pairs={{0,4},{1,3},{2,6},{3,1},{4,0},{5,7},{6,2},{7,5},{8,12},{9,11},{10,... | collective-permute-start | bytes 196616 | tf_op jit(solution)/shard_map/ppermute | solution.py:242
  77.5 7.8 %collective-permute-start.20 = (f32[3,128,128]{2,1,0:T(8,128)S(1)}, f32[3,128,128]{2,1,0:T(8,128)S(1)}, u32[]{:S(2)}, u32[]{:S(2)}) collective-permute-start(f32[3,128,128]{2,1,0:T(8,128)S(1)} %pad_maximum_fusion.5), channel_id=1, source_target_pairs={{0,8},{1,5},{2,10},{3,7},{4,12},{5,1},{6,14},{7,3},{8,0},{9,13},{1... | collective-permute-start | bytes 589832 | tf_op jit(solution)/shard_map/ppermute | solution.py:242
  78.5 7.0 %collective-permute-start.19 = (f32[3,128,128]{2,1,0:T(8,128)S(1)}, f32[3,128,128]{2,1,0:T(8,128)S(1)}, u32[]{:S(2)}, u32[]{:S(2)}) collective-permute-start(f32[3,128,128]{2,1,0:T(8,128)S(1)} %pad_maximum_fusion.6), channel_id=1, source_target_pairs={{0,4},{1,3},{2,6},{3,1},{4,0},{5,7},{6,2},{7,5},{8,12},{9,11},{10,... | collective-permute-start | bytes 589832 | tf_op jit(solution)/shard_map/ppermute | solution.py:242
  80.5 7.2 %collective-permute-start.18 = (f32[2,128,128]{2,1,0:T(8,128)S(1)}, f32[2,128,128]{2,1,0:T(8,128)S(1)}, u32[]{:S(2)}, u32[]{:S(2)}) collective-permute-start(f32[2,128,128]{2,1,0:T(8,128)S(1)} %pad_maximum_fusion.8), channel_id=1, source_target_pairs={{0,2},{1,9},{2,0},{3,11},{4,6},{5,13},{6,4},{7,15},{8,10},{9,1},{1... | collective-permute-start | bytes 393224 | tf_op jit(solution)/shard_map/ppermute | solution.py:242
  85.3 7.8 %collective-permute-start.23 = (f32[3,256,128]{2,1,0:T(8,128)S(1)}, f32[3,256,128]{2,1,0:T(8,128)S(1)}, u32[]{:S(2)}, u32[]{:S(2)}) collective-permute-start(f32[3,256,128]{2,1,0:T(8,128)S(1)} %pad_maximum_fusion.mine_ref), channel_id=1, source_target_pairs={{0,4},{1,3},{2,6},{3,1},{4,0},{5,7},{6,2},{7,5},{8,12},{9,11},{10,... | collective-permute-start | bytes 1179656 | tf_op jit(solution)/shard_map/ppermute | solution.py:242
  85.6 8.6 %collective-permute-start.22 = (f32[3,256,128]{2,1,0:T(8,128)S(1)}, f32[3,256,128]{2,1,0:T(8,128)S(1)}, u32[]{:S(2)}, u32[]{:S(2)}) collective-permute-start(f32[3,256,128]{2,1,0:T(8,128)S(1)} %pad_maximum_fusion.1.mine_ref), channel_id=1, source_target_pairs={{0,2},{1,9},{2,0},{3,11},{4,6},{5,13},{6,4},{7,15},{8,10},{9,1},{1... | collective-permute-start | bytes 1179656 | tf_op jit(solution)/shard_map/ppermute | solution.py:242
  87.7 7.4 %collective-permute-start.21 = (f32[2,256,128]{2,1,0:T(8,128)S(1)}, f32[2,256,128]{2,1,0:T(8,128)S(1)}, u32[]{:S(2)}, u32[]{:S(2)}) collective-permute-start(f32[2,256,128]{2,1,0:T(8,128)S(1)} %pad_maximum_fusion.2.mine_ref), channel_id=1, source_target_pairs={{0,8},{1,5},{2,10},{3,7},{4,12},{5,1},{6,14},{7,3},{8,0},{9,13},{1... | collective-permute-start | bytes 786440 | tf_op jit(solution)/shard_map/ppermute | solution.py:242

commit v5 on v4

--- a/solution.py
+++ b/solution.py
@@ -18,14 +18,12 @@
     return ref[row * SUB : (row + 1) * SUB, :]
 
 
-def edge_kernel(spans, x_hbm, w_hbm, sums_ref, *refs):
-    edge_refs, refs = refs[: len(spans)], refs[len(spans) :]
-    x_ref, w_ref, tall_ref, acc_ref, sem, w_sem = refs
+def edge_kernel(first, x_hbm, w_hbm, sums_ref, edge_ref, x_ref, w_ref, tall_ref, acc_ref, sem, w_sem):
     groups, rows, _ = x_ref.shape
     half = LAGS // 2
 
     def fetch(g):
-        at = pl.ds(pl.multiple_of(g * GROUP, GROUP), GROUP)
+        at = pl.ds(pl.multiple_of((first + g) * GROUP, GROUP), GROUP)
         return pltpu.make_async_copy(x_hbm.at[:, at], x_ref.at[g], sem.at[g])
 
     weights = pltpu.make_async_copy(w_hbm, w_ref, w_sem)
@@ -35,11 +33,10 @@
     acc_ref[...] = jnp.zeros_like(acc_ref)
     weights.wait()
 
-    def one_group(first, edge_ref, slot, carry):
-        g = slot + first
+    def one_group(g, carry):
         fetch(g).wait()
         for c in range(SUB):
-            at = pl.ds(pl.multiple_of(g * GROUP + c * LANE, LANE), LANE)
+            at = pl.ds(pl.multiple_of((first + g) * GROUP + c * LANE, LANE), LANE)
             weight = jnp.broadcast_to(w_ref[:, at], (SUB, LANE))
             acc_ref[rows : rows + SUB, :] += weight
             for i in range(rows // SUB):
@@ -47,7 +44,7 @@
                 value = x_ref[g, part, c * LANE : (c + 1) * LANE]
                 acc_ref[part, :] += value * weight
                 tall_ref[pl.ds(i * SUB * SUB + c, SUB, stride=SUB), :] = value
-        edge_ref[slot, : LAGS * SUB, :] = tall_ref[: LAGS * SUB, :]
+        edge_ref[g, : LAGS * SUB, :] = tall_ref[: LAGS * SUB, :]
         for level in range(1, LEVELS):
             span = 1 << level
             for j in range(half):
@@ -55,11 +52,10 @@
                 while len(group) > 1:
                     group = [(a + b) * 0.5 for a, b in zip(group[::2], group[1::2])]
                 row = LAGS + (level - 1) * half + j
-                edge_ref[slot, row * SUB : (row + 1) * SUB, :] = group[0]
+                edge_ref[g, row * SUB : (row + 1) * SUB, :] = group[0]
         return carry
 
-    for (first, count), edge_ref in zip(spans, edge_refs):
-        lax.fori_loop(0, count, functools.partial(one_group, first, edge_ref), 0)
+    lax.fori_loop(0, groups, one_group, 0)
     sums_ref[...] = jnp.sum(acc_ref[...], axis=1, keepdims=True)
 
 
@@ -322,23 +318,28 @@
     head = parts[0][1]
     spans = [(0, head), (head, groups - head)]
     back = [(i, i - 1) for i in range(1, size)]
-    sums, *edges = pl.pallas_call(
-        functools.partial(edge_kernel, spans),
-        in_specs=[pl.BlockSpec(memory_space=pl.ANY)] * 2,
-        out_specs=[VMEM] * (1 + len(spans)),
-        out_shape=[f32(rows + SUB, 1)]
-        + [f32(count, EDGE_ROWS * SUB, LANE) for _, count in spans],
-        scratch_shapes=[
-            pltpu.VMEM((groups, rows, GROUP), jnp.float32),
-            pltpu.VMEM((1, pixels), jnp.float32),
-            pltpu.VMEM((rows * SUB, LANE), jnp.float32),
-            pltpu.VMEM((rows + SUB, LANE), jnp.float32),
-            pltpu.SemaphoreType.DMA((groups,)),
-            pltpu.SemaphoreType.DMA,
-        ],
-        compiler_params=params(),
-        name="edges",
-    )(stored, in_hbm(ref_weight.reshape(1, pixels)))
+    all_sums, edges = [], []
+    for p, (first, count) in enumerate(spans):
+        source = stored if p == 0 else in_hbm(after(frames, all_sums[0]))
+        sums, edge = pl.pallas_call(
+            functools.partial(edge_kernel, first),
+            in_specs=[pl.BlockSpec(memory_space=pl.ANY)] * 2,
+            out_specs=[VMEM, VMEM],
+            out_shape=[f32(rows + SUB, 1), f32(count, EDGE_ROWS * SUB, LANE)],
+            scratch_shapes=[
+                pltpu.VMEM((count, rows, GROUP), jnp.float32),
+                pltpu.VMEM((1, pixels), jnp.float32),
+                pltpu.VMEM((rows * SUB, LANE), jnp.float32),
+                pltpu.VMEM((rows + SUB, LANE), jnp.float32),
+                pltpu.SemaphoreType.DMA((count,)),
+                pltpu.SemaphoreType.DMA,
+            ],
+            compiler_params=params(),
+            name=f"edges_{p}",
+        )(source, in_hbm(ref_weight.reshape(1, pixels)))
+        all_sums.append(sums)
+        edges.append(edge)
+    sums = sum(all_sums[1:], all_sums[0])
     next_edges = [lax.ppermute(edges[0], "tm", back)]
     sums = lax.psum(sums[:, 0], "pix")
     mean = sums[:rows] / sums[rows]

time: 96.3 us -> 94.5 us (0.981)
  waiting for transfers between devices: 27.2 us -> 23.7 us
    ppermute x1, waiting for transfers between devices: 12.9 us -> 10.5 us  [on_device(): next_mean = lax.ppermute(mean, 'tm', back)]
    ppermute x21, waiting for transfers between devices: 14.2 us -> 13.2 us  [swap(): return lax.ppermute(block, ('tm', 'pix'), route)]
    pallas_call x1 -> x2, Pallas kernels: 3.4 us -> 4.12 us  [on_device(): pl.pallas_call(functools.partial(edge_kernel, first), in_specs=[pl.BlockS...]
  transfers between devices with their start and end apart: 24 -> 24, of which waited for: 12 -> 10; matrix products, arithmetic and copies ran while one was open for 2% -> 2% of each run, Pallas kernels for 19% -> 22%
where the time goes in v5:
time: 94.5 us; the launch traced here: 94.2 us
  starting transfers between devices  41.6 us (44%)
  Pallas kernels  23.7 us (25%)
  waiting for transfers between devices  23.7 us (25%)
  blocking collectives  2.59 us (3%)
  other arithmetic  1.65 us (2%)
    ppermute x21, starting transfers between devices, swap(): return lax.ppermute(block, ('tm', 'pix'), route)  37.8 us
    ppermute x21, waiting for transfers between devices, swap(): return lax.ppermute(block, ('tm', 'pix'), route)  13.2 us
    pallas_call x3, Pallas kernels, inner(): pl.pallas_call(inner_kernel, grid=(count,), in_specs=[SMEM, pl.BlockSpec(...  13 us
    ppermute x1, waiting for transfers between devices, on_device(): next_mean = lax.ppermute(mean, 'tm', back)  10.5 us
    pallas_call x2, Pallas kernels, on_device(): pl.pallas_call(functools.partial(edge_kernel, first), in_specs=[pl.BlockS...  4.12 us
    pallas_call x3, Pallas kernels, border(): pl.pallas_call(functools.partial(border_kernel, first - spans[p > 0][0]),...  3.83 us
    pallas_call x3, Pallas kernels, on_device(): pl.pallas_call(functools.partial(finish_kernel, first, total_frames), in_...  2.8 us
    psum x1, blocking collectives, on_device(): sums = lax.psum(sums[:, 0], 'pix')  2.59 us
  transfers between devices with their start and end apart: 24, of which 10 were waited for; matrix products, arithmetic and copies ran while one was open for 2% of the time, Pallas kernels for 22%

profile of v5, /device:TPU:0, one launch (start us, length us, event | category | flops | bytes accessed | tf_op | source)
XLA Modules:
  0.0 94.2 jit_solution(17465909482846662766)
XLA Ops:
  0.0 1.7 %edges_0.1 = (f32[136,1]{1,0:T(8,128)S(1)}, f32[3,320,128]{2,1,0:T(8,128)S(1)}) custom-call(f32[128,8192]{1,0:T(8,128)} %x_ref.5, f32[1,8192]{1,0:T(1,128)} %bitcast.5), custom_call_target="tpu_custom_call" | custom-call | tf_op jit(solution)/shard_map/edges_0/pallas_call | solution.py:324
  3.0 2.4 %edges_1.1 = (f32[136,1]{1,0:T(8,128)S(1)}, f32[5,320,128]{2,1,0:T(8,128)S(1)}) custom-call(f32[128,8192]{1,0:T(8,128)} %x_ref.5, f32[1,8192]{1,0:T(1,128)} %bitcast.6), custom_call_target="tpu_custom_call" | custom-call | tf_op jit(solution)/shard_map/edges_1/pallas_call | solution.py:324
  5.5 2.6 %psum.7 = f32[136]{0:T(256)S(1)} all-reduce(f32[136]{0:T(256)S(1)} %add_reduce_fusion), channel_id=1, replica_groups=mesh['tm'=16,'pix'=2] {'pix'}, use_global_device_ids=true, to_apply=%region_0.1 | all-reduce | flops 136 | bytes 1088 | tf_op jit(solution)/shard_map/psum | solution.py:344
  11.9 4.7 %inner_0.1 = (f32[3,512,128]{2,1,0:T(8,128)S(1)}, f32[3,512,128]{2,1,0:T(8,128)S(1)}, f32[3,8,128]{2,1,0:T(8,128)S(1)}) custom-call(f32[128]{0:T(128)S(1)} %slice_divide_fusion.mean_ref, f32[128,8192]{1,0:T(8,128)} %x_ref.5), custom_call_target="tpu_custom_call" | custom-call | tf_op jit(solution)/shard_map/inner_0/pallas_call | solution.py:352
  16.6 4.7 %inner_1.1 = (f32[3,512,128]{2,1,0:T(8,128)S(1)}, f32[3,512,128]{2,1,0:T(8,128)S(1)}, f32[3,8,128]{2,1,0:T(8,128)S(1)}) custom-call(f32[128]{0:T(128)S(1)} %slice_divide_fusion.mean_ref, f32[128,8192]{1,0:T(8,128)} %x_ref.5), custom_call_target="tpu_custom_call" | custom-call | tf_op jit(solution)/shard_map/inner_1/pallas_call | solution.py:352
  21.4 3.5 %inner_2.1 = (f32[2,512,128]{2,1,0:T(8,128)S(1)}, f32[2,512,128]{2,1,0:T(8,128)S(1)}, f32[2,8,128]{2,1,0:T(8,128)S(1)}) custom-call(f32[128]{0:T(128)S(1)} %slice_divide_fusion.mean_ref, f32[128,8192]{1,0:T(8,128)} %x_ref.5), custom_call_target="tpu_custom_call" | custom-call | tf_op jit(solution)/shard_map/inner_2/pallas_call | solution.py:352
  24.9 10.5 %collective-permute-done.mean_ref = f32[128]{0:T(128)S(1)} collective-permute-done((f32[128]{0:T(128)S(1)}, f32[128]{0:T(128)S(1)}, u32[]{:S(2)}, u32[]{:S(2)}) %collective-permute-start) | collective-permute-done | bytes 544 | tf_op jit(solution)/shard_map/ppermute | solution.py:346
  35.4 1.4 %border_0.1 = (f32[3,256,128]{2,1,0:T(8,128)S(1)}, f32[3,264,128]{2,1,0:T(8,128)S(1)}) custom-call(f32[128]{0:T(128)S(1)} %collective-permute-done.mean_ref, s32[1]{0:T(128)} %bitcast.1.side_ref, f32[3,320,128]{2,1,0:T(8,128)S(1)} %collective-permute-done.2.edge_ref, f32[3,512,128]{2,1,0:T(8,128)S(1)} %get-tuple-element.76.last_ref, ...), custom_call_target="tpu_custom_call" | custom-call | tf_op jit(solution)/shard_map/border_0/pallas_call | solution.py:376
  36.8 1.8 %collective-permute-start.5 = (f32[3,264,128]{2,1,0:T(8,128)S(1)}, f32[3,264,128]{2,1,0:T(8,128)S(1)}, u32[]{:S(2)}, u32[]{:S(2)}) collective-permute-start(f32[3,264,128]{2,1,0:T(8,128)S(1)} %get-tuple-element.78), channel_id=1, source_target_pairs={{0,4},{1,3},{2,6},{3,1},{4,0},{5,7},{6,2},{7,5},{8,12},{9,11},{10,... | collective-permute-start | bytes 1216520 | tf_op jit(solution)/shard_map/ppermute | solution.py:238
  38.6 1.4 %border_1.1 = (f32[3,256,128]{2,1,0:T(8,128)S(1)}, f32[3,264,128]{2,1,0:T(8,128)S(1)}) custom-call(f32[128]{0:T(128)S(1)} %collective-permute-done.mean_ref, s32[1]{0:T(128)} %bitcast.side_ref, f32[5,320,128]{2,1,0:T(8,128)S(1)} %collective-permute-done.1.edge_ref, f32[3,512,128]{2,1,0:T(8,128)S(1)} %get-tuple-element.80.last_ref, ...), custom_call_target="tpu_custom_call" | custom-call | tf_op jit(solution)/shard_map/border_1/pallas_call | solution.py:376
  40.0 3.4 %collective-permute-start.4 = (f32[3,264,128]{2,1,0:T(8,128)S(1)}, f32[3,264,128]{2,1,0:T(8,128)S(1)}, u32[]{:S(2)}, u32[]{:S(2)}) collective-permute-start(f32[3,264,128]{2,1,0:T(8,128)S(1)} %get-tuple-element.82), channel_id=1, source_target_pairs={{0,2},{1,9},{2,0},{3,11},{4,6},{5,13},{6,4},{7,15},{8,10},{9,1},{1... | collective-permute-start | bytes 1216520 | tf_op jit(solution)/shard_map/ppermute | solution.py:238
  44.4 1.6 %collective-permute-start.3 = (f32[2,264,128]{2,1,0:T(8,128)S(1)}, f32[2,264,128]{2,1,0:T(8,128)S(1)}, u32[]{:S(2)}, u32[]{:S(2)}) collective-permute-start(f32[2,264,128]{2,1,0:T(8,128)S(1)} %get-tuple-element.87), channel_id=1, source_target_pairs={{0,8},{1,5},{2,10},{3,7},{4,12},{5,1},{6,14},{7,3},{8,0},{9,13},{1... | collective-permute-start | bytes 811016 | tf_op jit(solution)/shard_map/ppermute | solution.py:238
  46.2 1.8 %collective-permute-start.8 = (f32[3,136,128]{2,1,0:T(8,128)S(1)}, f32[3,136,128]{2,1,0:T(8,128)S(1)}, u32[]{:S(2)}, u32[]{:S(2)}) collective-permute-start(f32[3,136,128]{2,1,0:T(8,128)S(1)} %pad_maximum_fusion.3), channel_id=1, source_target_pairs={{0,8},{1,5},{2,10},{3,7},{4,12},{5,1},{6,14},{7,3},{8,0},{9,13},{1... | collective-permute-start | bytes 626696 | tf_op jit(solution)/shard_map/ppermute | solution.py:238
  51.0 4.5 %collective-permute-start.6 = (f32[2,136,128]{2,1,0:T(8,128)S(1)}, f32[2,136,128]{2,1,0:T(8,128)S(1)}, u32[]{:S(2)}, u32[]{:S(2)}) collective-permute-start(f32[2,136,128]{2,1,0:T(8,128)S(1)} %pad_maximum_fusion.7), channel_id=1, source_target_pairs={{0,2},{1,9},{2,0},{3,11},{4,6},{5,13},{6,4},{7,15},{8,10},{9,1},{1... | collective-permute-start | bytes 417800 | tf_op jit(solution)/shard_map/ppermute | solution.py:238
  55.6 3.0 %collective-permute-start.11 = (f32[3,72,128]{2,1,0:T(8,128)S(1)}, f32[3,72,128]{2,1,0:T(8,128)S(1)}, u32[]{:S(2)}, u32[]{:S(2)}) collective-permute-start(f32[3,72,128]{2,1,0:T(8,128)S(1)} %pad_maximum_fusion.9), channel_id=1, source_target_pairs={{0,2},{1,9},{2,0},{3,11},{4,6},{5,13},{6,4},{7,15},{8,10},{9,1},{1... | collective-permute-start | bytes 331784 | tf_op jit(solution)/shard_map/ppermute | solution.py:238
  60.2 2.4 %collective-permute-start.9 = (f32[2,72,128]{2,1,0:T(8,128)S(1)}, f32[2,72,128]{2,1,0:T(8,128)S(1)}, u32[]{:S(2)}, u32[]{:S(2)}) collective-permute-start(f32[2,72,128]{2,1,0:T(8,128)S(1)} %pad_maximum_fusion.13), channel_id=1, source_target_pairs={{0,4},{1,3},{2,6},{3,1},{4,0},{5,7},{6,2},{7,5},{8,12},{9,11},{10,... | collective-permute-start | bytes 221192 | tf_op jit(solution)/shard_map/ppermute | solution.py:238
  65.0 2.4 %collective-permute-start.13 = (f32[3,72,128]{2,1,0:T(8,128)S(1)}, f32[3,72,128]{2,1,0:T(8,128)S(1)}, u32[]{:S(2)}, u32[]{:S(2)}) collective-permute-start(f32[3,72,128]{2,1,0:T(8,128)S(1)} %pad_maximum_fusion.12), channel_id=1, source_target_pairs={{0,16},{1,17},{2,18},{3,19},{4,20},{5,21},{6,22},{7,23},{8,24},{9,... | collective-permute-start | bytes 331784 | tf_op jit(solution)/shard_map/ppermute | solution.py:238
  68.0 1.4 %collective-permute-done.14 = f32[3,72,128]{2,1,0:T(8,128)S(1)} collective-permute-done((f32[3,72,128]{2,1,0:T(8,128)S(1)}, f32[3,72,128]{2,1,0:T(8,128)S(1)}, u32[]{:S(2)}, u32[]{:S(2)}) %collective-permute-start.14) | collective-permute-done | bytes 110624 | tf_op jit(solution)/shard_map/ppermute | solution.py:238
  70.4 1.5 %collective-permute-done.13 = f32[3,72,128]{2,1,0:T(8,128)S(1)} collective-permute-done((f32[3,72,128]{2,1,0:T(8,128)S(1)}, f32[3,72,128]{2,1,0:T(8,128)S(1)}, u32[]{:S(2)}, u32[]{:S(2)}) %collective-permute-start.13) | collective-permute-done | bytes 110624 | tf_op jit(solution)/shard_map/ppermute | solution.py:238
  73.2 2.5 %collective-permute-start.15 = (f32[2,64,128]{2,1,0:T(8,128)S(1)}, f32[2,64,128]{2,1,0:T(8,128)S(1)}, u32[]{:S(2)}, u32[]{:S(2)}) collective-permute-start(f32[2,64,128]{2,1,0:T(8,128)S(1)} %slice_add_fusion.10), channel_id=1, source_target_pairs={{0,4},{1,3},{2,6},{3,1},{4,0},{5,7},{6,2},{7,5},{8,12},{9,11},{10,... | collective-permute-start | bytes 196616 | tf_op jit(solution)/shard_map/ppermute | solution.py:238
  77.1 2.5 %collective-permute-start.19 = (f32[3,128,128]{2,1,0:T(8,128)S(1)}, f32[3,128,128]{2,1,0:T(8,128)S(1)}, u32[]{:S(2)}, u32[]{:S(2)}) collective-permute-start(f32[3,128,128]{2,1,0:T(8,128)S(1)} %pad_maximum_fusion.6), channel_id=1, source_target_pairs={{0,4},{1,3},{2,6},{3,1},{4,0},{5,7},{6,2},{7,5},{8,12},{9,11},{10,... | collective-permute-start | bytes 589832 | tf_op jit(solution)/shard_map/ppermute | solution.py:238
  80.6 2.8 %collective-permute-done.20 = f32[3,128,128]{2,1,0:T(8,128)S(1)} collective-permute-done((f32[3,128,128]{2,1,0:T(8,128)S(1)}, f32[3,128,128]{2,1,0:T(8,128)S(1)}, u32[]{:S(2)}, u32[]{:S(2)}) %collective-permute-start.20) | collective-permute-done | bytes 196640 | tf_op jit(solution)/shard_map/ppermute | solution.py:238
  83.9 2.2 %collective-permute-start.22 = (f32[3,256,128]{2,1,0:T(8,128)S(1)}, f32[3,256,128]{2,1,0:T(8,128)S(1)}, u32[]{:S(2)}, u32[]{:S(2)}) collective-permute-start(f32[3,256,128]{2,1,0:T(8,128)S(1)} %pad_maximum_fusion.1.mine_ref), channel_id=1, source_target_pairs={{0,2},{1,9},{2,0},{3,11},{4,6},{5,13},{6,4},{7,15},{8,10},{9,1},{1... | collective-permute-start | bytes 1179656 | tf_op jit(solution)/shard_map/ppermute | solution.py:238
  86.8 4.6 %collective-permute-done.23.got_ref = f32[3,256,128]{2,1,0:T(8,128)S(1)} collective-permute-done((f32[3,256,128]{2,1,0:T(8,128)S(1)}, f32[3,256,128]{2,1,0:T(8,128)S(1)}, u32[]{:S(2)}, u32[]{:S(2)}) %collective-permute-start.23) | collective-permute-done | bytes 393248 | tf_op jit(solution)/shard_map/ppermute | solution.py:238
  (90 shorter events, 22.7 us)
Async XLA Ops:
  1.7 23.2 %collective-permute-start.2 = (f32[3,320,128]{2,1,0:T(8,128)S(1)}, f32[3,320,128]{2,1,0:T(8,128)S(1)}, u32[]{:S(2)}, u32[]{:S(2)}) collective-permute-start(f32[3,320,128]{2,1,0:T(8,128)S(1)} %get-tuple-element.68), channel_id=1, source_target_pairs={{2,0},{4,2},{6,4},{8,6},{10,8},{12,10},{14,12},{16,14},{18,16},{20... | collective-permute-start | bytes 1474568 | tf_op jit(solution)/shard_map/ppermute | solution.py:343
  9.3 29.3 %collective-permute-start.1 = (f32[5,320,128]{2,1,0:T(8,128)S(1)}, f32[5,320,128]{2,1,0:T(8,128)S(1)}, u32[]{:S(2)}, u32[]{:S(2)}) collective-permute-start(f32[5,320,128]{2,1,0:T(8,128)S(1)} %get-tuple-element.65), channel_id=1, source_target_pairs={{2,0},{4,2},{6,4},{8,6},{10,8},{12,10},{14,12},{16,14},{18,16},{20... | collective-permute-start | bytes 2457608 | tf_op jit(solution)/shard_map/ppermute | solution.py:348
  10.6 24.8 %collective-permute-start = (f32[128]{0:T(128)S(1)}, f32[128]{0:T(128)S(1)}, u32[]{:S(2)}, u32[]{:S(2)}) collective-permute-start(f32[128]{0:T(128)S(1)} %slice_divide_fusion.mean_ref), channel_id=1, source_target_pairs={{2,0},{4,2},{6,4},{8,6},{10,8},{12,10},{14,12},{16,14},{18,16},{20... | collective-permute-start | bytes 1544 | tf_op jit(solution)/shard_map/ppermute | solution.py:346
  36.8 9.3 %collective-permute-start.5 = (f32[3,264,128]{2,1,0:T(8,128)S(1)}, f32[3,264,128]{2,1,0:T(8,128)S(1)}, u32[]{:S(2)}, u32[]{:S(2)}) collective-permute-start(f32[3,264,128]{2,1,0:T(8,128)S(1)} %get-tuple-element.78), channel_id=1, source_target_pairs={{0,4},{1,3},{2,6},{3,1},{4,0},{5,7},{6,2},{7,5},{8,12},{9,11},{10,... | collective-permute-start | bytes 1216520 | tf_op jit(solution)/shard_map/ppermute | solution.py:238
  40.0 9.2 %collective-permute-start.4 = (f32[3,264,128]{2,1,0:T(8,128)S(1)}, f32[3,264,128]{2,1,0:T(8,128)S(1)}, u32[]{:S(2)}, u32[]{:S(2)}) collective-permute-start(f32[3,264,128]{2,1,0:T(8,128)S(1)} %get-tuple-element.82), channel_id=1, source_target_pairs={{0,2},{1,9},{2,0},{3,11},{4,6},{5,13},{6,4},{7,15},{8,10},{9,1},{1... | collective-permute-start | bytes 1216520 | tf_op jit(solution)/shard_map/ppermute | solution.py:238
  44.4 6.5 %collective-permute-start.3 = (f32[2,264,128]{2,1,0:T(8,128)S(1)}, f32[2,264,128]{2,1,0:T(8,128)S(1)}, u32[]{:S(2)}, u32[]{:S(2)}) collective-permute-start(f32[2,264,128]{2,1,0:T(8,128)S(1)} %get-tuple-element.87), channel_id=1, source_target_pairs={{0,8},{1,5},{2,10},{3,7},{4,12},{5,1},{6,14},{7,3},{8,0},{9,13},{1... | collective-permute-start | bytes 811016 | tf_op jit(solution)/shard_map/ppermute | solution.py:238
  46.2 9.3 %collective-permute-start.8 = (f32[3,136,128]{2,1,0:T(8,128)S(1)}, f32[3,136,128]{2,1,0:T(8,128)S(1)}, u32[]{:S(2)}, u32[]{:S(2)}) collective-permute-start(f32[3,136,128]{2,1,0:T(8,128)S(1)} %pad_maximum_fusion.3), channel_id=1, source_target_pairs={{0,8},{1,5},{2,10},{3,7},{4,12},{5,1},{6,14},{7,3},{8,0},{9,13},{1... | collective-permute-start | bytes 626696 | tf_op jit(solution)/shard_map/ppermute | solution.py:238
  49.3 9.3 %collective-permute-start.7 = (f32[3,136,128]{2,1,0:T(8,128)S(1)}, f32[3,136,128]{2,1,0:T(8,128)S(1)}, u32[]{:S(2)}, u32[]{:S(2)}) collective-permute-start(f32[3,136,128]{2,1,0:T(8,128)S(1)} %pad_maximum_fusion.4), channel_id=1, source_target_pairs={{0,4},{1,3},{2,6},{3,1},{4,0},{5,7},{6,2},{7,5},{8,12},{9,11},{10,... | collective-permute-start | bytes 626696 | tf_op jit(solution)/shard_map/ppermute | solution.py:238
  51.0 7.9 %collective-permute-start.6 = (f32[2,136,128]{2,1,0:T(8,128)S(1)}, f32[2,136,128]{2,1,0:T(8,128)S(1)}, u32[]{:S(2)}, u32[]{:S(2)}) collective-permute-start(f32[2,136,128]{2,1,0:T(8,128)S(1)} %pad_maximum_fusion.7), channel_id=1, source_target_pairs={{0,2},{1,9},{2,0},{3,11},{4,6},{5,13},{6,4},{7,15},{8,10},{9,1},{1... | collective-permute-start | bytes 417800 | tf_op jit(solution)/shard_map/ppermute | solution.py:238
  55.6 7.0 %collective-permute-start.11 = (f32[3,72,128]{2,1,0:T(8,128)S(1)}, f32[3,72,128]{2,1,0:T(8,128)S(1)}, u32[]{:S(2)}, u32[]{:S(2)}) collective-permute-start(f32[3,72,128]{2,1,0:T(8,128)S(1)} %pad_maximum_fusion.9), channel_id=1, source_target_pairs={{0,2},{1,9},{2,0},{3,11},{4,6},{5,13},{6,4},{7,15},{8,10},{9,1},{1... | collective-permute-start | bytes 331784 | tf_op jit(solution)/shard_map/ppermute | solution.py:238
  59.0 5.5 %collective-permute-start.10 = (f32[3,72,128]{2,1,0:T(8,128)S(1)}, f32[3,72,128]{2,1,0:T(8,128)S(1)}, u32[]{:S(2)}, u32[]{:S(2)}) collective-permute-start(f32[3,72,128]{2,1,0:T(8,128)S(1)} %pad_maximum_fusion.10), channel_id=1, source_target_pairs={{0,8},{1,5},{2,10},{3,7},{4,12},{5,1},{6,14},{7,3},{8,0},{9,13},{1... | collective-permute-start | bytes 331784 | tf_op jit(solution)/shard_map/ppermute | solution.py:238
  60.2 4.7 %collective-permute-start.9 = (f32[2,72,128]{2,1,0:T(8,128)S(1)}, f32[2,72,128]{2,1,0:T(8,128)S(1)}, u32[]{:S(2)}, u32[]{:S(2)}) collective-permute-start(f32[2,72,128]{2,1,0:T(8,128)S(1)} %pad_maximum_fusion.13), channel_id=1, source_target_pairs={{0,4},{1,3},{2,6},{3,1},{4,0},{5,7},{6,2},{7,5},{8,12},{9,11},{10,... | collective-permute-start | bytes 221192 | tf_op jit(solution)/shard_map/ppermute | solution.py:238
  62.7 6.7 %collective-permute-start.14 = (f32[3,72,128]{2,1,0:T(8,128)S(1)}, f32[3,72,128]{2,1,0:T(8,128)S(1)}, u32[]{:S(2)}, u32[]{:S(2)}) collective-permute-start(f32[3,72,128]{2,1,0:T(8,128)S(1)} %pad_maximum_fusion.11), channel_id=1, source_target_pairs={{0,16},{1,17},{2,18},{3,19},{4,20},{5,21},{6,22},{7,23},{8,24},{9,... | collective-permute-start | bytes 331784 | tf_op jit(solution)/shard_map/ppermute | solution.py:238
  65.0 6.9 %collective-permute-start.13 = (f32[3,72,128]{2,1,0:T(8,128)S(1)}, f32[3,72,128]{2,1,0:T(8,128)S(1)}, u32[]{:S(2)}, u32[]{:S(2)}) collective-permute-start(f32[3,72,128]{2,1,0:T(8,128)S(1)} %pad_maximum_fusion.12), channel_id=1, source_target_pairs={{0,16},{1,17},{2,18},{3,19},{4,20},{5,21},{6,22},{7,23},{8,24},{9,... | collective-permute-start | bytes 331784 | tf_op jit(solution)/shard_map/ppermute | solution.py:238
  67.4 5.8 %collective-permute-start.12 = (f32[2,72,128]{2,1,0:T(8,128)S(1)}, f32[2,72,128]{2,1,0:T(8,128)S(1)}, u32[]{:S(2)}, u32[]{:S(2)}) collective-permute-start(f32[2,72,128]{2,1,0:T(8,128)S(1)} %pad_maximum_fusion.14), channel_id=1, source_target_pairs={{0,16},{1,17},{2,18},{3,19},{4,20},{5,21},{6,22},{7,23},{8,24},{9,... | collective-permute-start | bytes 221192 | tf_op jit(solution)/shard_map/ppermute | solution.py:238
  69.4 6.2 %collective-permute-start.17 = (f32[3,64,128]{2,1,0:T(8,128)S(1)}, f32[3,64,128]{2,1,0:T(8,128)S(1)}, u32[]{:S(2)}, u32[]{:S(2)}) collective-permute-start(f32[3,64,128]{2,1,0:T(8,128)S(1)} %slice_add_fusion.7), channel_id=1, source_target_pairs={{0,2},{1,9},{2,0},{3,11},{4,6},{5,13},{6,4},{7,15},{8,10},{9,1},{1... | collective-permute-start | bytes 294920 | tf_op jit(solution)/shard_map/ppermute | solution.py:238
  71.9 5.1 %collective-permute-start.16 = (f32[3,64,128]{2,1,0:T(8,128)S(1)}, f32[3,64,128]{2,1,0:T(8,128)S(1)}, u32[]{:S(2)}, u32[]{:S(2)}) collective-permute-start(f32[3,64,128]{2,1,0:T(8,128)S(1)} %slice_add_fusion.6), channel_id=1, source_target_pairs={{0,8},{1,5},{2,10},{3,7},{4,12},{5,1},{6,14},{7,3},{8,0},{9,13},{1... | collective-permute-start | bytes 294920 | tf_op jit(solution)/shard_map/ppermute | solution.py:238
  73.2 6.3 %collective-permute-start.15 = (f32[2,64,128]{2,1,0:T(8,128)S(1)}, f32[2,64,128]{2,1,0:T(8,128)S(1)}, u32[]{:S(2)}, u32[]{:S(2)}) collective-permute-start(f32[2,64,128]{2,1,0:T(8,128)S(1)} %slice_add_fusion.10), channel_id=1, source_target_pairs={{0,4},{1,3},{2,6},{3,1},{4,0},{5,7},{6,2},{7,5},{8,12},{9,11},{10,... | collective-permute-start | bytes 196616 | tf_op jit(solution)/shard_map/ppermute | solution.py:238
  75.7 7.8 %collective-permute-start.20 = (f32[3,128,128]{2,1,0:T(8,128)S(1)}, f32[3,128,128]{2,1,0:T(8,128)S(1)}, u32[]{:S(2)}, u32[]{:S(2)}) collective-permute-start(f32[3,128,128]{2,1,0:T(8,128)S(1)} %pad_maximum_fusion.5), channel_id=1, source_target_pairs={{0,8},{1,5},{2,10},{3,7},{4,12},{5,1},{6,14},{7,3},{8,0},{9,13},{1... | collective-permute-start | bytes 589832 | tf_op jit(solution)/shard_map/ppermute | solution.py:238
  77.1 6.8 %collective-permute-start.19 = (f32[3,128,128]{2,1,0:T(8,128)S(1)}, f32[3,128,128]{2,1,0:T(8,128)S(1)}, u32[]{:S(2)}, u32[]{:S(2)}) collective-permute-start(f32[3,128,128]{2,1,0:T(8,128)S(1)} %pad_maximum_fusion.6), channel_id=1, source_target_pairs={{0,4},{1,3},{2,6},{3,1},{4,0},{5,7},{6,2},{7,5},{8,12},{9,11},{10,... | collective-permute-start | bytes 589832 | tf_op jit(solution)/shard_map/ppermute | solution.py:238
  79.6 6.6 %collective-permute-start.18 = (f32[2,128,128]{2,1,0:T(8,128)S(1)}, f32[2,128,128]{2,1,0:T(8,128)S(1)}, u32[]{:S(2)}, u32[]{:S(2)}) collective-permute-start(f32[2,128,128]{2,1,0:T(8,128)S(1)} %pad_maximum_fusion.8), channel_id=1, source_target_pairs={{0,2},{1,9},{2,0},{3,11},{4,6},{5,13},{6,4},{7,15},{8,10},{9,1},{1... | collective-permute-start | bytes 393224 | tf_op jit(solution)/shard_map/ppermute | solution.py:238
  83.5 7.8 %collective-permute-start.23 = (f32[3,256,128]{2,1,0:T(8,128)S(1)}, f32[3,256,128]{2,1,0:T(8,128)S(1)}, u32[]{:S(2)}, u32[]{:S(2)}) collective-permute-start(f32[3,256,128]{2,1,0:T(8,128)S(1)} %pad_maximum_fusion.mine_ref), channel_id=1, source_target_pairs={{0,4},{1,3},{2,6},{3,1},{4,0},{5,7},{6,2},{7,5},{8,12},{9,11},{10,... | collective-permute-start | bytes 1179656 | tf_op jit(solution)/shard_map/ppermute | solution.py:238
  83.9 8.4 %collective-permute-start.22 = (f32[3,256,128]{2,1,0:T(8,128)S(1)}, f32[3,256,128]{2,1,0:T(8,128)S(1)}, u32[]{:S(2)}, u32[]{:S(2)}) collective-permute-start(f32[3,256,128]{2,1,0:T(8,128)S(1)} %pad_maximum_fusion.1.mine_ref), channel_id=1, source_target_pairs={{0,2},{1,9},{2,0},{3,11},{4,6},{5,13},{6,4},{7,15},{8,10},{9,1},{1... | collective-permute-start | bytes 1179656 | tf_op jit(solution)/shard_map/ppermute | solution.py:238
  86.2 7.1 %collective-permute-start.21 = (f32[2,256,128]{2,1,0:T(8,128)S(1)}, f32[2,256,128]{2,1,0:T(8,128)S(1)}, u32[]{:S(2)}, u32[]{:S(2)}) collective-permute-start(f32[2,256,128]{2,1,0:T(8,128)S(1)} %pad_maximum_fusion.2.mine_ref), channel_id=1, source_target_pairs={{0,8},{1,5},{2,10},{3,7},{4,12},{5,1},{6,14},{7,3},{8,0},{9,13},{1... | collective-permute-start | bytes 786440 | tf_op jit(solution)/shard_map/ppermute | solution.py:238

commit v6 on v5

--- a/solution.py
+++ b/solution.py
@@ -315,8 +315,9 @@
     sides = {o[0]: uppers[o[0]].astype(jnp.int32).reshape(1) for _, _, o in parts}
     ref_weight, uppers, sides = lax.optimization_barrier((ref_weight, uppers, sides))
     stored = in_hbm(frames)
-    head = parts[0][1]
-    spans = [(0, head), (head, groups - head)]
+    cut = parts[-1][0]
+    spans = [(cut, groups - cut), (0, cut)]
+    span_of = [1] * (len(parts) - 1) + [0]
     back = [(i, i - 1) for i in range(1, size)]
     all_sums, edges = [], []
     for p, (first, count) in enumerate(spans):
@@ -374,7 +375,7 @@
         first, count, order = parts[p]
         totals, last, pixel_sum = sums
         kept, sent = pl.pallas_call(
-            functools.partial(border_kernel, first - spans[p > 0][0]),
+            functools.partial(border_kernel, first - spans[span_of[p]][0]),
             in_specs=[SMEM, SMEM] + [VMEM] * 4,
             out_specs=[VMEM, VMEM],
             out_shape=[
@@ -384,7 +385,7 @@
             scratch_shapes=[pltpu.SMEM((EDGE_ROWS,), jnp.float32)],
             compiler_params=params(),
             name=f"border_{p}",
-        )(next_mean, sides[order[0]], after(next_edges[p > 0], token), last, totals, pixel_sum)
+        )(next_mean, sides[order[0]], after(next_edges[span_of[p]], token), last, totals, pixel_sum)
         return Part(order, uppers, kept, sent)
 
     sums = []

time: 94.5 us -> 107 us (1.13)
  waiting for transfers between devices: 23.7 us -> 42.8 us
  starting transfers between devices: 41.6 us -> 34.8 us
    ppermute x21, waiting for transfers between devices: 13.2 us -> 25.8 us  [swap(): return lax.ppermute(block, ('tm', 'pix'), route)]
    ppermute x1, waiting for transfers between devices: 0.01 us -> 11.2 us  [on_device(): next_edges.append(lax.ppermute(after(edge, mean), 'tm', back))]
    ppermute x1, waiting for transfers between devices: 10.5 us -> 0.06 us  [on_device(): next_mean = lax.ppermute(mean, 'tm', back)]
    ppermute x21, starting transfers between devices: 37.8 us -> 30.9 us  [swap(): return lax.ppermute(block, ('tm', 'pix'), route)]
    ppermute x1, waiting for transfers between devices: 0.01 us -> 5.72 us  [on_device(): next_edges = [lax.ppermute(edges[0], 'tm', back)]]
  transfers between devices with their start and end apart: 24 -> 24, of which waited for: 10 -> 17; matrix products, arithmetic and copies ran while one was open for 2% -> 1% of each run, Pallas kernels for 22% -> 16%
where the time goes in v6:
time: 107 us
  waiting for transfers between devices  42.8 us (40%)
  starting transfers between devices  34.8 us (33%)
  Pallas kernels  23.8 us (22%)
  blocking collectives  2.59 us (2%)
  other arithmetic  1.63 us (2%)
    ppermute x21, starting transfers between devices, swap(): return lax.ppermute(block, ('tm', 'pix'), route)  30.9 us
    ppermute x21, waiting for transfers between devices, swap(): return lax.ppermute(block, ('tm', 'pix'), route)  25.8 us
    pallas_call x3, Pallas kernels, inner(): pl.pallas_call(inner_kernel, grid=(count,), in_specs=[SMEM, pl.BlockSpec(...  13 us
    ppermute x1, waiting for transfers between devices, on_device(): next_edges.append(lax.ppermute(after(edge, mean), 'tm', back))  11.2 us
    ppermute x1, waiting for transfers between devices, on_device(): next_edges = [lax.ppermute(edges[0], 'tm', back)]  5.72 us
    pallas_call x2, Pallas kernels, on_device(): pl.pallas_call(functools.partial(edge_kernel, first), in_specs=[pl.BlockS...  4.2 us
    pallas_call x3, Pallas kernels, border(): pl.pallas_call(functools.partial(border_kernel, first - spans[span_of[p]]...  3.84 us
    pallas_call x3, Pallas kernels, on_device(): pl.pallas_call(functools.partial(finish_kernel, first, total_frames), in_...  2.8 us
  transfers between devices with their start and end apart: 24, of which 17 were waited for; matrix products, arithmetic and copies ran while one was open for 1% of the time, Pallas kernels for 16%

profile of v6, /device:TPU:0, one launch (start us, length us, event | category | flops | bytes accessed | tf_op | source)
XLA Modules:
  0.0 106.6 jit_solution(11128058216277361884)
XLA Ops:
  1.5 2.7 %edges_1.1 = (f32[136,1]{1,0:T(8,128)S(1)}, f32[6,320,128]{2,1,0:T(8,128)S(1)}) custom-call(f32[128,8192]{1,0:T(8,128)} %x_ref.5, f32[1,8192]{1,0:T(1,128)} %bitcast.6), custom_call_target="tpu_custom_call" | custom-call | tf_op jit(solution)/shard_map/edges_1/pallas_call | solution.py:325
  4.3 2.6 %psum.7 = f32[136]{0:T(256)S(1)} all-reduce(f32[136]{0:T(256)S(1)} %add_reduce_fusion), channel_id=1, replica_groups=mesh['tm'=16,'pix'=2] {'pix'}, use_global_device_ids=true, to_apply=%region_0.1 | all-reduce | flops 136 | bytes 1088 | tf_op jit(solution)/shard_map/psum | solution.py:345
  10.7 4.7 %inner_0.1 = (f32[3,512,128]{2,1,0:T(8,128)S(1)}, f32[3,512,128]{2,1,0:T(8,128)S(1)}, f32[3,8,128]{2,1,0:T(8,128)S(1)}) custom-call(f32[128]{0:T(128)S(1)} %slice_divide_fusion.mean_ref, f32[128,8192]{1,0:T(8,128)} %x_ref.5), custom_call_target="tpu_custom_call" | custom-call | tf_op jit(solution)/shard_map/inner_0/pallas_call | solution.py:353
  15.4 4.7 %inner_1.1 = (f32[3,512,128]{2,1,0:T(8,128)S(1)}, f32[3,512,128]{2,1,0:T(8,128)S(1)}, f32[3,8,128]{2,1,0:T(8,128)S(1)}) custom-call(f32[128]{0:T(128)S(1)} %slice_divide_fusion.mean_ref, f32[128,8192]{1,0:T(8,128)} %x_ref.5), custom_call_target="tpu_custom_call" | custom-call | tf_op jit(solution)/shard_map/inner_1/pallas_call | solution.py:353
  20.1 3.5 %inner_2.1 = (f32[2,512,128]{2,1,0:T(8,128)S(1)}, f32[2,512,128]{2,1,0:T(8,128)S(1)}, f32[2,8,128]{2,1,0:T(8,128)S(1)}) custom-call(f32[128]{0:T(128)S(1)} %slice_divide_fusion.mean_ref, f32[128,8192]{1,0:T(8,128)} %x_ref.5), custom_call_target="tpu_custom_call" | custom-call | tf_op jit(solution)/shard_map/inner_2/pallas_call | solution.py:353
  23.7 11.2 %collective-permute-done.2.edge_ref = f32[6,320,128]{2,1,0:T(8,128)S(1)} collective-permute-done((f32[6,320,128]{2,1,0:T(8,128)S(1)}, f32[6,320,128]{2,1,0:T(8,128)S(1)}, u32[]{:S(2)}, u32[]{:S(2)}) %collective-permute-start.2) | collective-permute-done | bytes 983072 | tf_op jit(solution)/shard_map/ppermute | solution.py:349
  36.3 1.8 %collective-permute-start.5 = (f32[3,264,128]{2,1,0:T(8,128)S(1)}, f32[3,264,128]{2,1,0:T(8,128)S(1)}, u32[]{:S(2)}, u32[]{:S(2)}) collective-permute-start(f32[3,264,128]{2,1,0:T(8,128)S(1)} %get-tuple-element.78), channel_id=1, source_target_pairs={{0,4},{1,3},{2,6},{3,1},{4,0},{5,7},{6,2},{7,5},{8,12},{9,11},{10,... | collective-permute-start | bytes 1216520 | tf_op jit(solution)/shard_map/ppermute | solution.py:238
  40.8 4.0 %collective-permute-start.4 = (f32[3,264,128]{2,1,0:T(8,128)S(1)}, f32[3,264,128]{2,1,0:T(8,128)S(1)}, u32[]{:S(2)}, u32[]{:S(2)}) collective-permute-start(f32[3,264,128]{2,1,0:T(8,128)S(1)} %get-tuple-element.82), channel_id=1, source_target_pairs={{0,2},{1,9},{2,0},{3,11},{4,6},{5,13},{6,4},{7,15},{8,10},{9,1},{1... | collective-permute-start | bytes 1216520 | tf_op jit(solution)/shard_map/ppermute | solution.py:238
  44.8 5.7 %collective-permute-done.1.edge_ref = f32[2,320,128]{2,1,0:T(8,128)S(1)} collective-permute-done((f32[2,320,128]{2,1,0:T(8,128)S(1)}, f32[2,320,128]{2,1,0:T(8,128)S(1)}, u32[]{:S(2)}, u32[]{:S(2)}) %collective-permute-start.1) | collective-permute-done | bytes 327712 | tf_op jit(solution)/shard_map/ppermute | solution.py:344
  51.7 2.1 %collective-permute-start.3 = (f32[2,264,128]{2,1,0:T(8,128)S(1)}, f32[2,264,128]{2,1,0:T(8,128)S(1)}, u32[]{:S(2)}, u32[]{:S(2)}) collective-permute-start(f32[2,264,128]{2,1,0:T(8,128)S(1)} %get-tuple-element.87), channel_id=1, source_target_pairs={{0,8},{1,5},{2,10},{3,7},{4,12},{5,1},{6,14},{7,3},{8,0},{9,13},{1... | collective-permute-start | bytes 811016 | tf_op jit(solution)/shard_map/ppermute | solution.py:238
  55.0 2.5 %collective-permute-start.7 = (f32[3,136,128]{2,1,0:T(8,128)S(1)}, f32[3,136,128]{2,1,0:T(8,128)S(1)}, u32[]{:S(2)}, u32[]{:S(2)}) collective-permute-start(f32[3,136,128]{2,1,0:T(8,128)S(1)} %pad_maximum_fusion.4), channel_id=1, source_target_pairs={{0,4},{1,3},{2,6},{3,1},{4,0},{5,7},{6,2},{7,5},{8,12},{9,11},{10,... | collective-permute-start | bytes 626696 | tf_op jit(solution)/shard_map/ppermute | solution.py:238
  58.5 3.5 %collective-permute-start.6 = (f32[2,136,128]{2,1,0:T(8,128)S(1)}, f32[2,136,128]{2,1,0:T(8,128)S(1)}, u32[]{:S(2)}, u32[]{:S(2)}) collective-permute-start(f32[2,136,128]{2,1,0:T(8,128)S(1)} %pad_maximum_fusion.7), channel_id=1, source_target_pairs={{0,2},{1,9},{2,0},{3,11},{4,6},{5,13},{6,4},{7,15},{8,10},{9,1},{1... | collective-permute-start | bytes 417800 | tf_op jit(solution)/shard_map/ppermute | solution.py:238
  65.1 1.6 %collective-permute-start.10 = (f32[3,72,128]{2,1,0:T(8,128)S(1)}, f32[3,72,128]{2,1,0:T(8,128)S(1)}, u32[]{:S(2)}, u32[]{:S(2)}) collective-permute-start(f32[3,72,128]{2,1,0:T(8,128)S(1)} %pad_maximum_fusion.10), channel_id=1, source_target_pairs={{0,8},{1,5},{2,10},{3,7},{4,12},{5,1},{6,14},{7,3},{8,0},{9,13},{1... | collective-permute-start | bytes 331784 | tf_op jit(solution)/shard_map/ppermute | solution.py:238
  66.7 2.0 %collective-permute-start.11 = (f32[3,72,128]{2,1,0:T(8,128)S(1)}, f32[3,72,128]{2,1,0:T(8,128)S(1)}, u32[]{:S(2)}, u32[]{:S(2)}) collective-permute-start(f32[3,72,128]{2,1,0:T(8,128)S(1)} %pad_maximum_fusion.9), channel_id=1, source_target_pairs={{0,2},{1,9},{2,0},{3,11},{4,6},{5,13},{6,4},{7,15},{8,10},{9,1},{1... | collective-permute-start | bytes 331784 | tf_op jit(solution)/shard_map/ppermute | solution.py:238
  69.3 2.2 %collective-permute-done.11 = f32[3,72,128]{2,1,0:T(8,128)S(1)} collective-permute-done((f32[3,72,128]{2,1,0:T(8,128)S(1)}, f32[3,72,128]{2,1,0:T(8,128)S(1)}, u32[]{:S(2)}, u32[]{:S(2)}) %collective-permute-start.11) | collective-permute-done | bytes 110624 | tf_op jit(solution)/shard_map/ppermute | solution.py:238
  71.6 1.6 %collective-permute-done.9 = f32[2,72,128]{2,1,0:T(8,128)S(1)} collective-permute-done((f32[2,72,128]{2,1,0:T(8,128)S(1)}, f32[2,72,128]{2,1,0:T(8,128)S(1)}, u32[]{:S(2)}, u32[]{:S(2)}) %collective-permute-start.9) | collective-permute-done | bytes 73760 | tf_op jit(solution)/shard_map/ppermute | solution.py:238
  74.5 1.8 %collective-permute-start.14 = (f32[3,72,128]{2,1,0:T(8,128)S(1)}, f32[3,72,128]{2,1,0:T(8,128)S(1)}, u32[]{:S(2)}, u32[]{:S(2)}) collective-permute-start(f32[3,72,128]{2,1,0:T(8,128)S(1)} %pad_maximum_fusion.11), channel_id=1, source_target_pairs={{0,16},{1,17},{2,18},{3,19},{4,20},{5,21},{6,22},{7,23},{8,24},{9,... | collective-permute-start | bytes 331784 | tf_op jit(solution)/shard_map/ppermute | solution.py:238
  77.4 7.8 %collective-permute-done.14 = f32[3,72,128]{2,1,0:T(8,128)S(1)} collective-permute-done((f32[3,72,128]{2,1,0:T(8,128)S(1)}, f32[3,72,128]{2,1,0:T(8,128)S(1)}, u32[]{:S(2)}, u32[]{:S(2)}) %collective-permute-start.14) | collective-permute-done | bytes 110624 | tf_op jit(solution)/shard_map/ppermute | solution.py:238
  86.2 1.7 %collective-permute-start.15 = (f32[2,64,128]{2,1,0:T(8,128)S(1)}, f32[2,64,128]{2,1,0:T(8,128)S(1)}, u32[]{:S(2)}, u32[]{:S(2)}) collective-permute-start(f32[2,64,128]{2,1,0:T(8,128)S(1)} %slice_add_fusion.10), channel_id=1, source_target_pairs={{0,4},{1,3},{2,6},{3,1},{4,0},{5,7},{6,2},{7,5},{8,12},{9,11},{10,... | collective-permute-start | bytes 196616 | tf_op jit(solution)/shard_map/ppermute | solution.py:238
  87.9 2.0 %collective-permute-done.17 = f32[3,64,128]{2,1,0:T(8,128)S(1)} collective-permute-done((f32[3,64,128]{2,1,0:T(8,128)S(1)}, f32[3,64,128]{2,1,0:T(8,128)S(1)}, u32[]{:S(2)}, u32[]{:S(2)}) %collective-permute-start.17) | collective-permute-done | bytes 98336 | tf_op jit(solution)/shard_map/ppermute | solution.py:238
  90.8 1.8 %collective-permute-start.19 = (f32[3,128,128]{2,1,0:T(8,128)S(1)}, f32[3,128,128]{2,1,0:T(8,128)S(1)}, u32[]{:S(2)}, u32[]{:S(2)}) collective-permute-start(f32[3,128,128]{2,1,0:T(8,128)S(1)} %pad_maximum_fusion.6), channel_id=1, source_target_pairs={{0,4},{1,3},{2,6},{3,1},{4,0},{5,7},{6,2},{7,5},{8,12},{9,11},{10,... | collective-permute-start | bytes 589832 | tf_op jit(solution)/shard_map/ppermute | solution.py:238
  93.0 2.7 %collective-permute-done.20 = f32[3,128,128]{2,1,0:T(8,128)S(1)} collective-permute-done((f32[3,128,128]{2,1,0:T(8,128)S(1)}, f32[3,128,128]{2,1,0:T(8,128)S(1)}, u32[]{:S(2)}, u32[]{:S(2)}) %collective-permute-start.20) | collective-permute-done | bytes 196640 | tf_op jit(solution)/shard_map/ppermute | solution.py:238
  96.8 2.2 %collective-permute-start.22 = (f32[3,256,128]{2,1,0:T(8,128)S(1)}, f32[3,256,128]{2,1,0:T(8,128)S(1)}, u32[]{:S(2)}, u32[]{:S(2)}) collective-permute-start(f32[3,256,128]{2,1,0:T(8,128)S(1)} %pad_maximum_fusion.1.mine_ref), channel_id=1, source_target_pairs={{0,2},{1,9},{2,0},{3,11},{4,6},{5,13},{6,4},{7,15},{8,10},{9,1},{1... | collective-permute-start | bytes 1179656 | tf_op jit(solution)/shard_map/ppermute | solution.py:238
  99.6 4.0 %collective-permute-done.23.got_ref = f32[3,256,128]{2,1,0:T(8,128)S(1)} collective-permute-done((f32[3,256,128]{2,1,0:T(8,128)S(1)}, f32[3,256,128]{2,1,0:T(8,128)S(1)}, u32[]{:S(2)}, u32[]{:S(2)}) %collective-permute-start.23) | collective-permute-done | bytes 393248 | tf_op jit(solution)/shard_map/ppermute | solution.py:238
  (90 shorter events, 25.9 us)
Async XLA Ops:
  8.1 26.8 %collective-permute-start.2 = (f32[6,320,128]{2,1,0:T(8,128)S(1)}, f32[6,320,128]{2,1,0:T(8,128)S(1)}, u32[]{:S(2)}, u32[]{:S(2)}) collective-permute-start(f32[6,320,128]{2,1,0:T(8,128)S(1)} %get-tuple-element.67), channel_id=1, source_target_pairs={{2,0},{4,2},{6,4},{8,6},{10,8},{12,10},{14,12},{16,14},{18,16},{20... | collective-permute-start | bytes 2949128 | tf_op jit(solution)/shard_map/ppermute | solution.py:349
  9.4 25.6 %collective-permute-start = (f32[128]{0:T(128)S(1)}, f32[128]{0:T(128)S(1)}, u32[]{:S(2)}, u32[]{:S(2)}) collective-permute-start(f32[128]{0:T(128)S(1)} %slice_divide_fusion.mean_ref), channel_id=1, source_target_pairs={{2,0},{4,2},{6,4},{8,6},{10,8},{12,10},{14,12},{16,14},{18,16},{20... | collective-permute-start | bytes 1544 | tf_op jit(solution)/shard_map/ppermute | solution.py:347
  36.3 17.4 %collective-permute-start.5 = (f32[3,264,128]{2,1,0:T(8,128)S(1)}, f32[3,264,128]{2,1,0:T(8,128)S(1)}, u32[]{:S(2)}, u32[]{:S(2)}) collective-permute-start(f32[3,264,128]{2,1,0:T(8,128)S(1)} %get-tuple-element.78), channel_id=1, source_target_pairs={{0,4},{1,3},{2,6},{3,1},{4,0},{5,7},{6,2},{7,5},{8,12},{9,11},{10,... | collective-permute-start | bytes 1216520 | tf_op jit(solution)/shard_map/ppermute | solution.py:238
  38.2 12.4 %collective-permute-start.1 = (f32[2,320,128]{2,1,0:T(8,128)S(1)}, f32[2,320,128]{2,1,0:T(8,128)S(1)}, u32[]{:S(2)}, u32[]{:S(2)}) collective-permute-start(f32[2,320,128]{2,1,0:T(8,128)S(1)} %get-tuple-element.64), channel_id=1, source_target_pairs={{2,0},{4,2},{6,4},{8,6},{10,8},{12,10},{14,12},{16,14},{18,16},{20... | collective-permute-start | bytes 983048 | tf_op jit(solution)/shard_map/ppermute | solution.py:344
  40.8 14.0 %collective-permute-start.4 = (f32[3,264,128]{2,1,0:T(8,128)S(1)}, f32[3,264,128]{2,1,0:T(8,128)S(1)}, u32[]{:S(2)}, u32[]{:S(2)}) collective-permute-start(f32[3,264,128]{2,1,0:T(8,128)S(1)} %get-tuple-element.82), channel_id=1, source_target_pairs={{0,2},{1,9},{2,0},{3,11},{4,6},{5,13},{6,4},{7,15},{8,10},{9,1},{1... | collective-permute-start | bytes 1216520 | tf_op jit(solution)/shard_map/ppermute | solution.py:238
  51.7 6.8 %collective-permute-start.3 = (f32[2,264,128]{2,1,0:T(8,128)S(1)}, f32[2,264,128]{2,1,0:T(8,128)S(1)}, u32[]{:S(2)}, u32[]{:S(2)}) collective-permute-start(f32[2,264,128]{2,1,0:T(8,128)S(1)} %get-tuple-element.87), channel_id=1, source_target_pairs={{0,8},{1,5},{2,10},{3,7},{4,12},{5,1},{6,14},{7,3},{8,0},{9,13},{1... | collective-permute-start | bytes 811016 | tf_op jit(solution)/shard_map/ppermute | solution.py:238
  53.8 8.2 %collective-permute-start.8 = (f32[3,136,128]{2,1,0:T(8,128)S(1)}, f32[3,136,128]{2,1,0:T(8,128)S(1)}, u32[]{:S(2)}, u32[]{:S(2)}) collective-permute-start(f32[3,136,128]{2,1,0:T(8,128)S(1)} %pad_maximum_fusion.3), channel_id=1, source_target_pairs={{0,8},{1,5},{2,10},{3,7},{4,12},{5,1},{6,14},{7,3},{8,0},{9,13},{1... | collective-permute-start | bytes 626696 | tf_op jit(solution)/shard_map/ppermute | solution.py:238
  55.0 8.4 %collective-permute-start.7 = (f32[3,136,128]{2,1,0:T(8,128)S(1)}, f32[3,136,128]{2,1,0:T(8,128)S(1)}, u32[]{:S(2)}, u32[]{:S(2)}) collective-permute-start(f32[3,136,128]{2,1,0:T(8,128)S(1)} %pad_maximum_fusion.4), channel_id=1, source_target_pairs={{0,4},{1,3},{2,6},{3,1},{4,0},{5,7},{6,2},{7,5},{8,12},{9,11},{10,... | collective-permute-start | bytes 626696 | tf_op jit(solution)/shard_map/ppermute | solution.py:238
  58.5 6.5 %collective-permute-start.6 = (f32[2,136,128]{2,1,0:T(8,128)S(1)}, f32[2,136,128]{2,1,0:T(8,128)S(1)}, u32[]{:S(2)}, u32[]{:S(2)}) collective-permute-start(f32[2,136,128]{2,1,0:T(8,128)S(1)} %pad_maximum_fusion.7), channel_id=1, source_target_pairs={{0,2},{1,9},{2,0},{3,11},{4,6},{5,13},{6,4},{7,15},{8,10},{9,1},{1... | collective-permute-start | bytes 417800 | tf_op jit(solution)/shard_map/ppermute | solution.py:238
  65.1 6.4 %collective-permute-start.10 = (f32[3,72,128]{2,1,0:T(8,128)S(1)}, f32[3,72,128]{2,1,0:T(8,128)S(1)}, u32[]{:S(2)}, u32[]{:S(2)}) collective-permute-start(f32[3,72,128]{2,1,0:T(8,128)S(1)} %pad_maximum_fusion.10), channel_id=1, source_target_pairs={{0,8},{1,5},{2,10},{3,7},{4,12},{5,1},{6,14},{7,3},{8,0},{9,13},{1... | collective-permute-start | bytes 331784 | tf_op jit(solution)/shard_map/ppermute | solution.py:238
  66.7 4.7 %collective-permute-start.11 = (f32[3,72,128]{2,1,0:T(8,128)S(1)}, f32[3,72,128]{2,1,0:T(8,128)S(1)}, u32[]{:S(2)}, u32[]{:S(2)}) collective-permute-start(f32[3,72,128]{2,1,0:T(8,128)S(1)} %pad_maximum_fusion.9), channel_id=1, source_target_pairs={{0,2},{1,9},{2,0},{3,11},{4,6},{5,13},{6,4},{7,15},{8,10},{9,1},{1... | collective-permute-start | bytes 331784 | tf_op jit(solution)/shard_map/ppermute | solution.py:238
  68.8 4.4 %collective-permute-start.9 = (f32[2,72,128]{2,1,0:T(8,128)S(1)}, f32[2,72,128]{2,1,0:T(8,128)S(1)}, u32[]{:S(2)}, u32[]{:S(2)}) collective-permute-start(f32[2,72,128]{2,1,0:T(8,128)S(1)} %pad_maximum_fusion.13), channel_id=1, source_target_pairs={{0,4},{1,3},{2,6},{3,1},{4,0},{5,7},{6,2},{7,5},{8,12},{9,11},{10,... | collective-permute-start | bytes 221192 | tf_op jit(solution)/shard_map/ppermute | solution.py:238
  73.2 12.8 %collective-permute-start.13 = (f32[3,72,128]{2,1,0:T(8,128)S(1)}, f32[3,72,128]{2,1,0:T(8,128)S(1)}, u32[]{:S(2)}, u32[]{:S(2)}) collective-permute-start(f32[3,72,128]{2,1,0:T(8,128)S(1)} %pad_maximum_fusion.12), channel_id=1, source_target_pairs={{0,16},{1,17},{2,18},{3,19},{4,20},{5,21},{6,22},{7,23},{8,24},{9,... | collective-permute-start | bytes 331784 | tf_op jit(solution)/shard_map/ppermute | solution.py:238
  74.5 10.7 %collective-permute-start.14 = (f32[3,72,128]{2,1,0:T(8,128)S(1)}, f32[3,72,128]{2,1,0:T(8,128)S(1)}, u32[]{:S(2)}, u32[]{:S(2)}) collective-permute-start(f32[3,72,128]{2,1,0:T(8,128)S(1)} %pad_maximum_fusion.11), channel_id=1, source_target_pairs={{0,16},{1,17},{2,18},{3,19},{4,20},{5,21},{6,22},{7,23},{8,24},{9,... | collective-permute-start | bytes 331784 | tf_op jit(solution)/shard_map/ppermute | solution.py:238
  76.2 9.9 %collective-permute-start.12 = (f32[2,72,128]{2,1,0:T(8,128)S(1)}, f32[2,72,128]{2,1,0:T(8,128)S(1)}, u32[]{:S(2)}, u32[]{:S(2)}) collective-permute-start(f32[2,72,128]{2,1,0:T(8,128)S(1)} %pad_maximum_fusion.14), channel_id=1, source_target_pairs={{0,16},{1,17},{2,18},{3,19},{4,20},{5,21},{6,22},{7,23},{8,24},{9,... | collective-permute-start | bytes 221192 | tf_op jit(solution)/shard_map/ppermute | solution.py:238
  85.2 4.7 %collective-permute-start.17 = (f32[3,64,128]{2,1,0:T(8,128)S(1)}, f32[3,64,128]{2,1,0:T(8,128)S(1)}, u32[]{:S(2)}, u32[]{:S(2)}) collective-permute-start(f32[3,64,128]{2,1,0:T(8,128)S(1)} %slice_add_fusion.7), channel_id=1, source_target_pairs={{0,2},{1,9},{2,0},{3,11},{4,6},{5,13},{6,4},{7,15},{8,10},{9,1},{1... | collective-permute-start | bytes 294920 | tf_op jit(solution)/shard_map/ppermute | solution.py:238
  86.1 4.7 %collective-permute-start.16 = (f32[3,64,128]{2,1,0:T(8,128)S(1)}, f32[3,64,128]{2,1,0:T(8,128)S(1)}, u32[]{:S(2)}, u32[]{:S(2)}) collective-permute-start(f32[3,64,128]{2,1,0:T(8,128)S(1)} %slice_add_fusion.6), channel_id=1, source_target_pairs={{0,8},{1,5},{2,10},{3,7},{4,12},{5,1},{6,14},{7,3},{8,0},{9,13},{1... | collective-permute-start | bytes 294920 | tf_op jit(solution)/shard_map/ppermute | solution.py:238
  86.2 6.4 %collective-permute-start.15 = (f32[2,64,128]{2,1,0:T(8,128)S(1)}, f32[2,64,128]{2,1,0:T(8,128)S(1)}, u32[]{:S(2)}, u32[]{:S(2)}) collective-permute-start(f32[2,64,128]{2,1,0:T(8,128)S(1)} %slice_add_fusion.10), channel_id=1, source_target_pairs={{0,4},{1,3},{2,6},{3,1},{4,0},{5,7},{6,2},{7,5},{8,12},{9,11},{10,... | collective-permute-start | bytes 196616 | tf_op jit(solution)/shard_map/ppermute | solution.py:238
  89.9 5.7 %collective-permute-start.20 = (f32[3,128,128]{2,1,0:T(8,128)S(1)}, f32[3,128,128]{2,1,0:T(8,128)S(1)}, u32[]{:S(2)}, u32[]{:S(2)}) collective-permute-start(f32[3,128,128]{2,1,0:T(8,128)S(1)} %pad_maximum_fusion.5), channel_id=1, source_target_pairs={{0,8},{1,5},{2,10},{3,7},{4,12},{5,1},{6,14},{7,3},{8,0},{9,13},{1... | collective-permute-start | bytes 589832 | tf_op jit(solution)/shard_map/ppermute | solution.py:238
  90.8 6.0 %collective-permute-start.19 = (f32[3,128,128]{2,1,0:T(8,128)S(1)}, f32[3,128,128]{2,1,0:T(8,128)S(1)}, u32[]{:S(2)}, u32[]{:S(2)}) collective-permute-start(f32[3,128,128]{2,1,0:T(8,128)S(1)} %pad_maximum_fusion.6), channel_id=1, source_target_pairs={{0,4},{1,3},{2,6},{3,1},{4,0},{5,7},{6,2},{7,5},{8,12},{9,11},{10,... | collective-permute-start | bytes 589832 | tf_op jit(solution)/shard_map/ppermute | solution.py:238
  92.6 6.5 %collective-permute-start.18 = (f32[2,128,128]{2,1,0:T(8,128)S(1)}, f32[2,128,128]{2,1,0:T(8,128)S(1)}, u32[]{:S(2)}, u32[]{:S(2)}) collective-permute-start(f32[2,128,128]{2,1,0:T(8,128)S(1)} %pad_maximum_fusion.8), channel_id=1, source_target_pairs={{0,2},{1,9},{2,0},{3,11},{4,6},{5,13},{6,4},{7,15},{8,10},{9,1},{1... | collective-permute-start | bytes 393224 | tf_op jit(solution)/shard_map/ppermute | solution.py:238
  95.7 7.8 %collective-permute-start.23 = (f32[3,256,128]{2,1,0:T(8,128)S(1)}, f32[3,256,128]{2,1,0:T(8,128)S(1)}, u32[]{:S(2)}, u32[]{:S(2)}) collective-permute-start(f32[3,256,128]{2,1,0:T(8,128)S(1)} %pad_maximum_fusion.mine_ref), channel_id=1, source_target_pairs={{0,4},{1,3},{2,6},{3,1},{4,0},{5,7},{6,2},{7,5},{8,12},{9,11},{10,... | collective-permute-start | bytes 1179656 | tf_op jit(solution)/shard_map/ppermute | solution.py:238
  96.8 7.9 %collective-permute-start.22 = (f32[3,256,128]{2,1,0:T(8,128)S(1)}, f32[3,256,128]{2,1,0:T(8,128)S(1)}, u32[]{:S(2)}, u32[]{:S(2)}) collective-permute-start(f32[3,256,128]{2,1,0:T(8,128)S(1)} %pad_maximum_fusion.1.mine_ref), channel_id=1, source_target_pairs={{0,2},{1,9},{2,0},{3,11},{4,6},{5,13},{6,4},{7,15},{8,10},{9,1},{1... | collective-permute-start | bytes 1179656 | tf_op jit(solution)/shard_map/ppermute | solution.py:238
  99.2 6.5 %collective-permute-start.21 = (f32[2,256,128]{2,1,0:T(8,128)S(1)}, f32[2,256,128]{2,1,0:T(8,128)S(1)}, u32[]{:S(2)}, u32[]{:S(2)}) collective-permute-start(f32[2,256,128]{2,1,0:T(8,128)S(1)} %pad_maximum_fusion.2.mine_ref), channel_id=1, source_target_pairs={{0,8},{1,5},{2,10},{3,7},{4,12},{5,1},{6,14},{7,3},{8,0},{9,13},{1... | collective-permute-start | bytes 786440 | tf_op jit(solution)/shard_map/ppermute | solution.py:238

commit v7 on v5

--- a/solution.py
+++ b/solution.py
@@ -288,8 +288,8 @@
 def plan(groups, bits):
     x, y, z = (bits + bits[-1:] * 2)[:3]
     cuts = [groups * i // 8 for i in CUTS]
-    even = [[y, z, x], [x, y, z], [z, x, y]]
-    odd = [[x, y, z], [z, x, y], [y, z, x]]
+    even = [[z, y, x], [y, x, z], [x, z, y]]
+    odd = [[y, x, z], [x, z, y], [z, y, x]]
     orders = [list(zip(e + bits[3:], o + bits[3:])) for e, o in zip(even, odd)]
     orders = [o[: len(bits)] for o in orders]
     return [(a, b - a, o) for a, b, o in zip(cuts, cuts[1:], orders)]

time: 94.5 us -> 94.5 us (level)
  starting transfers between devices: 41.6 us -> 39.3 us
  waiting for transfers between devices: 23.7 us -> 26 us
    ppermute x21, starting transfers between devices: 37.8 us -> 35.5 us  [swap(): return lax.ppermute(block, ('tm', 'pix'), route)]
    ppermute x21, waiting for transfers between devices: 13.2 us -> 15.5 us  [swap(): return lax.ppermute(block, ('tm', 'pix'), route)]
  transfers between devices with their start and end apart: 24 -> 24, of which waited for: 10 -> 12; matrix products, arithmetic and copies ran while one was open for 2% -> 2% of each run, Pallas kernels for 22% -> 22%
where the time goes in v7:
time: 94.5 us; the launch traced here: 94.2 us
  starting transfers between devices  39.3 us (42%)
  waiting for transfers between devices  26 us (28%)
  Pallas kernels  23.7 us (25%)
  blocking collectives  2.59 us (3%)
  other arithmetic  1.65 us (2%)
    ppermute x21, starting transfers between devices, swap(): return lax.ppermute(block, ('tm', 'pix'), route)  35.5 us
    ppermute x21, waiting for transfers between devices, swap(): return lax.ppermute(block, ('tm', 'pix'), route)  15.5 us
    pallas_call x3, Pallas kernels, inner(): pl.pallas_call(inner_kernel, grid=(count,), in_specs=[SMEM, pl.BlockSpec(...  13 us
    ppermute x1, waiting for transfers between devices, on_device(): next_mean = lax.ppermute(mean, 'tm', back)  10.5 us
    pallas_call x2, Pallas kernels, on_device(): pl.pallas_call(functools.partial(edge_kernel, first), in_specs=[pl.BlockS...  4.12 us
    pallas_call x3, Pallas kernels, border(): pl.pallas_call(functools.partial(border_kernel, first - spans[p > 0][0]),...  3.83 us
    pallas_call x3, Pallas kernels, on_device(): pl.pallas_call(functools.partial(finish_kernel, first, total_frames), in_...  2.8 us
    psum x1, blocking collectives, on_device(): sums = lax.psum(sums[:, 0], 'pix')  2.59 us
  transfers between devices with their start and end apart: 24, of which 12 were waited for; matrix products, arithmetic and copies ran while one was open for 2% of the time, Pallas kernels for 22%

profile of v7, /device:TPU:0, one launch (start us, length us, event | category | flops | bytes accessed | tf_op | source)
XLA Modules:
  0.0 94.2 jit_solution(7807053312101074026)
XLA Ops:
  0.0 1.7 %edges_0.1 = (f32[136,1]{1,0:T(8,128)S(1)}, f32[3,320,128]{2,1,0:T(8,128)S(1)}) custom-call(f32[128,8192]{1,0:T(8,128)} %x_ref.5, f32[1,8192]{1,0:T(1,128)} %bitcast.5), custom_call_target="tpu_custom_call" | custom-call | tf_op jit(solution)/shard_map/edges_0/pallas_call | solution.py:324
  3.0 2.4 %edges_1.1 = (f32[136,1]{1,0:T(8,128)S(1)}, f32[5,320,128]{2,1,0:T(8,128)S(1)}) custom-call(f32[128,8192]{1,0:T(8,128)} %x_ref.5, f32[1,8192]{1,0:T(1,128)} %bitcast.6), custom_call_target="tpu_custom_call" | custom-call | tf_op jit(solution)/shard_map/edges_1/pallas_call | solution.py:324
  5.5 2.6 %psum.7 = f32[136]{0:T(256)S(1)} all-reduce(f32[136]{0:T(256)S(1)} %add_reduce_fusion), channel_id=1, replica_groups=mesh['tm'=16,'pix'=2] {'pix'}, use_global_device_ids=true, to_apply=%region_0.1 | all-reduce | flops 136 | bytes 1088 | tf_op jit(solution)/shard_map/psum | solution.py:344
  11.9 4.7 %inner_0.1 = (f32[3,512,128]{2,1,0:T(8,128)S(1)}, f32[3,512,128]{2,1,0:T(8,128)S(1)}, f32[3,8,128]{2,1,0:T(8,128)S(1)}) custom-call(f32[128]{0:T(128)S(1)} %slice_divide_fusion.mean_ref, f32[128,8192]{1,0:T(8,128)} %x_ref.5), custom_call_target="tpu_custom_call" | custom-call | tf_op jit(solution)/shard_map/inner_0/pallas_call | solution.py:352
  16.6 4.7 %inner_1.1 = (f32[3,512,128]{2,1,0:T(8,128)S(1)}, f32[3,512,128]{2,1,0:T(8,128)S(1)}, f32[3,8,128]{2,1,0:T(8,128)S(1)}) custom-call(f32[128]{0:T(128)S(1)} %slice_divide_fusion.mean_ref, f32[128,8192]{1,0:T(8,128)} %x_ref.5), custom_call_target="tpu_custom_call" | custom-call | tf_op jit(solution)/shard_map/inner_1/pallas_call | solution.py:352
  21.4 3.5 %inner_2.1 = (f32[2,512,128]{2,1,0:T(8,128)S(1)}, f32[2,512,128]{2,1,0:T(8,128)S(1)}, f32[2,8,128]{2,1,0:T(8,128)S(1)}) custom-call(f32[128]{0:T(128)S(1)} %slice_divide_fusion.mean_ref, f32[128,8192]{1,0:T(8,128)} %x_ref.5), custom_call_target="tpu_custom_call" | custom-call | tf_op jit(solution)/shard_map/inner_2/pallas_call | solution.py:352
  24.9 10.5 %collective-permute-done.mean_ref = f32[128]{0:T(128)S(1)} collective-permute-done((f32[128]{0:T(128)S(1)}, f32[128]{0:T(128)S(1)}, u32[]{:S(2)}, u32[]{:S(2)}) %collective-permute-start) | collective-permute-done | bytes 544 | tf_op jit(solution)/shard_map/ppermute | solution.py:346
  36.8 2.1 %collective-permute-start.5 = (f32[3,264,128]{2,1,0:T(8,128)S(1)}, f32[3,264,128]{2,1,0:T(8,128)S(1)}, u32[]{:S(2)}, u32[]{:S(2)}) collective-permute-start(f32[3,264,128]{2,1,0:T(8,128)S(1)} %get-tuple-element.78), channel_id=1, source_target_pairs={{0,8},{1,5},{2,10},{3,7},{4,12},{5,1},{6,14},{7,3},{8,0},{9,13},{1... | collective-permute-start | bytes 1216520 | tf_op jit(solution)/shard_map/ppermute | solution.py:238
  38.9 1.4 %border_1.1 = (f32[3,256,128]{2,1,0:T(8,128)S(1)}, f32[3,264,128]{2,1,0:T(8,128)S(1)}) custom-call(f32[128]{0:T(128)S(1)} %collective-permute-done.mean_ref, s32[1]{0:T(128)} %bitcast.1.side_ref, f32[5,320,128]{2,1,0:T(8,128)S(1)} %collective-permute-done.1.edge_ref, f32[3,512,128]{2,1,0:T(8,128)S(1)} %get-tuple-element.80.last_ref, ...), custom_call_target="tpu_custom_call" | custom-call | tf_op jit(solution)/shard_map/border_1/pallas_call | solution.py:376
  42.7 3.4 %collective-permute-start.3 = (f32[2,264,128]{2,1,0:T(8,128)S(1)}, f32[2,264,128]{2,1,0:T(8,128)S(1)}, u32[]{:S(2)}, u32[]{:S(2)}) collective-permute-start(f32[2,264,128]{2,1,0:T(8,128)S(1)} %get-tuple-element.87), channel_id=1, source_target_pairs={{0,2},{1,9},{2,0},{3,11},{4,6},{5,13},{6,4},{7,15},{8,10},{9,1},{1... | collective-permute-start | bytes 811016 | tf_op jit(solution)/shard_map/ppermute | solution.py:238
  48.3 4.9 %collective-permute-start.7 = (f32[3,136,128]{2,1,0:T(8,128)S(1)}, f32[3,136,128]{2,1,0:T(8,128)S(1)}, u32[]{:S(2)}, u32[]{:S(2)}) collective-permute-start(f32[3,136,128]{2,1,0:T(8,128)S(1)} %pad_maximum_fusion.4), channel_id=1, source_target_pairs={{0,2},{1,9},{2,0},{3,11},{4,6},{5,13},{6,4},{7,15},{8,10},{9,1},{1... | collective-permute-start | bytes 626696 | tf_op jit(solution)/shard_map/ppermute | solution.py:238
  53.3 1.5 %collective-permute-start.6 = (f32[2,136,128]{2,1,0:T(8,128)S(1)}, f32[2,136,128]{2,1,0:T(8,128)S(1)}, u32[]{:S(2)}, u32[]{:S(2)}) collective-permute-start(f32[2,136,128]{2,1,0:T(8,128)S(1)} %pad_maximum_fusion.7), channel_id=1, source_target_pairs={{0,8},{1,5},{2,10},{3,7},{4,12},{5,1},{6,14},{7,3},{8,0},{9,13},{1... | collective-permute-start | bytes 417800 | tf_op jit(solution)/shard_map/ppermute | solution.py:238
  54.9 2.5 %collective-permute-start.11 = (f32[3,72,128]{2,1,0:T(8,128)S(1)}, f32[3,72,128]{2,1,0:T(8,128)S(1)}, u32[]{:S(2)}, u32[]{:S(2)}) collective-permute-start(f32[3,72,128]{2,1,0:T(8,128)S(1)} %pad_maximum_fusion.9), channel_id=1, source_target_pairs={{0,2},{1,9},{2,0},{3,11},{4,6},{5,13},{6,4},{7,15},{8,10},{9,1},{1... | collective-permute-start | bytes 331784 | tf_op jit(solution)/shard_map/ppermute | solution.py:238
  58.5 1.5 %collective-permute-start.10 = (f32[3,72,128]{2,1,0:T(8,128)S(1)}, f32[3,72,128]{2,1,0:T(8,128)S(1)}, u32[]{:S(2)}, u32[]{:S(2)}) collective-permute-start(f32[3,72,128]{2,1,0:T(8,128)S(1)} %pad_maximum_fusion.10), channel_id=1, source_target_pairs={{0,8},{1,5},{2,10},{3,7},{4,12},{5,1},{6,14},{7,3},{8,0},{9,13},{1... | collective-permute-start | bytes 331784 | tf_op jit(solution)/shard_map/ppermute | solution.py:238
  60.8 2.2 %collective-permute-start.14 = (f32[3,72,128]{2,1,0:T(8,128)S(1)}, f32[3,72,128]{2,1,0:T(8,128)S(1)}, u32[]{:S(2)}, u32[]{:S(2)}) collective-permute-start(f32[3,72,128]{2,1,0:T(8,128)S(1)} %pad_maximum_fusion.11), channel_id=1, source_target_pairs={{0,16},{1,17},{2,18},{3,19},{4,20},{5,21},{6,22},{7,23},{8,24},{9,... | collective-permute-start | bytes 331784 | tf_op jit(solution)/shard_map/ppermute | solution.py:238
  62.9 1.5 %collective-permute-done.10 = f32[3,72,128]{2,1,0:T(8,128)S(1)} collective-permute-done((f32[3,72,128]{2,1,0:T(8,128)S(1)}, f32[3,72,128]{2,1,0:T(8,128)S(1)}, u32[]{:S(2)}, u32[]{:S(2)}) %collective-permute-start.10) | collective-permute-done | bytes 110624 | tf_op jit(solution)/shard_map/ppermute | solution.py:238
  64.5 2.0 %collective-permute-start.13 = (f32[3,72,128]{2,1,0:T(8,128)S(1)}, f32[3,72,128]{2,1,0:T(8,128)S(1)}, u32[]{:S(2)}, u32[]{:S(2)}) collective-permute-start(f32[3,72,128]{2,1,0:T(8,128)S(1)} %pad_maximum_fusion.12), channel_id=1, source_target_pairs={{0,16},{1,17},{2,18},{3,19},{4,20},{5,21},{6,22},{7,23},{8,24},{9,... | collective-permute-start | bytes 331784 | tf_op jit(solution)/shard_map/ppermute | solution.py:238
  68.9 2.0 %collective-permute-start.17 = (f32[3,64,128]{2,1,0:T(8,128)S(1)}, f32[3,64,128]{2,1,0:T(8,128)S(1)}, u32[]{:S(2)}, u32[]{:S(2)}) collective-permute-start(f32[3,64,128]{2,1,0:T(8,128)S(1)} %slice_add_fusion.7), channel_id=1, source_target_pairs={{0,2},{1,9},{2,0},{3,11},{4,6},{5,13},{6,4},{7,15},{8,10},{9,1},{1... | collective-permute-start | bytes 294920 | tf_op jit(solution)/shard_map/ppermute | solution.py:238
  73.0 1.7 %collective-permute-start.15 = (f32[2,64,128]{2,1,0:T(8,128)S(1)}, f32[2,64,128]{2,1,0:T(8,128)S(1)}, u32[]{:S(2)}, u32[]{:S(2)}) collective-permute-start(f32[2,64,128]{2,1,0:T(8,128)S(1)} %slice_add_fusion.10), channel_id=1, source_target_pairs={{0,4},{1,3},{2,6},{3,1},{4,0},{5,7},{6,2},{7,5},{8,12},{9,11},{10,... | collective-permute-start | bytes 196616 | tf_op jit(solution)/shard_map/ppermute | solution.py:238
  76.5 1.8 %collective-permute-start.19 = (f32[3,128,128]{2,1,0:T(8,128)S(1)}, f32[3,128,128]{2,1,0:T(8,128)S(1)}, u32[]{:S(2)}, u32[]{:S(2)}) collective-permute-start(f32[3,128,128]{2,1,0:T(8,128)S(1)} %pad_maximum_fusion.6), channel_id=1, source_target_pairs={{0,2},{1,9},{2,0},{3,11},{4,6},{5,13},{6,4},{7,15},{8,10},{9,1},{1... | collective-permute-start | bytes 589832 | tf_op jit(solution)/shard_map/ppermute | solution.py:238
  78.7 3.6 %collective-permute-done.20 = f32[3,128,128]{2,1,0:T(8,128)S(1)} collective-permute-done((f32[3,128,128]{2,1,0:T(8,128)S(1)}, f32[3,128,128]{2,1,0:T(8,128)S(1)}, u32[]{:S(2)}, u32[]{:S(2)}) %collective-permute-start.20) | collective-permute-done | bytes 196640 | tf_op jit(solution)/shard_map/ppermute | solution.py:238
  83.0 1.4 %collective-permute-done.19 = f32[3,128,128]{2,1,0:T(8,128)S(1)} collective-permute-done((f32[3,128,128]{2,1,0:T(8,128)S(1)}, f32[3,128,128]{2,1,0:T(8,128)S(1)}, u32[]{:S(2)}, u32[]{:S(2)}) %collective-permute-start.19) | collective-permute-done | bytes 196640 | tf_op jit(solution)/shard_map/ppermute | solution.py:238
  85.5 2.0 %collective-permute-start.21 = (f32[2,256,128]{2,1,0:T(8,128)S(1)}, f32[2,256,128]{2,1,0:T(8,128)S(1)}, u32[]{:S(2)}, u32[]{:S(2)}) collective-permute-start(f32[2,256,128]{2,1,0:T(8,128)S(1)} %pad_maximum_fusion.2.mine_ref), channel_id=1, source_target_pairs={{0,2},{1,9},{2,0},{3,11},{4,6},{5,13},{6,4},{7,15},{8,10},{9,1},{1... | collective-permute-start | bytes 786440 | tf_op jit(solution)/shard_map/ppermute | solution.py:238
  87.5 2.7 %collective-permute-done.23.got_ref = f32[3,256,128]{2,1,0:T(8,128)S(1)} collective-permute-done((f32[3,256,128]{2,1,0:T(8,128)S(1)}, f32[3,256,128]{2,1,0:T(8,128)S(1)}, u32[]{:S(2)}, u32[]{:S(2)}) %collective-permute-start.23) | collective-permute-done | bytes 393248 | tf_op jit(solution)/shard_map/ppermute | solution.py:238
  (90 shorter events, 25.7 us)
Async XLA Ops:
  1.7 23.2 %collective-permute-start.2 = (f32[3,320,128]{2,1,0:T(8,128)S(1)}, f32[3,320,128]{2,1,0:T(8,128)S(1)}, u32[]{:S(2)}, u32[]{:S(2)}) collective-permute-start(f32[3,320,128]{2,1,0:T(8,128)S(1)} %get-tuple-element.68), channel_id=1, source_target_pairs={{2,0},{4,2},{6,4},{8,6},{10,8},{12,10},{14,12},{16,14},{18,16},{20... | collective-permute-start | bytes 1474568 | tf_op jit(solution)/shard_map/ppermute | solution.py:343
  9.3 29.6 %collective-permute-start.1 = (f32[5,320,128]{2,1,0:T(8,128)S(1)}, f32[5,320,128]{2,1,0:T(8,128)S(1)}, u32[]{:S(2)}, u32[]{:S(2)}) collective-permute-start(f32[5,320,128]{2,1,0:T(8,128)S(1)} %get-tuple-element.65), channel_id=1, source_target_pairs={{2,0},{4,2},{6,4},{8,6},{10,8},{12,10},{14,12},{16,14},{18,16},{20... | collective-permute-start | bytes 2457608 | tf_op jit(solution)/shard_map/ppermute | solution.py:348
  10.6 24.8 %collective-permute-start = (f32[128]{0:T(128)S(1)}, f32[128]{0:T(128)S(1)}, u32[]{:S(2)}, u32[]{:S(2)}) collective-permute-start(f32[128]{0:T(128)S(1)} %slice_divide_fusion.mean_ref), channel_id=1, source_target_pairs={{2,0},{4,2},{6,4},{8,6},{10,8},{12,10},{14,12},{16,14},{18,16},{20... | collective-permute-start | bytes 1544 | tf_op jit(solution)/shard_map/ppermute | solution.py:346
  36.8 9.3 %collective-permute-start.5 = (f32[3,264,128]{2,1,0:T(8,128)S(1)}, f32[3,264,128]{2,1,0:T(8,128)S(1)}, u32[]{:S(2)}, u32[]{:S(2)}) collective-permute-start(f32[3,264,128]{2,1,0:T(8,128)S(1)} %get-tuple-element.78), channel_id=1, source_target_pairs={{0,8},{1,5},{2,10},{3,7},{4,12},{5,1},{6,14},{7,3},{8,0},{9,13},{1... | collective-permute-start | bytes 1216520 | tf_op jit(solution)/shard_map/ppermute | solution.py:238
  40.2 8.0 %collective-permute-start.4 = (f32[3,264,128]{2,1,0:T(8,128)S(1)}, f32[3,264,128]{2,1,0:T(8,128)S(1)}, u32[]{:S(2)}, u32[]{:S(2)}) collective-permute-start(f32[3,264,128]{2,1,0:T(8,128)S(1)} %get-tuple-element.82), channel_id=1, source_target_pairs={{0,4},{1,3},{2,6},{3,1},{4,0},{5,7},{6,2},{7,5},{8,12},{9,11},{10,... | collective-permute-start | bytes 1216520 | tf_op jit(solution)/shard_map/ppermute | solution.py:238
  42.7 10.5 %collective-permute-start.3 = (f32[2,264,128]{2,1,0:T(8,128)S(1)}, f32[2,264,128]{2,1,0:T(8,128)S(1)}, u32[]{:S(2)}, u32[]{:S(2)}) collective-permute-start(f32[2,264,128]{2,1,0:T(8,128)S(1)} %get-tuple-element.87), channel_id=1, source_target_pairs={{0,2},{1,9},{2,0},{3,11},{4,6},{5,13},{6,4},{7,15},{8,10},{9,1},{1... | collective-permute-start | bytes 811016 | tf_op jit(solution)/shard_map/ppermute | solution.py:238
  46.2 8.6 %collective-permute-start.8 = (f32[3,136,128]{2,1,0:T(8,128)S(1)}, f32[3,136,128]{2,1,0:T(8,128)S(1)}, u32[]{:S(2)}, u32[]{:S(2)}) collective-permute-start(f32[3,136,128]{2,1,0:T(8,128)S(1)} %pad_maximum_fusion.3), channel_id=1, source_target_pairs={{0,4},{1,3},{2,6},{3,1},{4,0},{5,7},{6,2},{7,5},{8,12},{9,11},{10,... | collective-permute-start | bytes 626696 | tf_op jit(solution)/shard_map/ppermute | solution.py:238
  48.3 9.1 %collective-permute-start.7 = (f32[3,136,128]{2,1,0:T(8,128)S(1)}, f32[3,136,128]{2,1,0:T(8,128)S(1)}, u32[]{:S(2)}, u32[]{:S(2)}) collective-permute-start(f32[3,136,128]{2,1,0:T(8,128)S(1)} %pad_maximum_fusion.4), channel_id=1, source_target_pairs={{0,2},{1,9},{2,0},{3,11},{4,6},{5,13},{6,4},{7,15},{8,10},{9,1},{1... | collective-permute-start | bytes 626696 | tf_op jit(solution)/shard_map/ppermute | solution.py:238
  53.3 5.1 %collective-permute-start.6 = (f32[2,136,128]{2,1,0:T(8,128)S(1)}, f32[2,136,128]{2,1,0:T(8,128)S(1)}, u32[]{:S(2)}, u32[]{:S(2)}) collective-permute-start(f32[2,136,128]{2,1,0:T(8,128)S(1)} %pad_maximum_fusion.7), channel_id=1, source_target_pairs={{0,8},{1,5},{2,10},{3,7},{4,12},{5,1},{6,14},{7,3},{8,0},{9,13},{1... | collective-permute-start | bytes 417800 | tf_op jit(solution)/shard_map/ppermute | solution.py:238
  54.9 5.8 %collective-permute-start.11 = (f32[3,72,128]{2,1,0:T(8,128)S(1)}, f32[3,72,128]{2,1,0:T(8,128)S(1)}, u32[]{:S(2)}, u32[]{:S(2)}) collective-permute-start(f32[3,72,128]{2,1,0:T(8,128)S(1)} %pad_maximum_fusion.9), channel_id=1, source_target_pairs={{0,2},{1,9},{2,0},{3,11},{4,6},{5,13},{6,4},{7,15},{8,10},{9,1},{1... | collective-permute-start | bytes 331784 | tf_op jit(solution)/shard_map/ppermute | solution.py:238
  58.5 5.9 %collective-permute-start.10 = (f32[3,72,128]{2,1,0:T(8,128)S(1)}, f32[3,72,128]{2,1,0:T(8,128)S(1)}, u32[]{:S(2)}, u32[]{:S(2)}) collective-permute-start(f32[3,72,128]{2,1,0:T(8,128)S(1)} %pad_maximum_fusion.10), channel_id=1, source_target_pairs={{0,8},{1,5},{2,10},{3,7},{4,12},{5,1},{6,14},{7,3},{8,0},{9,13},{1... | collective-permute-start | bytes 331784 | tf_op jit(solution)/shard_map/ppermute | solution.py:238
  60.0 4.5 %collective-permute-start.9 = (f32[2,72,128]{2,1,0:T(8,128)S(1)}, f32[2,72,128]{2,1,0:T(8,128)S(1)}, u32[]{:S(2)}, u32[]{:S(2)}) collective-permute-start(f32[2,72,128]{2,1,0:T(8,128)S(1)} %pad_maximum_fusion.13), channel_id=1, source_target_pairs={{0,4},{1,3},{2,6},{3,1},{4,0},{5,7},{6,2},{7,5},{8,12},{9,11},{10,... | collective-permute-start | bytes 221192 | tf_op jit(solution)/shard_map/ppermute | solution.py:238
  60.8 8.0 %collective-permute-start.14 = (f32[3,72,128]{2,1,0:T(8,128)S(1)}, f32[3,72,128]{2,1,0:T(8,128)S(1)}, u32[]{:S(2)}, u32[]{:S(2)}) collective-permute-start(f32[3,72,128]{2,1,0:T(8,128)S(1)} %pad_maximum_fusion.11), channel_id=1, source_target_pairs={{0,16},{1,17},{2,18},{3,19},{4,20},{5,21},{6,22},{7,23},{8,24},{9,... | collective-permute-start | bytes 331784 | tf_op jit(solution)/shard_map/ppermute | solution.py:238
  64.5 6.9 %collective-permute-start.13 = (f32[3,72,128]{2,1,0:T(8,128)S(1)}, f32[3,72,128]{2,1,0:T(8,128)S(1)}, u32[]{:S(2)}, u32[]{:S(2)}) collective-permute-start(f32[3,72,128]{2,1,0:T(8,128)S(1)} %pad_maximum_fusion.12), channel_id=1, source_target_pairs={{0,16},{1,17},{2,18},{3,19},{4,20},{5,21},{6,22},{7,23},{8,24},{9,... | collective-permute-start | bytes 331784 | tf_op jit(solution)/shard_map/ppermute | solution.py:238
  66.5 6.5 %collective-permute-start.12 = (f32[2,72,128]{2,1,0:T(8,128)S(1)}, f32[2,72,128]{2,1,0:T(8,128)S(1)}, u32[]{:S(2)}, u32[]{:S(2)}) collective-permute-start(f32[2,72,128]{2,1,0:T(8,128)S(1)} %pad_maximum_fusion.14), channel_id=1, source_target_pairs={{0,16},{1,17},{2,18},{3,19},{4,20},{5,21},{6,22},{7,23},{8,24},{9,... | collective-permute-start | bytes 221192 | tf_op jit(solution)/shard_map/ppermute | solution.py:238
  68.9 5.8 %collective-permute-start.17 = (f32[3,64,128]{2,1,0:T(8,128)S(1)}, f32[3,64,128]{2,1,0:T(8,128)S(1)}, u32[]{:S(2)}, u32[]{:S(2)}) collective-permute-start(f32[3,64,128]{2,1,0:T(8,128)S(1)} %slice_add_fusion.7), channel_id=1, source_target_pairs={{0,2},{1,9},{2,0},{3,11},{4,6},{5,13},{6,4},{7,15},{8,10},{9,1},{1... | collective-permute-start | bytes 294920 | tf_op jit(solution)/shard_map/ppermute | solution.py:238
  71.4 5.1 %collective-permute-start.16 = (f32[3,64,128]{2,1,0:T(8,128)S(1)}, f32[3,64,128]{2,1,0:T(8,128)S(1)}, u32[]{:S(2)}, u32[]{:S(2)}) collective-permute-start(f32[3,64,128]{2,1,0:T(8,128)S(1)} %slice_add_fusion.6), channel_id=1, source_target_pairs={{0,8},{1,5},{2,10},{3,7},{4,12},{5,1},{6,14},{7,3},{8,0},{9,13},{1... | collective-permute-start | bytes 294920 | tf_op jit(solution)/shard_map/ppermute | solution.py:238
  73.0 5.3 %collective-permute-start.15 = (f32[2,64,128]{2,1,0:T(8,128)S(1)}, f32[2,64,128]{2,1,0:T(8,128)S(1)}, u32[]{:S(2)}, u32[]{:S(2)}) collective-permute-start(f32[2,64,128]{2,1,0:T(8,128)S(1)} %slice_add_fusion.10), channel_id=1, source_target_pairs={{0,4},{1,3},{2,6},{3,1},{4,0},{5,7},{6,2},{7,5},{8,12},{9,11},{10,... | collective-permute-start | bytes 196616 | tf_op jit(solution)/shard_map/ppermute | solution.py:238
  74.7 7.7 %collective-permute-start.20 = (f32[3,128,128]{2,1,0:T(8,128)S(1)}, f32[3,128,128]{2,1,0:T(8,128)S(1)}, u32[]{:S(2)}, u32[]{:S(2)}) collective-permute-start(f32[3,128,128]{2,1,0:T(8,128)S(1)} %pad_maximum_fusion.5), channel_id=1, source_target_pairs={{0,4},{1,3},{2,6},{3,1},{4,0},{5,7},{6,2},{7,5},{8,12},{9,11},{10,... | collective-permute-start | bytes 589832 | tf_op jit(solution)/shard_map/ppermute | solution.py:238
  76.5 7.9 %collective-permute-start.19 = (f32[3,128,128]{2,1,0:T(8,128)S(1)}, f32[3,128,128]{2,1,0:T(8,128)S(1)}, u32[]{:S(2)}, u32[]{:S(2)}) collective-permute-start(f32[3,128,128]{2,1,0:T(8,128)S(1)} %pad_maximum_fusion.6), channel_id=1, source_target_pairs={{0,2},{1,9},{2,0},{3,11},{4,6},{5,13},{6,4},{7,15},{8,10},{9,1},{1... | collective-permute-start | bytes 589832 | tf_op jit(solution)/shard_map/ppermute | solution.py:238
  78.3 7.2 %collective-permute-start.18 = (f32[2,128,128]{2,1,0:T(8,128)S(1)}, f32[2,128,128]{2,1,0:T(8,128)S(1)}, u32[]{:S(2)}, u32[]{:S(2)}) collective-permute-start(f32[2,128,128]{2,1,0:T(8,128)S(1)} %pad_maximum_fusion.8), channel_id=1, source_target_pairs={{0,8},{1,5},{2,10},{3,7},{4,12},{5,1},{6,14},{7,3},{8,0},{9,13},{1... | collective-permute-start | bytes 393224 | tf_op jit(solution)/shard_map/ppermute | solution.py:238
  82.4 7.8 %collective-permute-start.23 = (f32[3,256,128]{2,1,0:T(8,128)S(1)}, f32[3,256,128]{2,1,0:T(8,128)S(1)}, u32[]{:S(2)}, u32[]{:S(2)}) collective-permute-start(f32[3,256,128]{2,1,0:T(8,128)S(1)} %pad_maximum_fusion.mine_ref), channel_id=1, source_target_pairs={{0,8},{1,5},{2,10},{3,7},{4,12},{5,1},{6,14},{7,3},{8,0},{9,13},{1... | collective-permute-start | bytes 1179656 | tf_op jit(solution)/shard_map/ppermute | solution.py:238
  84.5 7.8 %collective-permute-start.22 = (f32[3,256,128]{2,1,0:T(8,128)S(1)}, f32[3,256,128]{2,1,0:T(8,128)S(1)}, u32[]{:S(2)}, u32[]{:S(2)}) collective-permute-start(f32[3,256,128]{2,1,0:T(8,128)S(1)} %pad_maximum_fusion.1.mine_ref), channel_id=1, source_target_pairs={{0,4},{1,3},{2,6},{3,1},{4,0},{5,7},{6,2},{7,5},{8,12},{9,11},{10,... | collective-permute-start | bytes 1179656 | tf_op jit(solution)/shard_map/ppermute | solution.py:238
  85.5 7.8 %collective-permute-start.21 = (f32[2,256,128]{2,1,0:T(8,128)S(1)}, f32[2,256,128]{2,1,0:T(8,128)S(1)}, u32[]{:S(2)}, u32[]{:S(2)}) collective-permute-start(f32[2,256,128]{2,1,0:T(8,128)S(1)} %pad_maximum_fusion.2.mine_ref), channel_id=1, source_target_pairs={{0,2},{1,9},{2,0},{3,11},{4,6},{5,13},{6,4},{7,15},{8,10},{9,1},{1... | collective-permute-start | bytes 786440 | tf_op jit(solution)/shard_map/ppermute | solution.py:238
